TPU v7x, 512 devices: a whole 4x4x16 slice. The times are simulated.
512 devices in a mesh: dp: 32 (over x, z_lo, core), factor: 16 (over y, z_hi).
Axes of the slice: x: 4, y: 4, z: 16 (z_hi: 4, z_lo: 4; z = z_hi * 4 + z_lo), core: 2. Of those that a mesh axis runs over, the one named last changes fastest.
Arguments:
- attn_in: bfloat16 [32768, 8192], P('dp', 'factor'), may hold values from -21 to 21
- mlp_in: bfloat16 [32768, 8192], P('dp', 'factor'), may hold values from -21 to 21
- attn_hgrad: bfloat16 [32768, 192], P('dp'), may hold values from -6 to 6
- mlp_hgrad: bfloat16 [32768, 128], P('dp'), may hold values from -6 to 6
- attn_basis: bfloat16 [8192, 8192], P('factor', 'dp'), may hold values from -0.0625 to 0.0625
- mlp_basis: bfloat16 [8192, 8192], P('factor', 'dp'), may hold values from -0.0625 to 0.0625
- attn_eig: float32 [8192], P('dp'), may hold values from 0.001 to 0.03
- mlp_eig: float32 [8192], P('dp'), may hold values from 0.001 to 0.03
- rank_basis: float32 [5, 64, 64], replicated, may hold values from -0.75 to 0.75
- rank_eig: float32 [5, 64], replicated, may hold values from 0.3 to 3
Outputs:
- attn_update: float32 [192, 8192], P(None, 'factor')
- mlp_update: float32 [128, 8192], P(None, 'factor')
All inputs are finite; a program needn't handle non-finite values.
Results may differ from a plain program's by a relative error of at most 0.0003.
Values sent between devices are 32-bit elements; how exact they have to be, the bound alone decides.
No kernel may reach another device: no remote copies, remote signals or barrier semaphores. Data moves between devices by JAX's collectives and lax.ppermute only.
A program may use at most 64 MiB of HBM per device.

v0:
```python
import jax
import jax.numpy as jnp
from jax import lax
from jax.sharding import PartitionSpec as P

damping = 0.001
kl_limit = 8000.0


def rank_rotate(blocks, grad, transpose):
    count = blocks.shape[0]
    rank = blocks.shape[1]
    split = grad.reshape(count, rank, grad.shape[1])
    if transpose:
        out = jnp.einsum("pab,pan->pbn", blocks, split, precision=lax.Precision.HIGHEST)
    else:
        out = jnp.einsum("pab,pbn->pan", blocks, split, precision=lax.Precision.HIGHEST)
    return out.reshape(count * rank, grad.shape[1])


def one_group(inputs, hgrad, basis, eig_in, blocks, eig_out):
    total_tokens = inputs.shape[0] * lax.axis_size("dp")
    partial_grad = (
        lax.dot_general(hgrad, inputs, (((0,), (0,)), ((), ())), preferred_element_type=jnp.float32)
        / total_tokens
    )
    grad = lax.psum(partial_grad, "dp")
    pre = rank_rotate(blocks, grad, True)
    wide = basis.astype(jnp.float32)
    rot_part = jnp.dot(pre, wide, precision=lax.Precision.HIGHEST)
    out_eig = eig_out.reshape(-1)[:, None]
    rotated = lax.psum(rot_part, "factor")
    scaled = rotated / (out_eig * eig_in[None, :] + damping)
    back_part = jnp.dot(scaled, wide.T, precision=lax.Precision.HIGHEST)
    back = lax.psum(back_part, "dp")
    prec = rank_rotate(blocks, back, False)
    return (prec, grad)


def body(
    attn_in,
    mlp_in,
    attn_hgrad,
    mlp_hgrad,
    attn_basis,
    mlp_basis,
    attn_eig,
    mlp_eig,
    rank_basis,
    rank_eig,
):
    attn_prec, attn_grad = one_group(
        attn_in, attn_hgrad, attn_basis, attn_eig, rank_basis[:3], rank_eig[:3]
    )
    mlp_prec, mlp_grad = one_group(
        mlp_in, mlp_hgrad, mlp_basis, mlp_eig, rank_basis[3:], rank_eig[3:]
    )
    local_quad = jnp.sum(attn_prec * attn_grad) + jnp.sum(mlp_prec * mlp_grad)
    quad = lax.psum(local_quad, "factor")
    clip = jnp.minimum(jnp.float32(1.0), jnp.sqrt(kl_limit / quad))
    attn_update = clip * attn_prec
    mlp_update = clip * mlp_prec
    return (attn_update, mlp_update)


def solution(mesh):
    in_specs = (
        P("dp", "factor"),
        P("dp", "factor"),
        P("dp", None),
        P("dp", None),
        P("factor", "dp"),
        P("factor", "dp"),
        P("dp"),
        P("dp"),
        P(),
        P(),
    )
    out_specs = (P(None, "factor"), P(None, "factor"))
    return jax.shard_map(body, mesh=mesh, in_specs=in_specs, out_specs=out_specs, check_vma=False)
```

profile of v0, /device:TPU:1, one launch (start us, length us, event | category | flops | bytes accessed | tf_op | source)
XLA Modules:
  0.0 849.5 jit_solution(9519111154749781680)
XLA Ops:
  7.2 2.4 convolution_multiply_fusion.1
  9.7 1.1 convolution_multiply_fusion
  10.9 288.5 %all-reduce.9.cloned.1.call-done = (f32[192,512]{1,0:T(8,128)}, f32[128,512]{1,0:T(8,128)}) async-done(((f32[192,512]{1,0:T(8,128)}, f32[128,512]{1,0:T(8,128)}), (f32[192,512]{1,0:T(8,128)}, f32[128,512]{1,0:T(8,128)})) %all-reduce.9.cloned.1.call-update) | async-done | bytes 655376 | tf_op jit(solution)/shard_map/psum | solution.py:27
  299.4 1.4 fusion.20
  300.9 0.5 fusion.13
  301.4 0.4 copy-done.6
  301.8 0.9 fusion.27
  302.8 1.0 fusion.26
  303.8 0.6 copy-done.8
  304.5 0.6 slice-done
  305.2 190.9 %all-reduce.11.cloned.1.call-done = (f32[192,256]{1,0:T(8,128)}, f32[128,256]{1,0:T(8,128)}) async-done(((f32[192,256]{1,0:T(8,128)}, f32[128,256]{1,0:T(8,128)}), (f32[192,256]{1,0:T(8,128)}, f32[128,256]{1,0:T(8,128)})) %all-reduce.11.cloned.1.call-update) | async-done | bytes 327696 | tf_op jit(solution)/shard_map/psum | solution.py:32
  496.1 2.1 fusion.2
  498.3 0.7 copy-done.11
  498.9 1.1 fusion.6
  500.1 289.0 %all-reduce.7.cloned.1.call-done = (f32[3,64,512]{2,1,0:T(8,128)}, f32[2,64,512]{2,1,0:T(8,128)}) async-done(((f32[3,64,512]{2,1,0:T(8,128)}, f32[2,64,512]{2,1,0:T(8,128)}), (f32[3,64,512]{2,1,0:T(8,128)}, f32[2,64,512]{2,1,0:T(8,128)})) %all-reduce.7.cloned.1.call-update) | async-done | bytes 655376 | tf_op jit(solution)/shard_map/psum | solution.py:35
  789.1 1.5 fusion.15
  790.6 0.7 fusion
  791.3 0.2 copy-done.7
  791.5 0.4 fusion.22
  791.9 0.6 copy-done.2
  792.5 0.7 fusion.1
  794.4 46.3 %psum.55 = f32[]{:T(128)} all-reduce(f32[]{:T(128)S(6)} %add.33), channel_id=1, replica_groups=mesh['dp'=32,'factor'=16] {'factor'}, use_global_device_ids=true, to_apply=%region_8.0 | all-reduce | flops 1 | bytes 8 | tf_op jit(solution)/shard_map/psum | solution.py:59
  841.5 0.7 bitcast_multiply_fusion.2
  842.2 0.8 bitcast_multiply_fusion
  (29 shorter events, 0.4 us)
Async XLA Ops:
  7.2 2.5 copy-start
  7.2 2.5 copy-start.4
  7.2 292.2 %all-reduce.9.cloned.1.call-start = ((), (), s32[]{:S(2)}) async-start(), calls=%async_computation.1 | async-start | bytes 1310720 | tf_op jit(solution)/shard_map/psum | solution.py:27
  10.8 288.6 %copy-start.3 = (f32[5,64,64]{2,1,0:T(8,128)S(1)}, f32[5,64,64]{2,1,0:T(8,128)}, u32[]{:S(2)}) copy-start(f32[5,64,64]{2,1,0:T(8,128)} %param.18) | copy-start | bytes 245764
  10.8 485.3 %all-reduce.11.cloned.1.call-start = ((), (), s32[]{:S(2)}) async-start(), calls=%async_computation.2 | async-start | bytes 655360 | tf_op jit(solution)/shard_map/psum | solution.py:32
  299.4 1.4 copy-start.1
  300.9 1.0 copy-start.6
  301.8 0.9 copy-start.5
  303.8 0.7 copy-start.8
  303.8 485.3 %all-reduce.7.cloned.1.call-start = ((), (), s32[]{:S(2)}) async-start(), calls=%async_computation | async-start | bytes 1310720 | tf_op jit(solution)/shard_map/psum | solution.py:35
  304.5 0.7 slice-start
  305.2 190.9 %copy-start.10 = (f32[256]{0:T(256)S(1)}, f32[256]{0:T(256)}, u32[]{:S(2)}) copy-start(f32[256]{0:T(256)} %param.16) | copy-start | bytes 3076
  496.1 2.2 copy-start.9
  498.3 0.7 copy-start.11
  790.6 1.0 copy-start.7
  791.5 0.9 copy-start.2
Sparse Core Ops, SparseCore 0:
  11.6 287.8 all-reduce.8
  303.9 192.1 all-reduce.10
  500.2 288.8 all-reduce.6
where the time goes:
time: 855 us; the launch traced here: 849 us
  waiting for transfers between devices  768 us (90%)
  blocking collectives  46.3 us (5%)
  between operations  15.9 us (2%)
  matrix products  12.5 us (1%)
    psum x1, waiting for transfers between devices, one_group(): back = lax.psum(back_part, 'dp')  289 us
    psum x1, waiting for transfers between devices, one_group(): grad = lax.psum(partial_grad, 'dp')  289 us
    psum x1, waiting for transfers between devices, one_group(): rotated = lax.psum(rot_part, 'factor')  191 us
    psum x1, blocking collectives, body(): quad = lax.psum(local_quad, 'factor')  46.3 us
  transfers between devices with their start and end apart: 3, of which 3 were waited for; matrix products, arithmetic and copies ran while one was open for 0% of the time, Pallas kernels for 0%

commit v1 on v0

v1 whole, which is shorter than its diff:
```python
import jax
import jax.numpy as jnp
from jax import lax
from jax.sharding import PartitionSpec as P

damping = 0.001
kl_limit = 8000.0
HI = lax.Precision.HIGHEST

CORE_PAIRS = [[x * 8 + z * 2 + c for c in range(2)] for x in range(4) for z in range(4)]
CHIPS = [[x * 8 + z * 2 + c for x in range(4) for z in range(4)] for c in range(2)]
Y_GROUPS = [[y * 4 + z for y in range(4)] for z in range(4)]
Z_GROUPS = [[y * 4 + z for z in range(4)] for y in range(4)]


def exchange(x, axis, groups):
    return lax.all_to_all(x, axis, 0, 0, axis_index_groups=groups, tiled=True)


def copies(x, count):
    return jnp.broadcast_to(x[None], (count,) + x.shape)


def tiles(x):
    rows, cols = x.shape
    return x.reshape(rows // 8, 8, cols // 128, 128).transpose(0, 2, 1, 3).reshape(-1, 8, 128)


def untile(t, rows, cols):
    return t.reshape(rows // 8, cols // 128, 8, 128).transpose(0, 2, 1, 3).reshape(rows, cols)


def chip_halves(x):
    half = x.shape[1] // 2
    return jnp.stack([tiles(x[:, :half]), tiles(x[:, half:])])


def core_sum(x):
    return jnp.sum(exchange(chip_halves(x), "dp", CORE_PAIRS), axis=0)


def spread(shard, rows, cols):
    own = exchange(copies(shard, 16), "dp", CHIPS).reshape(-1, 8, 128)
    both = lax.all_gather(own, "dp", axis_index_groups=CORE_PAIRS)
    half = cols // 2
    return untile(both[0], rows, half), untile(both[1], rows, half)


def rank_rotate(blocks, x, transpose):
    count, rank = blocks.shape[0], blocks.shape[1]
    split = x.reshape(count, rank, x.shape[1])
    spec = "pab,pan->pbn" if transpose else "pab,pbn->pan"
    return jnp.einsum(spec, blocks, split, precision=HI).reshape(x.shape)


def body(
    attn_in,
    mlp_in,
    attn_hgrad,
    mlp_hgrad,
    attn_basis,
    mlp_basis,
    attn_eig,
    mlp_eig,
    rank_basis,
    rank_eig,
):
    total_tokens = attn_in.shape[0] * lax.axis_size("dp")
    ca, cm = attn_hgrad.shape[1], mlp_hgrad.shape[1]
    rows, feats, cols = ca + cm, attn_in.shape[1], attn_basis.shape[1]
    half = feats // 2
    contract0 = (((0,), (0,)), ((), ()))
    attn_part = lax.dot_general(attn_hgrad, attn_in, contract0, preferred_element_type=jnp.float32)
    mlp_part = lax.dot_general(mlp_hgrad, mlp_in, contract0, preferred_element_type=jnp.float32)
    part = jnp.concatenate([attn_part, mlp_part]) / total_tokens

    shard = exchange(core_sum(part).reshape(16, -1, 8, 128), "dp", CHIPS)
    lo, hi = spread(jnp.sum(shard, axis=0), rows, feats)
    wide_a, wide_m = attn_basis.astype(jnp.float32), mlp_basis.astype(jnp.float32)

    def rotate(g_lo, g_hi, wide):
        out = jnp.dot(g_lo, wide[:half], precision=HI)
        return out + jnp.dot(g_hi, wide[half:], precision=HI)

    rot_part = jnp.concatenate([rotate(lo[:ca], hi[:ca], wide_a), rotate(lo[ca:], hi[ca:], wide_m)])
    rot_part = rank_rotate(rank_basis, rot_part, True)

    block = jnp.sum(exchange(tiles(rot_part).reshape(4, -1, 8, 128), "factor", Y_GROUPS), axis=0)
    block = jnp.sum(exchange(copies(block, 4), "factor", Z_GROUPS), axis=0)
    y = lax.axis_index("factor") // 4
    rot = untile(block, rows // 4, cols)
    eig_rows = jnp.concatenate([jnp.broadcast_to(attn_eig, (ca, cols)), jnp.broadcast_to(mlp_eig, (cm, cols))])
    denominator = rank_eig.reshape(-1)[:, None] * eig_rows + damping
    scaled = rot / lax.dynamic_slice(denominator, (y * (rows // 4), 0), (rows // 4, cols))
    quad = jnp.broadcast_to(jnp.sum(scaled * rot), (1, 8, 128))
    sent = jnp.concatenate([tiles(scaled), quad])
    got = exchange(copies(sent, 4), "factor", Y_GROUPS)
    quad = jnp.sum(got[:, -1, 0, 0])
    scaled = untile(got[:, :-1].reshape(-1, 8, 128), rows, cols)
    scaled = rank_rotate(rank_basis, scaled, False)

    contract1 = (((1,), (1,)), ((), ()))
    back_part = jnp.concatenate(
        [
            lax.dot_general(scaled[:ca], wide_a, contract1, precision=HI),
            lax.dot_general(scaled[ca:], wide_m, contract1, precision=HI),
        ]
    )
    quad_tile = jnp.broadcast_to(quad, (2, 1, 8, 128))
    halves = jnp.concatenate([chip_halves(back_part), quad_tile], axis=1)
    summed = jnp.sum(exchange(halves, "dp", CORE_PAIRS), axis=0)
    sent = jnp.concatenate([summed[:-1].reshape(16, -1, 8, 128), copies(summed[-1:], 16)], axis=1)
    summed = jnp.sum(exchange(sent, "dp", CHIPS), axis=0)
    clip = jnp.minimum(jnp.float32(1.0), jnp.sqrt(kl_limit / summed[-1]))
    lo, hi = spread(clip * summed[:-1], rows, feats)
    update = jnp.concatenate([lo, hi], axis=1)
    return (update[:ca], update[ca:])


def solution(mesh):
    in_specs = (
        P("dp", "factor"),
        P("dp", "factor"),
        P("dp", None),
        P("dp", None),
        P("factor", "dp"),
        P("factor", "dp"),
        P("dp"),
        P("dp"),
        P(),
        P(),
    )
    out_specs = (P(None, "factor"), P(None, "factor"))
    return jax.shard_map(body, mesh=mesh, in_specs=in_specs, out_specs=out_specs, check_vma=False)
```

time: 855 us -> 154 us (0.18)
  waiting for transfers between devices: 768 us -> 16.8 us
  blocking collectives: 46.3 us -> 108 us
  between operations: 15.9 us -> 0.96 us
  starting transfers between devices: 0.12 us -> 12.1 us
    psum x3 -> x0, waiting for transfers between devices: 768 us -> none  [the longest x1 289 us: one_group(): back = lax.psum(back_part, 'dp')]
    all_to_all x0 -> x8, blocking collectives: none -> 101 us  [exchange(): return lax.all_to_all(x, axis, 0, 0, axis_index_groups=groups, tiled=True)]
    psum x1 -> x0, blocking collectives: 46.3 us -> none  [body(): quad = lax.psum(local_quad, 'factor')]
    all_to_all x0 -> x1, waiting for transfers between devices: none -> 16.8 us  [exchange(): return lax.all_to_all(x, axis, 0, 0, axis_index_groups=groups, tiled=True)]
    all_to_all x0 -> x1, starting transfers between devices: none -> 12.1 us  [exchange(): return lax.all_to_all(x, axis, 0, 0, axis_index_groups=groups, tiled=True)]
  transfers between devices with their start and end apart: 3 -> 1, of which waited for: 3 -> 1; matrix products, arithmetic and copies ran while one was open for 0% -> 0% of each run, Pallas kernels for 0% -> 0%
where the time goes in v1:
time: 154 us; the launch traced here: 153 us
  blocking collectives  108 us (70%)
  waiting for transfers between devices  16.8 us (11%)
  starting transfers between devices  12.1 us (8%)
  local copies, waits for them, and re-layouts  6.21 us (4%)
  matrix products  4.76 us (3%)
  other arithmetic  3.89 us (3%)
    all_to_all x8, blocking collectives, exchange(): return lax.all_to_all(x, axis, 0, 0, axis_index_groups=groups, tiled=True)  101 us
    all_to_all x1, waiting for transfers between devices, exchange(): return lax.all_to_all(x, axis, 0, 0, axis_index_groups=groups, tiled=True)  16.8 us
    all_to_all x1, starting transfers between devices, exchange(): return lax.all_to_all(x, axis, 0, 0, axis_index_groups=groups, tiled=True)  12.1 us
    all_gather x2, blocking collectives, spread(): both = lax.all_gather(own, 'dp', axis_index_groups=CORE_PAIRS)  7.59 us
    unnamed x18, local copies, waits for them, and re-layouts  3.84 us
  transfers between devices with their start and end apart: 1, of which 1 were waited for; matrix products, arithmetic and copies ran while one was open for 0% of the time, Pallas kernels for 0%

profile of v1, /device:TPU:1, one launch (start us, length us, event | category | flops | bytes accessed | tf_op | source)
XLA Modules:
  0.0 152.9 jit_solution(1812196103124833649)
XLA Ops:
  0.7 1.7 %fusion.20 = f32[128,512]{1,0:T(8,128)S(1)} fusion(bf16[1024,128]{1,0:T(8,128)(2,1)} %param.13, bf16[1024,512]{1,0:T(8,128)(2,1)} %param.11), kind=kOutput, calls=%fused_computation.45 | convolution fusion | flops 134217728 | bytes 1572864 | tf_op jit(solution)/shard_map/dot_general | solution.py:74
  3.0 10.7 %all_to_all.45 = f32[2,80,8,128]{3,2,1,0:T(8,128)S(1)} all-to-all(f32[2,80,8,128]{3,2,1,0:T(8,128)S(1)} %pad_maximum_fusion), channel_id=1, replica_groups={{0,16},{32,48},{64,80},{96,112},{128,144},{160,176},{192,208},{224,240}..., dimensions={0} | all-to-all | bytes 1310720 | tf_op jit(solution)/shard_map/all_to_all | solution.py:17
  13.7 14.0 %all_to_all.46 = f32[16,5,8,128]{3,2,1,0:T(8,128)S(1)} all-to-all(f32[16,5,8,128]{3,2,1,0:T(8,128)S(1)} %bitcast.105), channel_id=1, replica_groups={{0,32,64,96,128,160,192,224,256,288,320,352,384,416,448,480},{16,48,80,..., dimensions={0} | all-to-all | bytes 655360 | tf_op jit(solution)/shard_map/all_to_all | solution.py:17
  27.8 15.0 %all_to_all.47 = f32[16,5,8,128]{3,2,1,0:T(8,128)S(1)} all-to-all(f32[16,5,8,128]{3,2,1,0:T(8,128)S(1)} %broadcast_in_dim.16), channel_id=1, replica_groups={{0,32,64,96,128,160,192,224,256,288,320,352,384,416,448,480},{16,48,80,..., dimensions={0} | all-to-all | bytes 655360 | tf_op jit(solution)/shard_map/all_to_all | solution.py:17
  42.7 3.8 %all_gather.6 = f32[2,80,8,128]{3,2,1,0:T(8,128)S(1)} all-gather(f32[1,80,8,128]{3,2,1,0:T(8,128)S(1)} %bitcast.113), channel_id=1, replica_groups={{0,16},{32,48},{64,80},{96,112},{128,144},{160,176},{192,208},{224,240}..., dimensions={0}, use_global_device_ids=true | all-gather | bytes 983040 | tf_op jit(solution)/shard_map/all_gather | solution.py:44
  46.6 0.9 copy-done.2
  48.5 0.9 copy-done.4
  49.9 10.8 %all_to_all.48 = f32[4,20,8,128]{3,2,1,0:T(8,128)S(1)} all-to-all(f32[4,20,8,128]{3,2,1,0:T(8,128)S(1)} %bitcast.106), channel_id=1, replica_groups={{0,4,8,12},{1,5,9,13},{2,6,10,14},{3,7,11,15},{16,20,24,28},{17,21,25,2..., dimensions={0} | all-to-all | bytes 655360 | tf_op jit(solution)/shard_map/all_to_all | solution.py:17
  60.7 0.7 broadcast_in_dim.17
  61.4 12.1 %all-to-all-start.4 = ((f32[4,20,8,128]{3,2,1,0:T(8,128)}), f32[4,20,8,128]{3,2,1,0:T(8,128)S(1)}, u32[]{:S(2)}, u32[]{:S(2)}) async-start(f32[4,20,8,128]{3,2,1,0:T(8,128)} %broadcast_in_dim.17), calls=%async_computation.4 | async-start | bytes 655360 | tf_op jit(solution)/shard_map/all_to_all | solution.py:17
  73.5 0.7 copy-done.6
  74.4 16.8 %all-to-all-done.4 = f32[4,20,8,128]{3,2,1,0:T(8,128)S(1)} async-done(((f32[4,20,8,128]{3,2,1,0:T(8,128)}), f32[4,20,8,128]{3,2,1,0:T(8,128)S(1)}, u32[]{:S(2)}, u32[]{:S(2)}) %all-to-all-start.4) | async-done | bytes 327712 | tf_op jit(solution)/shard_map/all_to_all | solution.py:17
  91.3 0.7 copy-done.8
  92.0 0.7 multiply_reduce_fusion
  92.7 0.7 concatenate.27
  93.4 8.3 %all_to_all.49 = f32[4,21,8,128]{3,2,1,0:T(8,128)S(1)} all-to-all(f32[4,21,8,128]{3,2,1,0:T(8,128)S(1)} %broadcast_in_dim.20), channel_id=1, replica_groups={{0,4,8,12},{1,5,9,13},{2,6,10,14},{3,7,11,15},{16,20,24,28},{17,21,25,2..., dimensions={0} | all-to-all | bytes 688128 | tf_op jit(solution)/shard_map/all_to_all | solution.py:17
  102.2 0.7 copy-done.1
  104.9 0.7 select_maximum_fusion
  105.6 7.7 %all_to_all.50 = f32[2,81,8,128]{3,2,1,0:T(8,128)S(1)} all-to-all(f32[2,81,8,128]{3,2,1,0:T(8,128)S(1)} %select_maximum_fusion), channel_id=1, replica_groups={{0,16},{32,48},{64,80},{96,112},{128,144},{160,176},{192,208},{224,240}..., dimensions={0} | all-to-all | bytes 1327104 | tf_op jit(solution)/shard_map/all_to_all | solution.py:17
  113.4 19.4 %all_to_all.51 = f32[16,6,8,128]{3,2,1,0:T(8,128)S(1)} all-to-all(f32[16,6,8,128]{3,2,1,0:T(8,128)S(1)} %pad_maximum_fusion.1), channel_id=1, replica_groups={{0,32,64,96,128,160,192,224,256,288,320,352,384,416,448,480},{16,48,80,..., dimensions={0} | all-to-all | bytes 786432 | tf_op jit(solution)/shard_map/all_to_all | solution.py:17
  132.9 14.7 %all_to_all.52 = f32[16,5,8,128]{3,2,1,0:T(8,128)S(1)} all-to-all(f32[16,5,8,128]{3,2,1,0:T(8,128)S(1)} %broadcast_in_dim.23), channel_id=1, replica_groups={{0,32,64,96,128,160,192,224,256,288,320,352,384,416,448,480},{16,48,80,..., dimensions={0} | all-to-all | bytes 655360 | tf_op jit(solution)/shard_map/all_to_all | solution.py:17
  147.6 3.8 %all_gather.7 = f32[2,80,8,128]{3,2,1,0:T(8,128)S(1)} all-gather(f32[1,80,8,128]{3,2,1,0:T(8,128)S(1)} %bitcast.114), channel_id=1, replica_groups={{0,16},{32,48},{64,80},{96,112},{128,144},{160,176},{192,208},{224,240}..., dimensions={0}, use_global_device_ids=true | all-gather | bytes 983040 | tf_op jit(solution)/shard_map/all_gather | solution.py:44
  151.4 0.7 pad_maximum_fusion.4
  152.2 0.8 fusion
  (53 shorter events, 5.0 us)
Async XLA Ops:
  0.6 1.8 %copy-start = (bf16[1024,512]{1,0:T(8,128)(2,1)S(1)}, bf16[1024,512]{1,0:T(8,128)(2,1)}, u32[]{:S(2)}) copy-start(bf16[1024,512]{1,0:T(8,128)(2,1)} %param.10) | copy-start | bytes 3145732
  0.6 1.8 %copy-start.5 = (bf16[1024,192]{0,1:T(8,128)(2,1)S(1)}, bf16[1024,192]{0,1:T(8,128)(2,1)}, u32[]{:S(2)}) copy-start(bf16[1024,192]{0,1:T(8,128)(2,1)} %param.12) | copy-start | bytes 1179652
  46.5 0.9 copy-start.2
  46.6 1.1 copy-start.3
  48.5 0.9 copy-start.4
  61.4 29.8 %all-to-all-start.4 = ((f32[4,20,8,128]{3,2,1,0:T(8,128)}), f32[4,20,8,128]{3,2,1,0:T(8,128)S(1)}, u32[]{:S(2)}, u32[]{:S(2)}) async-start(f32[4,20,8,128]{3,2,1,0:T(8,128)} %broadcast_in_dim.17), calls=%async_computation.4 | async-start | bytes 655360 | tf_op jit(solution)/shard_map/all_to_all | solution.py:17
  73.5 0.7 copy-start.6
  74.4 16.9 %copy-start.7 = (f32[256]{0:T(256)S(1)}, f32[256]{0:T(256)}, u32[]{:S(2)}) copy-start(f32[256]{0:T(256)} %param.17) | copy-start | bytes 3076
  91.3 0.7 copy-start.8
  102.2 0.7 copy-start.1
  102.9 0.9 slice-start

commit v2 on v1

v2 whole, which is shorter than its diff:
```python
import jax
import jax.numpy as jnp
from jax import lax
from jax.sharding import PartitionSpec as P

damping = 0.001
kl_limit = 8000.0
HI = lax.Precision.HIGHEST

CORE_PAIRS = [[x * 8 + z * 2 + c for c in range(2)] for x in range(4) for z in range(4)]
CHIPS = [[x * 8 + z * 2 + c for x in range(4) for z in range(4)] for c in range(2)]
Y_GROUPS = [[y * 4 + z for y in range(4)] for z in range(4)]
Z_GROUPS = [[y * 4 + z for z in range(4)] for y in range(4)]


def exchange(x, axis, groups):
    return lax.all_to_all(x, axis, 0, 0, axis_index_groups=groups, tiled=True)


def copies(x, count):
    return jnp.broadcast_to(x[None], (count,) + x.shape)


def tiles(x):
    rows, cols = x.shape
    return x.reshape(rows // 8, 8, cols // 128, 128).transpose(0, 2, 1, 3).reshape(-1, 8, 128)


def untile(t, rows, cols):
    return t.reshape(rows // 8, cols // 128, 8, 128).transpose(0, 2, 1, 3).reshape(rows, cols)


def chip_halves(x):
    half = x.shape[1] // 2
    return jnp.stack([tiles(x[:, :half]), tiles(x[:, half:])])


def core_sum(x):
    return jnp.sum(exchange(chip_halves(x), "dp", CORE_PAIRS), axis=0)


def spread(shard, rows, cols):
    own = exchange(copies(shard, 16), "dp", CHIPS).reshape(-1, 8, 128)
    both = lax.all_gather(own, "dp", axis_index_groups=CORE_PAIRS)
    half = cols // 2
    return untile(both[0], rows, half), untile(both[1], rows, half)


def rank_rotate(blocks, x, transpose):
    count, rank = blocks.shape[0], blocks.shape[1]
    split = x.reshape(count, rank, x.shape[1])
    spec = "pab,pan->pbn" if transpose else "pab,pbn->pan"
    return jnp.einsum(spec, blocks, split, precision=HI).reshape(x.shape)


def to_rotated(inputs, hgrad, basis, eig_in, blocks, eig_out):
    total_tokens = inputs.shape[0] * lax.axis_size("dp")
    rows, feats, cols = hgrad.shape[1], inputs.shape[1], basis.shape[1]
    half = feats // 2
    contract0 = (((0,), (0,)), ((), ()))
    part = lax.dot_general(hgrad, inputs, contract0, preferred_element_type=jnp.float32) / total_tokens
    shard = exchange(core_sum(part).reshape(16, -1, 8, 128), "dp", CHIPS)
    lo, hi = spread(jnp.sum(shard, axis=0), rows, feats)
    wide = basis.astype(jnp.float32)
    rot_part = jnp.dot(lo, wide[:half], precision=HI) + jnp.dot(hi, wide[half:], precision=HI)
    rot_part = rank_rotate(blocks, rot_part, True)
    block = jnp.sum(exchange(tiles(rot_part).reshape(4, -1, 8, 128), "factor", Y_GROUPS), axis=0)
    block = jnp.sum(exchange(copies(block, 4), "factor", Z_GROUPS), axis=0)
    y = lax.axis_index("factor") >> 2
    rot = untile(block, rows // 4, cols)
    eig_rows = lax.dynamic_slice(eig_out.reshape(-1), (y * (rows // 4),), (rows // 4,))
    scaled = rot / (eig_rows[:, None] * eig_in[None, :] + damping)
    quad = jnp.broadcast_to(jnp.sum(scaled * rot), (1, 8, 128))
    sent = jnp.concatenate([tiles(scaled), quad])
    got = exchange(copies(sent, 4), "factor", Y_GROUPS)
    scaled = untile(got[:, :-1].reshape(-1, 8, 128), rows, cols)
    scaled = rank_rotate(blocks, scaled, False)
    contract1 = (((1,), (1,)), ((), ()))
    return lax.dot_general(scaled, wide, contract1, precision=HI), jnp.sum(got[:, -1], axis=0)


def body(
    attn_in,
    mlp_in,
    attn_hgrad,
    mlp_hgrad,
    attn_basis,
    mlp_basis,
    attn_eig,
    mlp_eig,
    rank_basis,
    rank_eig,
):
    attn_back, attn_quad = to_rotated(attn_in, attn_hgrad, attn_basis, attn_eig, rank_basis[:3], rank_eig[:3])
    mlp_back, mlp_quad = to_rotated(mlp_in, mlp_hgrad, mlp_basis, mlp_eig, rank_basis[3:], rank_eig[3:])
    shard = exchange(core_sum(attn_back).reshape(16, -1, 8, 128), "dp", CHIPS)
    attn_lo, attn_hi = spread(jnp.sum(shard, axis=0), *attn_back.shape)

    quad_tile = jnp.broadcast_to(attn_quad + mlp_quad, (2, 1, 8, 128))
    halves = jnp.concatenate([chip_halves(mlp_back), quad_tile], axis=1)
    summed = jnp.sum(exchange(halves, "dp", CORE_PAIRS), axis=0)
    sent = jnp.concatenate([summed[:-1].reshape(16, -1, 8, 128), copies(summed[-1:], 16)], axis=1)
    summed = jnp.sum(exchange(sent, "dp", CHIPS), axis=0)
    clip = jnp.minimum(jnp.float32(1.0), jnp.sqrt(kl_limit / summed[-1, 0, 0]))
    mlp_lo, mlp_hi = spread(summed[:-1], *mlp_back.shape)
    return (
        clip * jnp.concatenate([attn_lo, attn_hi], axis=1),
        clip * jnp.concatenate([mlp_lo, mlp_hi], axis=1),
    )


def solution(mesh):
    in_specs = (
        P("dp", "factor"),
        P("dp", "factor"),
        P("dp", None),
        P("dp", None),
        P("factor", "dp"),
        P("factor", "dp"),
        P("dp"),
        P("dp"),
        P(),
        P(),
    )
    out_specs = (P(None, "factor"), P(None, "factor"))
    return jax.shard_map(body, mesh=mesh, in_specs=in_specs, out_specs=out_specs, check_vma=False)
```

time: 154 us -> 224 us (1.45)
  blocking collectives: 108 us -> 39.9 us
  starting transfers between devices: 12.1 us -> 75.8 us
  waiting for transfers between devices: 16.8 us -> 77 us
  local copies, waits for them, and re-layouts: 6.21 us -> 13.9 us
  other arithmetic: 3.89 us -> 7.59 us
    all_to_all x8 -> x2, blocking collectives: 101 us -> 20.9 us  [exchange(): return lax.all_to_all(x, axis, 0, 0, axis_index_groups=groups, tiled=True)]
    all_to_all x1 -> x16, starting transfers between devices: 12.1 us -> 75.8 us  [exchange(): return lax.all_to_all(x, axis, 0, 0, axis_index_groups=groups, tiled=True)]
    all_to_all x1 -> x16, waiting for transfers between devices: 16.8 us -> 77 us  [exchange(): return lax.all_to_all(x, axis, 0, 0, axis_index_groups=groups, tiled=True)]
    all_gather x2 -> x4, blocking collectives: 7.59 us -> 18.9 us  [spread(): both = lax.all_gather(own, 'dp', axis_index_groups=CORE_PAIRS)]
    broadcast_in_dim x6 -> x10, local copies, waits for them, and re-layouts: 0.83 us -> 5.44 us  [copies(): return jnp.broadcast_to(x[None], (count,) + x.shape)]
  transfers between devices with their start and end apart: 1 -> 16, of which waited for: 1 -> 16; matrix products, arithmetic and copies ran while one was open for 0% -> 5% of each run, Pallas kernels for 0% -> 0%
where the time goes in v2:
time: 224 us; the launch traced here: 222 us
  waiting for transfers between devices  77 us (34%)
  starting transfers between devices  75.8 us (34%)
  blocking collectives  39.9 us (18%)
  local copies, waits for them, and re-layouts  13.9 us (6%)
  other arithmetic  7.59 us (3%)
  matrix products  6.46 us (3%)
    all_to_all x16, waiting for transfers between devices, exchange(): return lax.all_to_all(x, axis, 0, 0, axis_index_groups=groups, tiled=True)  77 us
    all_to_all x16, starting transfers between devices, exchange(): return lax.all_to_all(x, axis, 0, 0, axis_index_groups=groups, tiled=True)  75.8 us
    all_to_all x2, blocking collectives, exchange(): return lax.all_to_all(x, axis, 0, 0, axis_index_groups=groups, tiled=True)  20.9 us
    all_gather x4, blocking collectives, spread(): both = lax.all_gather(own, 'dp', axis_index_groups=CORE_PAIRS)  18.9 us
    broadcast_in_dim x10, local copies, waits for them, and re-layouts, copies(): return jnp.broadcast_to(x[None], (count,) + x.shape)  5.44 us
    unnamed x18, local copies, waits for them, and re-layouts  5.2 us
  transfers between devices with their start and end apart: 16, of which 16 were waited for; matrix products, arithmetic and copies ran while one was open for 5% of the time, Pallas kernels for 0%

profile of v2, /device:TPU:1, one launch (start us, length us, event | category | flops | bytes accessed | tf_op | source)
XLA Modules:
  0.0 222.4 jit_solution(5588504291518527862)
XLA Ops:
  2.4 10.4 %all_to_all.90 = f32[2,32,8,128]{3,2,1,0:T(8,128)S(1)} all-to-all(f32[2,32,8,128]{3,2,1,0:T(8,128)S(1)} %pad_maximum_fusion.3), channel_id=1, replica_groups={{0,16},{32,48},{64,80},{96,112},{128,144},{160,176},{192,208},{224,240}..., dimensions={0} | all-to-all | bytes 524288 | tf_op jit(solution)/shard_map/all_to_all | solution.py:17
  18.2 6.0 %all-to-all-done.1 = f32[16,2,8,128]{3,2,1,0:T(8,128)S(1)} async-done(((f32[16,2,8,128]{3,2,1,0:T(8,128)}), f32[16,2,8,128]{3,2,1,0:T(8,128)S(1)}, u32[]{:S(2)}, u32[]{:S(2)}) %all-to-all-start.1) | async-done | bytes 131104 | tf_op jit(solution)/shard_map/all_to_all | solution.py:17
  24.2 5.3 %all-to-all-start.6 = ((f32[2,48,8,128]{3,2,1,0:T(8,128)}), f32[2,48,8,128]{3,2,1,0:T(8,128)S(1)}, u32[]{:S(2)}, u32[]{:S(2)}) async-start(f32[2,48,8,128]{3,2,1,0:T(8,128)} %pad_maximum_fusion), calls=%async_computation.6 | async-start | bytes 786432 | tf_op jit(solution)/shard_map/all_to_all | solution.py:17
  35.7 6.5 %all-to-all-done.2 = f32[16,2,8,128]{3,2,1,0:T(8,128)S(1)} async-done(((f32[16,2,8,128]{3,2,1,0:T(8,128)}), f32[16,2,8,128]{3,2,1,0:T(8,128)S(1)}, u32[]{:S(2)}, u32[]{:S(2)}) %all-to-all-start.2) | async-done | bytes 131104 | tf_op jit(solution)/shard_map/all_to_all | solution.py:17
  42.2 3.9 %all-to-all-start.7 = ((f32[16,3,8,128]{3,2,1,0:T(8,128)}), f32[16,3,8,128]{3,2,1,0:T(8,128)S(1)}, u32[]{:S(2)}, u32[]{:S(2)}) async-start(f32[16,3,8,128]{3,2,1,0:T(8,128)} %bitcast.41), calls=%async_computation.7 | async-start | bytes 393216 | tf_op jit(solution)/shard_map/all_to_all | solution.py:17
  57.3 4.8 %all-to-all-done.3 = f32[4,8,8,128]{3,2,1,0:T(8,128)S(1)} async-done(((f32[4,8,8,128]{3,2,1,0:T(8,128)}), f32[4,8,8,128]{3,2,1,0:T(8,128)S(1)}, u32[]{:S(2)}, u32[]{:S(2)}) %all-to-all-start.3) | async-done | bytes 131104 | tf_op jit(solution)/shard_map/all_to_all | solution.py:17
  62.8 5.8 %all-to-all-start.8 = ((f32[16,3,8,128]{3,2,1,0:T(8,128)}), f32[16,3,8,128]{3,2,1,0:T(8,128)S(1)}, u32[]{:S(2)}, u32[]{:S(2)}) async-start(f32[16,3,8,128]{3,2,1,0:T(8,128)} %broadcast_in_dim.25), calls=%async_computation.8 | async-start | bytes 393216 | tf_op jit(solution)/shard_map/all_to_all | solution.py:17
  69.5 6.6 %all-to-all-done.8 = f32[16,3,8,128]{3,2,1,0:T(8,128)S(1)} async-done(((f32[16,3,8,128]{3,2,1,0:T(8,128)}), f32[16,3,8,128]{3,2,1,0:T(8,128)S(1)}, u32[]{:S(2)}, u32[]{:S(2)}) %all-to-all-start.8) | async-done | bytes 196640 | tf_op jit(solution)/shard_map/all_to_all | solution.py:17
  76.8 12.1 %all-to-all-start.4 = ((f32[4,8,8,128]{3,2,1,0:T(8,128)}), f32[4,8,8,128]{3,2,1,0:T(8,128)S(1)}, u32[]{:S(2)}, u32[]{:S(2)}) async-start(f32[4,8,8,128]{3,2,1,0:T(8,128)} %broadcast_in_dim.23), calls=%async_computation.4 | async-start | bytes 262144 | tf_op jit(solution)/shard_map/all_to_all | solution.py:17
  88.9 5.2 %all_gather.13 = f32[2,48,8,128]{3,2,1,0:T(8,128)S(1)} all-gather(f32[1,48,8,128]{3,2,1,0:T(8,128)S(1)} %bitcast.149), channel_id=1, replica_groups={{0,16},{32,48},{64,80},{96,112},{128,144},{160,176},{192,208},{224,240}..., dimensions={0}, use_global_device_ids=true | all-gather | bytes 589824 | tf_op jit(solution)/shard_map/all_gather | solution.py:44
  96.6 4.4 %all-to-all-done.4 = f32[4,8,8,128]{3,2,1,0:T(8,128)S(1)} async-done(((f32[4,8,8,128]{3,2,1,0:T(8,128)}), f32[4,8,8,128]{3,2,1,0:T(8,128)S(1)}, u32[]{:S(2)}, u32[]{:S(2)}) %all-to-all-start.4) | async-done | bytes 131104 | tf_op jit(solution)/shard_map/all_to_all | solution.py:17
  113.5 4.9 %all-to-all-done.5 = f32[4,9,8,128]{3,2,1,0:T(8,128)S(1)} async-done(((f32[4,9,8,128]{3,2,1,0:T(8,128)}), f32[4,9,8,128]{3,2,1,0:T(8,128)S(1)}, u32[]{:S(2)}, u32[]{:S(2)}) %all-to-all-start.5) | async-done | bytes 147488 | tf_op jit(solution)/shard_map/all_to_all | solution.py:17
  119.0 7.6 %all-to-all-start.10 = ((f32[4,12,8,128]{3,2,1,0:T(8,128)}), f32[4,12,8,128]{3,2,1,0:T(8,128)S(1)}, u32[]{:S(2)}, u32[]{:S(2)}) async-start(f32[4,12,8,128]{3,2,1,0:T(8,128)} %broadcast_in_dim.26), calls=%async_computation.10 | async-start | bytes 393216 | tf_op jit(solution)/shard_map/all_to_all | solution.py:17
  128.9 10.2 %all-to-all-done.10 = f32[4,12,8,128]{3,2,1,0:T(8,128)S(1)} async-done(((f32[4,12,8,128]{3,2,1,0:T(8,128)}), f32[4,12,8,128]{3,2,1,0:T(8,128)S(1)}, u32[]{:S(2)}, u32[]{:S(2)}) %all-to-all-start.10) | async-done | bytes 196640 | tf_op jit(solution)/shard_map/all_to_all | solution.py:17
  144.7 5.2 %all-to-all-done.11 = f32[4,13,8,128]{3,2,1,0:T(8,128)S(1)} async-done(((f32[4,13,8,128]{3,2,1,0:T(8,128)}), f32[4,13,8,128]{3,2,1,0:T(8,128)S(1)}, u32[]{:S(2)}, u32[]{:S(2)}) %all-to-all-start.11) | async-done | bytes 213024 | tf_op jit(solution)/shard_map/all_to_all | solution.py:17
  149.9 10.5 %all_to_all.91 = f32[2,33,8,128]{3,2,1,0:T(8,128)S(1)} all-to-all(f32[2,33,8,128]{3,2,1,0:T(8,128)S(1)} %pad_maximum_fusion.2), channel_id=1, replica_groups={{0,16},{32,48},{64,80},{96,112},{128,144},{160,176},{192,208},{224,240}..., dimensions={0} | all-to-all | bytes 540672 | tf_op jit(solution)/shard_map/all_to_all | solution.py:17
  162.7 4.0 %all-to-all-start.14 = ((f32[2,48,8,128]{3,2,1,0:T(8,128)}), f32[2,48,8,128]{3,2,1,0:T(8,128)S(1)}, u32[]{:S(2)}, u32[]{:S(2)}) async-start(f32[2,48,8,128]{3,2,1,0:T(8,128)} %pad_maximum_fusion.1), calls=%async_computation.14 | async-start | bytes 786432 | tf_op jit(solution)/shard_map/all_to_all | solution.py:17
  172.2 6.8 %all-to-all-done.13 = f32[16,3,8,128]{3,2,1,0:T(8,128)S(1)} async-done(((f32[16,3,8,128]{3,2,1,0:T(8,128)}), f32[16,3,8,128]{3,2,1,0:T(8,128)S(1)}, u32[]{:S(2)}, u32[]{:S(2)}) %all-to-all-start.13) | async-done | bytes 196640 | tf_op jit(solution)/shard_map/all_to_all | solution.py:17
  179.1 5.0 %all-to-all-start.15 = ((f32[16,3,8,128]{3,2,1,0:T(8,128)}), f32[16,3,8,128]{3,2,1,0:T(8,128)S(1)}, u32[]{:S(2)}, u32[]{:S(2)}) async-start(f32[16,3,8,128]{3,2,1,0:T(8,128)} %bitcast.71), calls=%async_computation.15 | async-start | bytes 393216 | tf_op jit(solution)/shard_map/all_to_all | solution.py:17
  184.1 7.5 %all-to-all-done.15 = f32[16,3,8,128]{3,2,1,0:T(8,128)S(1)} async-done(((f32[16,3,8,128]{3,2,1,0:T(8,128)}), f32[16,3,8,128]{3,2,1,0:T(8,128)S(1)}, u32[]{:S(2)}, u32[]{:S(2)}) %all-to-all-start.15) | async-done | bytes 196640 | tf_op jit(solution)/shard_map/all_to_all | solution.py:17
  192.2 4.3 %all-to-all-start.17 = ((f32[16,2,8,128]{3,2,1,0:T(8,128)}), f32[16,2,8,128]{3,2,1,0:T(8,128)S(1)}, u32[]{:S(2)}, u32[]{:S(2)}) async-start(f32[16,2,8,128]{3,2,1,0:T(8,128)} %broadcast_in_dim.32), calls=%async_computation.17 | async-start | bytes 262144 | tf_op jit(solution)/shard_map/all_to_all | solution.py:17
  196.6 7.3 %all-to-all-done.17 = f32[16,2,8,128]{3,2,1,0:T(8,128)S(1)} async-done(((f32[16,2,8,128]{3,2,1,0:T(8,128)}), f32[16,2,8,128]{3,2,1,0:T(8,128)S(1)}, u32[]{:S(2)}, u32[]{:S(2)}) %all-to-all-start.17) | async-done | bytes 131104 | tf_op jit(solution)/shard_map/all_to_all | solution.py:17
  209.4 4.7 %all_gather.15 = f32[2,32,8,128]{3,2,1,0:T(8,128)S(1)} all-gather(f32[1,32,8,128]{3,2,1,0:T(8,128)S(1)} %bitcast.163), channel_id=1, replica_groups={{0,16},{32,48},{64,80},{96,112},{128,144},{160,176},{192,208},{224,240}..., dimensions={0}, use_global_device_ids=true | all-gather | bytes 393216 | tf_op jit(solution)/shard_map/all_gather | solution.py:44
  215.6 5.9 %all_gather.14 = f32[2,48,8,128]{3,2,1,0:T(8,128)S(1)} all-gather(f32[1,48,8,128]{3,2,1,0:T(8,128)S(1)} %bitcast.150), channel_id=1, replica_groups={{0,16},{32,48},{64,80},{96,112},{128,144},{160,176},{192,208},{224,240}..., dimensions={0}, use_global_device_ids=true | all-gather | bytes 589824 | tf_op jit(solution)/shard_map/all_gather | solution.py:44
  (112 shorter events, 65.8 us)
Async XLA Ops:
  0.6 16.4 %copy-start = (bf16[1024,512]{1,0:T(8,128)(2,1)S(1)}, bf16[1024,512]{1,0:T(8,128)(2,1)}, u32[]{:S(2)}) copy-start(bf16[1024,512]{1,0:T(8,128)(2,1)} %param.10) | copy-start | bytes 3145732
  12.8 4.2 %copy-start.5 = (bf16[1024,192]{0,1:T(8,128)(2,1)S(1)}, bf16[1024,192]{0,1:T(8,128)(2,1)}, u32[]{:S(2)}) copy-start(bf16[1024,192]{0,1:T(8,128)(2,1)} %param.12) | copy-start | bytes 1179652
  13.5 10.7 %all-to-all-start.1 = ((f32[16,2,8,128]{3,2,1,0:T(8,128)}), f32[16,2,8,128]{3,2,1,0:T(8,128)S(1)}, u32[]{:S(2)}, u32[]{:S(2)}) async-start(f32[16,2,8,128]{3,2,1,0:T(8,128)} %bitcast.6), calls=%async_computation.1 | async-start | bytes 262144 | tf_op jit(solution)/shard_map/all_to_all | solution.py:17
  24.2 6.6 %all-to-all-start.6 = ((f32[2,48,8,128]{3,2,1,0:T(8,128)}), f32[2,48,8,128]{3,2,1,0:T(8,128)S(1)}, u32[]{:S(2)}, u32[]{:S(2)}) async-start(f32[2,48,8,128]{3,2,1,0:T(8,128)} %pad_maximum_fusion), calls=%async_computation.6 | async-start | bytes 786432 | tf_op jit(solution)/shard_map/all_to_all | solution.py:17
  31.5 10.7 %all-to-all-start.2 = ((f32[16,2,8,128]{3,2,1,0:T(8,128)}), f32[16,2,8,128]{3,2,1,0:T(8,128)S(1)}, u32[]{:S(2)}, u32[]{:S(2)}) async-start(f32[16,2,8,128]{3,2,1,0:T(8,128)} %broadcast_in_dim.22), calls=%async_computation.2 | async-start | bytes 262144 | tf_op jit(solution)/shard_map/all_to_all | solution.py:17
  42.2 11.4 %all-to-all-start.7 = ((f32[16,3,8,128]{3,2,1,0:T(8,128)}), f32[16,3,8,128]{3,2,1,0:T(8,128)S(1)}, u32[]{:S(2)}, u32[]{:S(2)}) async-start(f32[16,3,8,128]{3,2,1,0:T(8,128)} %bitcast.41), calls=%async_computation.7 | async-start | bytes 393216 | tf_op jit(solution)/shard_map/all_to_all | solution.py:17
  49.2 0.9 copy-start.1
  50.4 0.9 copy-start.3
  53.6 8.5 %all-to-all-start.3 = ((f32[4,8,8,128]{3,2,1,0:T(8,128)}), f32[4,8,8,128]{3,2,1,0:T(8,128)S(1)}, u32[]{:S(2)}, u32[]{:S(2)}) async-start(f32[4,8,8,128]{3,2,1,0:T(8,128)} %bitcast.18), calls=%async_computation.3 | async-start | bytes 262144 | tf_op jit(solution)/shard_map/all_to_all | solution.py:17
  62.8 13.4 %all-to-all-start.8 = ((f32[16,3,8,128]{3,2,1,0:T(8,128)}), f32[16,3,8,128]{3,2,1,0:T(8,128)S(1)}, u32[]{:S(2)}, u32[]{:S(2)}) async-start(f32[16,3,8,128]{3,2,1,0:T(8,128)} %broadcast_in_dim.25), calls=%async_computation.8 | async-start | bytes 393216 | tf_op jit(solution)/shard_map/all_to_all | solution.py:17
  68.6 0.7 copy-start.6
  76.8 24.2 %all-to-all-start.4 = ((f32[4,8,8,128]{3,2,1,0:T(8,128)}), f32[4,8,8,128]{3,2,1,0:T(8,128)S(1)}, u32[]{:S(2)}, u32[]{:S(2)}) async-start(f32[4,8,8,128]{3,2,1,0:T(8,128)} %broadcast_in_dim.23), calls=%async_computation.4 | async-start | bytes 262144 | tf_op jit(solution)/shard_map/all_to_all | solution.py:17
  94.1 0.9 copy-start.2
  100.9 8.5 %all-to-all-start.9 = ((f32[4,12,8,128]{3,2,1,0:T(8,128)}), f32[4,12,8,128]{3,2,1,0:T(8,128)S(1)}, u32[]{:S(2)}, u32[]{:S(2)}) async-start(f32[4,12,8,128]{3,2,1,0:T(8,128)} %bitcast.53), calls=%async_computation.9 | async-start | bytes 393216 | tf_op jit(solution)/shard_map/all_to_all | solution.py:17
  104.3 0.7 copy-start.7
  110.1 8.2 %all-to-all-start.5 = ((f32[4,9,8,128]{3,2,1,0:T(8,128)}), f32[4,9,8,128]{3,2,1,0:T(8,128)S(1)}, u32[]{:S(2)}, u32[]{:S(2)}) async-start(f32[4,9,8,128]{3,2,1,0:T(8,128)} %broadcast_in_dim.24), calls=%async_computation.5 | async-start | bytes 294912 | tf_op jit(solution)/shard_map/all_to_all | solution.py:17
  119.0 20.1 %all-to-all-start.10 = ((f32[4,12,8,128]{3,2,1,0:T(8,128)}), f32[4,12,8,128]{3,2,1,0:T(8,128)S(1)}, u32[]{:S(2)}, u32[]{:S(2)}) async-start(f32[4,12,8,128]{3,2,1,0:T(8,128)} %broadcast_in_dim.26), calls=%async_computation.10 | async-start | bytes 393216 | tf_op jit(solution)/shard_map/all_to_all | solution.py:17
  141.3 8.6 %all-to-all-start.11 = ((f32[4,13,8,128]{3,2,1,0:T(8,128)}), f32[4,13,8,128]{3,2,1,0:T(8,128)S(1)}, u32[]{:S(2)}, u32[]{:S(2)}) async-start(f32[4,13,8,128]{3,2,1,0:T(8,128)} %broadcast_in_dim.27), calls=%async_computation.11 | async-start | bytes 425984 | tf_op jit(solution)/shard_map/all_to_all | solution.py:17
  162.7 4.0 %slice-start = ((f32[33,8,128]{2,1,0:T(8,128)}), f32[32,8,128]{2,1,0:T(8,128)S(1)}, s32[]{:S(2)}) async-start(f32[33,8,128]{2,1,0:T(8,128)} %copy-done.4), calls=%async_computation.18 | async-start | bytes 262144 | tf_op jit(solution)/shard_map/slice | solution.py:102
  162.7 5.2 %all-to-all-start.14 = ((f32[2,48,8,128]{3,2,1,0:T(8,128)}), f32[2,48,8,128]{3,2,1,0:T(8,128)S(1)}, u32[]{:S(2)}, u32[]{:S(2)}) async-start(f32[2,48,8,128]{3,2,1,0:T(8,128)} %pad_maximum_fusion.1), calls=%async_computation.14 | async-start | bytes 786432 | tf_op jit(solution)/shard_map/all_to_all | solution.py:17
  168.0 11.1 %all-to-all-start.13 = ((f32[16,3,8,128]{3,2,1,0:T(8,128)}), f32[16,3,8,128]{3,2,1,0:T(8,128)S(1)}, u32[]{:S(2)}, u32[]{:S(2)}) async-start(f32[16,3,8,128]{3,2,1,0:T(8,128)} %pad_maximum_fusion.4), calls=%async_computation.13 | async-start | bytes 393216 | tf_op jit(solution)/shard_map/all_to_all | solution.py:17
  179.1 12.5 %all-to-all-start.15 = ((f32[16,3,8,128]{3,2,1,0:T(8,128)}), f32[16,3,8,128]{3,2,1,0:T(8,128)S(1)}, u32[]{:S(2)}, u32[]{:S(2)}) async-start(f32[16,3,8,128]{3,2,1,0:T(8,128)} %bitcast.71), calls=%async_computation.15 | async-start | bytes 393216 | tf_op jit(solution)/shard_map/all_to_all | solution.py:17
  192.2 11.6 %all-to-all-start.17 = ((f32[16,2,8,128]{3,2,1,0:T(8,128)}), f32[16,2,8,128]{3,2,1,0:T(8,128)S(1)}, u32[]{:S(2)}, u32[]{:S(2)}) async-start(f32[16,2,8,128]{3,2,1,0:T(8,128)} %broadcast_in_dim.32), calls=%async_computation.17 | async-start | bytes 262144 | tf_op jit(solution)/shard_map/all_to_all | solution.py:17
  204.6 11.1 %all-to-all-start.16 = ((f32[16,3,8,128]{3,2,1,0:T(8,128)}), f32[16,3,8,128]{3,2,1,0:T(8,128)S(1)}, u32[]{:S(2)}, u32[]{:S(2)}) async-start(f32[16,3,8,128]{3,2,1,0:T(8,128)} %broadcast_in_dim.31), calls=%async_computation.16 | async-start | bytes 393216 | tf_op jit(solution)/shard_map/all_to_all | solution.py:17
  (3 other events, 2.0 us)

commit v3 on v1

v3 whole, which is shorter than its diff:
```python
import jax
import jax.numpy as jnp
from jax import lax
from jax.sharding import PartitionSpec as P

damping = 0.001
kl_limit = 8000.0
HI = lax.Precision.HIGHEST

CORE_PAIRS = [[x * 8 + z * 2 + c for c in range(2)] for x in range(4) for z in range(4)]
CHIPS = [[x * 8 + z * 2 + c for x in range(4) for z in range(4)] for c in range(2)]
Y_GROUPS = [[y * 4 + z for y in range(4)] for z in range(4)]
Z_GROUPS = [[y * 4 + z for z in range(4)] for y in range(4)]


def exchange(x, axis, groups):
    return lax.all_to_all(x, axis, 0, 0, axis_index_groups=groups, tiled=True)


def copies(x, count):
    return jnp.broadcast_to(x[None], (count,) + x.shape)


def tiles(x):
    rows, cols = x.shape
    return x.reshape(rows // 8, 8, cols // 128, 128).transpose(0, 2, 1, 3).reshape(-1, 8, 128)


def untile(t, rows, cols):
    return t.reshape(rows // 8, cols // 128, 8, 128).transpose(0, 2, 1, 3).reshape(rows, cols)


def rank_rotate(blocks, x, transpose):
    count, rank = blocks.shape[0], blocks.shape[1]
    split = x.reshape(count, rank, x.shape[1])
    spec = "pab,pan->pbn" if transpose else "pab,pbn->pan"
    return jnp.einsum(spec, blocks, split, precision=HI).reshape(x.shape)


def deal(attn, mlp, parts):
    ca, cm = attn.shape[0] // parts, mlp.shape[0] // parts
    return [
        jnp.concatenate([attn[p * ca : (p + 1) * ca], mlp[p * cm : (p + 1) * cm]]) for p in range(parts)
    ]


def body(
    attn_in,
    mlp_in,
    attn_hgrad,
    mlp_hgrad,
    attn_basis,
    mlp_basis,
    attn_eig,
    mlp_eig,
    rank_basis,
    rank_eig,
):
    total_tokens = attn_in.shape[0] * lax.axis_size("dp")
    ca, cm = attn_hgrad.shape[1], mlp_hgrad.shape[1]
    rows, feats, cols = ca + cm, attn_in.shape[1], attn_basis.shape[1]
    ca2, rows2, rows8 = ca // 2, rows // 2, rows // 8

    wide = jnp.concatenate(
        [
            attn_basis.astype(jnp.float32),
            mlp_basis.astype(jnp.float32),
            jnp.broadcast_to(attn_eig, (8, cols)),
            jnp.broadcast_to(mlp_eig, (8, cols)),
        ]
    )
    swap = [(i, i ^ 1) for i in range(lax.axis_size("dp"))]
    wide = jnp.concatenate([wide, lax.ppermute(wide, "dp", swap)], axis=1)
    wide_a, wide_m = wide[:feats], wide[feats : 2 * feats]

    contract0 = (((0,), (0,)), ((), ()))
    attn_part = lax.dot_general(attn_hgrad, attn_in, contract0, preferred_element_type=jnp.float32)
    mlp_part = lax.dot_general(mlp_hgrad, mlp_in, contract0, preferred_element_type=jnp.float32)
    attn_part = rank_rotate(rank_basis[:3], attn_part / total_tokens, True)
    mlp_part = rank_rotate(rank_basis[3:], mlp_part / total_tokens, True)

    halves = jnp.stack([tiles(h) for h in deal(attn_part, mlp_part, 2)])
    shard = jnp.sum(exchange(halves, "dp", CORE_PAIRS), axis=0)
    shard = jnp.sum(exchange(shard.reshape(16, -1, 8, 128), "dp", CHIPS), axis=0)
    pre = untile(exchange(copies(shard, 16), "dp", CHIPS), rows2, feats)

    rot_a = jnp.dot(pre[:ca2], wide_a, precision=HI)
    rot_m = jnp.dot(pre[ca2:], wide_m, precision=HI)
    block = jnp.stack([tiles(b) for b in deal(rot_a, rot_m, 4)])
    block = jnp.sum(exchange(block, "factor", Y_GROUPS), axis=0)
    block = jnp.sum(exchange(copies(block, 4), "factor", Z_GROUPS), axis=0)
    rot = untile(block, rows8, 2 * cols)
    order = jnp.stack(deal(*[e.reshape(-1) for e in (rank_eig[:3], rank_eig[3:])], 8))
    place = (lax.axis_index("dp") & 1) * 4 + (lax.axis_index("factor") >> 2)
    eig_out = lax.dynamic_slice(order, (place, 0), (1, rows8)).reshape(-1, 1)
    eig_in = jnp.concatenate([jnp.tile(wide[2 * feats : 2 * feats + 8], (ca // 64, 1)), jnp.tile(wide[2 * feats + 8 :], (cm // 64, 1))])
    scaled = rot / (eig_out * eig_in + damping)
    quad = jnp.broadcast_to(jnp.sum(scaled * rot), (1, 8, 128))
    got = exchange(copies(jnp.concatenate([tiles(scaled), quad]), 4), "factor", Y_GROUPS)
    quad = jnp.sum(got[:, -1:], axis=0)
    scaled = untile(got[:, :-1], rows2, 2 * cols).reshape(4, rows8, 2 * cols)
    scaled_a = scaled[:, : ca // 8].reshape(ca2, 2 * cols)
    scaled_m = scaled[:, ca // 8 :].reshape(cm // 2, 2 * cols)

    contract1 = (((1,), (1,)), ((), ()))
    back_a = lax.dot_general(scaled_a, wide_a, contract1, precision=HI)
    back_m = lax.dot_general(scaled_m, wide_m, contract1, precision=HI)
    back = tiles(jnp.concatenate([back_a, back_m])).reshape(16, -1, 8, 128)
    sent = jnp.concatenate([back, copies(quad, 16)], axis=1)
    summed = jnp.sum(exchange(sent, "dp", CHIPS), axis=0)
    back = exchange(copies(summed[:-1], 16), "dp", CHIPS).reshape(-1, 8, 128)
    both = lax.all_gather(jnp.concatenate([back, summed[-1:]]), "dp", axis_index_groups=CORE_PAIRS)
    clip = jnp.minimum(jnp.float32(1.0), jnp.sqrt(kl_limit / (both[0, -1, 0, 0] + both[1, -1, 0, 0])))
    back = [untile(b[:-1], rows2, feats) for b in both]
    attn_back = jnp.concatenate([b[:ca2] for b in back])
    mlp_back = jnp.concatenate([b[ca2:] for b in back])
    return (clip * rank_rotate(rank_basis[:3], attn_back, False), clip * rank_rotate(rank_basis[3:], mlp_back, False))


def solution(mesh):
    in_specs = (
        P("dp", "factor"),
        P("dp", "factor"),
        P("dp", None),
        P("dp", None),
        P("factor", "dp"),
        P("factor", "dp"),
        P("dp"),
        P("dp"),
        P(),
        P(),
    )
    out_specs = (P(None, "factor"), P(None, "factor"))
    return jax.shard_map(body, mesh=mesh, in_specs=in_specs, out_specs=out_specs, check_vma=False)
```

time: 154 us -> 147 us (0.955)
  blocking collectives: 108 us -> 44.2 us
  waiting for transfers between devices: 16.8 us -> 41 us
  starting transfers between devices: 12.1 us -> 28.1 us
  other arithmetic: 3.89 us -> 12.5 us
  matrix products: 4.76 us -> 9.95 us
  local copies, waits for them, and re-layouts: 6.21 us -> 8.12 us
  between operations: 0.96 us -> 2.53 us
    all_to_all x8 -> x3, blocking collectives: 101 us -> 33.1 us  [exchange(): return lax.all_to_all(x, axis, 0, 0, axis_index_groups=groups, tiled=True)]
    all_to_all x1 -> x5, waiting for transfers between devices: 16.8 us -> 41 us  [exchange(): return lax.all_to_all(x, axis, 0, 0, axis_index_groups=groups, tiled=True)]
    all_to_all x1 -> x5, starting transfers between devices: 12.1 us -> 25.8 us  [exchange(): return lax.all_to_all(x, axis, 0, 0, axis_index_groups=groups, tiled=True)]
    another operation x2 -> x6, other arithmetic: 0.73 us -> 4.78 us  [the longest x4 3.99 us: body(): jnp.stack(deal(*[e.reshape(-1) for e in (rank_eig[:3], rank_eig[3:])], 8))]
    unnamed x18 -> x22, local copies, waits for them, and re-layouts: 3.84 us -> 0.07 us
    all_gather x2 -> x1, blocking collectives: 7.59 us -> 11.1 us  [body(): lax.all_gather(jnp.concatenate([back, summed[-1:]]), 'dp', axis_index_gro...]
    dot_general x2 -> x4, matrix products: 0.88 us -> 4.09 us  [rank_rotate(): return jnp.einsum(spec, blocks, split, precision=HI).reshape(x.shape)]
    broadcast_in_dim x6 -> x5, local copies, waits for them, and re-layouts: 0.83 us -> 3.15 us  [copies(): return jnp.broadcast_to(x[None], (count,) + x.shape)]
  transfers between devices with their start and end apart: 1 -> 6, of which waited for: 1 -> 5; matrix products, arithmetic and copies ran while one was open for 0% -> 8% of each run, Pallas kernels for 0% -> 0%
where the time goes in v3:
time: 147 us; the launch traced here: 146 us
  blocking collectives  44.2 us (30%)
  waiting for transfers between devices  41 us (28%)
  starting transfers between devices  28.1 us (19%)
  other arithmetic  12.5 us (9%)
  matrix products  9.95 us (7%)
  local copies, waits for them, and re-layouts  8.12 us (6%)
  between operations  2.53 us (2%)
    all_to_all x5, waiting for transfers between devices, exchange(): return lax.all_to_all(x, axis, 0, 0, axis_index_groups=groups, tiled=True)  41 us
    all_to_all x3, blocking collectives, exchange(): return lax.all_to_all(x, axis, 0, 0, axis_index_groups=groups, tiled=True)  33.1 us
    all_to_all x5, starting transfers between devices, exchange(): return lax.all_to_all(x, axis, 0, 0, axis_index_groups=groups, tiled=True)  25.8 us
    all_gather x1, blocking collectives, body(): lax.all_gather(jnp.concatenate([back, summed[-1:]]), 'dp', axis_index_gro...  11.1 us
    dot_general x4, matrix products, rank_rotate(): return jnp.einsum(spec, blocks, split, precision=HI).reshape(x.shape)  4.09 us
    another operation x4, other arithmetic, body(): jnp.stack(deal(*[e.reshape(-1) for e in (rank_eig[:3], rank_eig[3:])], 8))  3.99 us
    broadcast_in_dim x5, local copies, waits for them, and re-layouts, copies(): return jnp.broadcast_to(x[None], (count,) + x.shape)  3.15 us
  transfers between devices with their start and end apart: 6, of which 5 were waited for; matrix products, arithmetic and copies ran while one was open for 8% of the time, Pallas kernels for 0%

profile of v3, /device:TPU:1, one launch (start us, length us, event | category | flops | bytes accessed | tf_op | source)
XLA Modules:
  0.0 146.4 jit_solution(16425838168197187037)
XLA Ops:
  0.7 1.7 %convolution_multiply_fusion.3 = f32[128,512]{1,0:T(8,128)S(1)} fusion(bf16[1024,128]{1,0:T(8,128)(2,1)} %param.13, bf16[1024,512]{1,0:T(8,128)(2,1)} %param.11), kind=kOutput, calls=%fused_computation.5 | convolution fusion | flops 134283264 | bytes 1572864 | tf_op jit(solution)/shard_map/dot_general | solution.py:78
  2.4 1.3 convolution_bitcast_fusion
  4.8 10.9 %all_to_all.40 = f32[2,80,8,128]{3,2,1,0:T(8,128)S(1)} all-to-all(f32[2,80,8,128]{3,2,1,0:T(8,128)S(1)} %pad_maximum_fusion.2), channel_id=1, replica_groups={{0,16},{32,48},{64,80},{96,112},{128,144},{160,176},{192,208},{224,240}..., dimensions={0} | all-to-all | bytes 1310720 | tf_op jit(solution)/shard_map/all_to_all | solution.py:17
  16.5 3.5 %all-to-all-start.1 = ((f32[16,5,8,128]{3,2,1,0:T(8,128)}), f32[16,5,8,128]{3,2,1,0:T(8,128)S(1)}, u32[]{:S(2)}, u32[]{:S(2)}) async-start(f32[16,5,8,128]{3,2,1,0:T(8,128)} %bitcast.14), calls=%async_computation.1 | async-start | bytes 655360 | tf_op jit(solution)/shard_map/all_to_all | solution.py:17
  21.4 2.3 %collective-permute-start = (f32[1040,256]{1,0:T(8,128)}, f32[1040,256]{1,0:T(8,128)}, u32[]{:S(2)}, u32[]{:S(2)}) collective-permute-start(f32[1040,256]{1,0:T(8,128)} %pad_maximum_fusion.1), channel_id=1, source_target_pairs={{0,16},{16,0},{32,48},{48,32},{64,80},{80,64},{96,112},{112,96},{1... | collective-permute-start | bytes 3194888 | tf_op jit(solution)/shard_map/ppermute | solution.py:73
  23.7 8.0 %all-to-all-done.1 = f32[16,5,8,128]{3,2,1,0:T(8,128)S(1)} async-done(((f32[16,5,8,128]{3,2,1,0:T(8,128)}), f32[16,5,8,128]{3,2,1,0:T(8,128)S(1)}, u32[]{:S(2)}, u32[]{:S(2)}) %all-to-all-start.1) | async-done | bytes 327712 | tf_op jit(solution)/shard_map/all_to_all | solution.py:17
  32.5 3.8 %all-to-all-start.2 = ((f32[16,5,8,128]{3,2,1,0:T(8,128)}), f32[16,5,8,128]{3,2,1,0:T(8,128)S(1)}, u32[]{:S(2)}, u32[]{:S(2)}) async-start(f32[16,5,8,128]{3,2,1,0:T(8,128)} %broadcast_in_dim.14), calls=%async_computation.2 | async-start | bytes 655360 | tf_op jit(solution)/shard_map/all_to_all | solution.py:17
  36.4 1.8 %pad_maximum_fusion = f32[1040,512]{1,0:T(8,128)S(1)} fusion(f32[1040,256]{1,0:T(8,128)} %collective-permute-done, f32[8,256]{1,0:T(8,128)S(1)} %broadcast_in_dim.16, f32[8,256]{1,0:T(8,128)S(1)} %broadcast_in_dim.15, f32[512,256]{1,0:T(8,128)} %copy-done.2, f32[512,256]{1,0:T(8,128)} %copy-done.1), kind=kLoop, calls=%fused_computation | loop fusion | flops 2129920 | bytes 4259840 | tf_op jit(solution)/shard_map/concatenate | solution.py:73
  38.1 9.4 %all-to-all-done.2 = f32[16,5,8,128]{3,2,1,0:T(8,128)S(1)} async-done(((f32[16,5,8,128]{3,2,1,0:T(8,128)}), f32[16,5,8,128]{3,2,1,0:T(8,128)S(1)}, u32[]{:S(2)}, u32[]{:S(2)}) %all-to-all-start.2) | async-done | bytes 327712 | tf_op jit(solution)/shard_map/all_to_all | solution.py:17
  49.9 3.5 %all-to-all-start.3 = ((f32[4,20,8,128]{3,2,1,0:T(8,128)}), f32[4,20,8,128]{3,2,1,0:T(8,128)S(1)}, u32[]{:S(2)}, u32[]{:S(2)}) async-start(f32[4,20,8,128]{3,2,1,0:T(8,128)} %pad_maximum_fusion.8), calls=%async_computation.3 | async-start | bytes 655360 | tf_op jit(solution)/shard_map/all_to_all | solution.py:17
  54.8 4.4 %all-to-all-done.3 = f32[4,20,8,128]{3,2,1,0:T(8,128)S(1)} async-done(((f32[4,20,8,128]{3,2,1,0:T(8,128)}), f32[4,20,8,128]{3,2,1,0:T(8,128)S(1)}, u32[]{:S(2)}, u32[]{:S(2)}) %all-to-all-start.3) | async-done | bytes 327712 | tf_op jit(solution)/shard_map/all_to_all | solution.py:17
  59.9 1.6 %broadcast_in_dim.17 = f32[4,20,8,128]{3,2,1,0:T(8,128)} broadcast(f32[20,8,128]{2,1,0:T(8,128)} %reduce_sum.65), dimensions={1,2,3} | broadcast | bytes 409600 | tf_op jit(solution)/shard_map/broadcast_in_dim | solution.py:21
  61.5 11.5 %all-to-all-start.4 = ((f32[4,20,8,128]{3,2,1,0:T(8,128)}), f32[4,20,8,128]{3,2,1,0:T(8,128)S(1)}, u32[]{:S(2)}, u32[]{:S(2)}) async-start(f32[4,20,8,128]{3,2,1,0:T(8,128)} %broadcast_in_dim.17), calls=%async_computation.4 | async-start | bytes 655360 | tf_op jit(solution)/shard_map/all_to_all | solution.py:17
  73.1 1.3 maximum_bitcast_fusion.7
  74.4 1.3 maximum_bitcast_fusion.5
  75.7 1.3 maximum_bitcast_fusion.3
  79.8 10.4 %all-to-all-done.4 = f32[4,20,8,128]{3,2,1,0:T(8,128)S(1)} async-done(((f32[4,20,8,128]{3,2,1,0:T(8,128)}), f32[4,20,8,128]{3,2,1,0:T(8,128)S(1)}, u32[]{:S(2)}, u32[]{:S(2)}) %all-to-all-start.4) | async-done | bytes 327712 | tf_op jit(solution)/shard_map/all_to_all | solution.py:17
  90.8 1.6 %multiply_reduce_fusion = (f32[]{:T(128)}, f32[5,8,4,128]{3,1,2,0:T(8,128)S(1)}) fusion(f32[5,8,4,128]{3,1,2,0:T(8,128)} %bitcast.160, f32[16,512]{1,0:T(8,128)} %broadcast_bitcast_fusion.1, f32[24,512]{1,0:T(8,128)S(1)} %broadcast_bitcast_fusion, f32[5,8]{1,0:T(8,128)} %mul.44), kind=kLoop, calls=%fused_computation.43 | loop fusion | flops 122879 | bytes 245924 | tf_op jit(solution)/shard_map/reduce_sum | solution.py:98
  93.1 8.3 %all_to_all.41 = f32[4,21,8,128]{3,2,1,0:T(8,128)S(1)} all-to-all(f32[4,21,8,128]{3,2,1,0:T(8,128)S(1)} %broadcast_in_dim.18), channel_id=1, replica_groups={{0,4,8,12},{1,5,9,13},{2,6,10,14},{3,7,11,15},{16,20,24,28},{17,21,25,2..., dimensions={0} | all-to-all | bytes 688128 | tf_op jit(solution)/shard_map/all_to_all | solution.py:17
  103.9 13.9 %all_to_all.42 = f32[16,6,8,128]{3,2,1,0:T(8,128)S(1)} all-to-all(f32[16,6,8,128]{3,2,1,0:T(8,128)S(1)} %pad_maximum_fusion.3), channel_id=1, replica_groups={{0,32,64,96,128,160,192,224,256,288,320,352,384,416,448,480},{16,48,80,..., dimensions={0} | all-to-all | bytes 786432 | tf_op jit(solution)/shard_map/all_to_all | solution.py:17
  118.5 3.5 %all-to-all-start.7 = ((f32[16,5,8,128]{3,2,1,0:T(8,128)}), f32[16,5,8,128]{3,2,1,0:T(8,128)S(1)}, u32[]{:S(2)}, u32[]{:S(2)}) async-start(f32[16,5,8,128]{3,2,1,0:T(8,128)} %broadcast_in_dim.20), calls=%async_computation.7 | async-start | bytes 655360 | tf_op jit(solution)/shard_map/all_to_all | solution.py:17
  122.1 8.8 %all-to-all-done.7 = f32[16,5,8,128]{3,2,1,0:T(8,128)S(1)} async-done(((f32[16,5,8,128]{3,2,1,0:T(8,128)}), f32[16,5,8,128]{3,2,1,0:T(8,128)S(1)}, u32[]{:S(2)}, u32[]{:S(2)}) %all-to-all-start.7) | async-done | bytes 327712 | tf_op jit(solution)/shard_map/all_to_all | solution.py:17
  130.9 11.1 %all-gather = f32[162,8,128]{2,1,0:T(8,128)S(1)} all-gather(f32[81,8,128]{2,1,0:T(8,128)S(1)} %pad_maximum_fusion.5), channel_id=2, replica_groups={{0,16},{32,48},{64,80},{96,112},{128,144},{160,176},{192,208},{224,240}..., dimensions={0}, use_global_device_ids=true | all-gather | bytes 995328 | tf_op jit(solution)/shard_map/all_gather | solution.py:112
  144.1 1.2 convolution_multiply_fusion.1
  (87 shorter events, 17.4 us)
Async XLA Ops:
  0.6 3.1 %copy-start = (bf16[1024,512]{1,0:T(8,128)(2,1)S(1)}, bf16[1024,512]{1,0:T(8,128)(2,1)}, u32[]{:S(2)}) copy-start(bf16[1024,512]{1,0:T(8,128)(2,1)} %param.10) | copy-start | bytes 3145732
  0.6 3.5 %copy-start.3 = (f32[5,64,64]{2,1,0:T(8,128)S(1)}, f32[5,64,64]{2,1,0:T(8,128)}, u32[]{:S(2)}) copy-start(f32[5,64,64]{2,1,0:T(8,128)} %param.18) | copy-start | bytes 245764
  0.7 3.1 %copy-start.5 = (bf16[1024,192]{0,1:T(8,128)(2,1)S(1)}, bf16[1024,192]{0,1:T(8,128)(2,1)}, u32[]{:S(2)}) copy-start(bf16[1024,192]{0,1:T(8,128)(2,1)} %param.12) | copy-start | bytes 1179652
  4.7 15.3 %copy-start.6 = (bf16[512,256]{1,0:T(8,128)(2,1)S(1)}, bf16[512,256]{1,0:T(8,128)(2,1)}, u32[]{:S(2)}) copy-start(bf16[512,256]{1,0:T(8,128)(2,1)} %param.14) | copy-start | bytes 786436
  4.8 15.3 %copy-start.7 = (bf16[512,256]{1,0:T(8,128)(2,1)S(1)}, bf16[512,256]{1,0:T(8,128)(2,1)}, u32[]{:S(2)}) copy-start(bf16[512,256]{1,0:T(8,128)(2,1)} %param.15) | copy-start | bytes 786436
  4.8 15.3 %copy-start.9 = (f32[256]{0:T(256)S(1)}, f32[256]{0:T(256)}, u32[]{:S(2)}) copy-start(f32[256]{0:T(256)} %param.16) | copy-start | bytes 3076
  4.8 15.3 %copy-start.10 = (f32[256]{0:T(256)S(1)}, f32[256]{0:T(256)}, u32[]{:S(2)}) copy-start(f32[256]{0:T(256)} %param.17) | copy-start | bytes 3076
  16.5 15.2 %all-to-all-start.1 = ((f32[16,5,8,128]{3,2,1,0:T(8,128)}), f32[16,5,8,128]{3,2,1,0:T(8,128)S(1)}, u32[]{:S(2)}, u32[]{:S(2)}) async-start(f32[16,5,8,128]{3,2,1,0:T(8,128)} %bitcast.14), calls=%async_computation.1 | async-start | bytes 655360 | tf_op jit(solution)/shard_map/all_to_all | solution.py:17
  20.1 12.4 %copy-start.1 = (f32[512,256]{1,0:T(8,128)}, f32[512,256]{1,0:T(8,128)S(1)}, u32[]{:S(2)}) copy-start(f32[512,256]{1,0:T(8,128)S(1)} %convert_element_type.6) | copy-start | bytes 1572868
  20.1 16.2 %copy-start.8 = (f32[5,64]{1,0:T(8,128)S(1)}, f32[5,64]{1,0:T(8,128)}, u32[]{:S(2)}) copy-start(f32[5,64]{1,0:T(8,128)} %param.19) | copy-start | bytes 3844
  20.2 16.2 %copy-start.2 = (f32[512,256]{1,0:T(8,128)}, f32[512,256]{1,0:T(8,128)S(1)}, u32[]{:S(2)}) copy-start(f32[512,256]{1,0:T(8,128)S(1)} %convert_element_type.7) | copy-start | bytes 1572868
  21.4 14.9 %collective-permute-start = (f32[1040,256]{1,0:T(8,128)}, f32[1040,256]{1,0:T(8,128)}, u32[]{:S(2)}, u32[]{:S(2)}) collective-permute-start(f32[1040,256]{1,0:T(8,128)} %pad_maximum_fusion.1), channel_id=1, source_target_pairs={{0,16},{16,0},{32,48},{48,32},{64,80},{80,64},{96,112},{112,96},{1... | collective-permute-start | bytes 3194888 | tf_op jit(solution)/shard_map/ppermute | solution.py:73
  32.5 15.1 %all-to-all-start.2 = ((f32[16,5,8,128]{3,2,1,0:T(8,128)}), f32[16,5,8,128]{3,2,1,0:T(8,128)S(1)}, u32[]{:S(2)}, u32[]{:S(2)}) async-start(f32[16,5,8,128]{3,2,1,0:T(8,128)} %broadcast_in_dim.14), calls=%async_computation.2 | async-start | bytes 655360 | tf_op jit(solution)/shard_map/all_to_all | solution.py:17
  48.3 5.7 %slice-start = ((f32[5,64]{1,0:T(8,128)}), f32[3,64]{1,0:T(4,128)S(1)}, s32[]{:S(2)}) async-start(f32[5,64]{1,0:T(8,128)} %param.19), calls=%async_computation.8 | async-start | bytes 4096 | tf_op jit(solution)/shard_map/slice | solution.py:93
  49.9 9.3 %all-to-all-start.3 = ((f32[4,20,8,128]{3,2,1,0:T(8,128)}), f32[4,20,8,128]{3,2,1,0:T(8,128)S(1)}, u32[]{:S(2)}, u32[]{:S(2)}) async-start(f32[4,20,8,128]{3,2,1,0:T(8,128)} %pad_maximum_fusion.8), calls=%async_computation.3 | async-start | bytes 655360 | tf_op jit(solution)/shard_map/all_to_all | solution.py:17
  61.5 28.6 %all-to-all-start.4 = ((f32[4,20,8,128]{3,2,1,0:T(8,128)}), f32[4,20,8,128]{3,2,1,0:T(8,128)S(1)}, u32[]{:S(2)}, u32[]{:S(2)}) async-start(f32[4,20,8,128]{3,2,1,0:T(8,128)} %broadcast_in_dim.17), calls=%async_computation.4 | async-start | bytes 655360 | tf_op jit(solution)/shard_map/all_to_all | solution.py:17
  118.5 12.3 %all-to-all-start.7 = ((f32[16,5,8,128]{3,2,1,0:T(8,128)}), f32[16,5,8,128]{3,2,1,0:T(8,128)S(1)}, u32[]{:S(2)}, u32[]{:S(2)}) async-start(f32[16,5,8,128]{3,2,1,0:T(8,128)} %broadcast_in_dim.20), calls=%async_computation.7 | async-start | bytes 655360 | tf_op jit(solution)/shard_map/all_to_all | solution.py:17
  130.9 13.2 %copy-start.4 = (f32[5,64,64]{2,1,0:T(8,128)S(1)}, f32[5,64,64]{2,1,0:T(8,128)}, u32[]{:S(2)}) copy-start(f32[5,64,64]{2,1,0:T(8,128)} %param.18) | copy-start | bytes 245764

commit v4 on v0

v4 whole, which is shorter than its diff:
```python
import functools

import jax
import jax.numpy as jnp
from jax import lax
from jax.experimental import pallas as pl
from jax.experimental.pallas import tpu as pltpu
from jax.sharding import PartitionSpec as P


damping = 0.001
kl_limit = 8000.0
HI = lax.Precision.HIGHEST
F32, BF16 = jnp.float32, jnp.bfloat16

CORE_PAIRS = [[x * 8 + z * 2 + c for c in range(2)] for x in range(4) for z in range(4)]
CHIPS = [[x * 8 + z * 2 + c for x in range(4) for z in range(4)] for c in range(2)]
Y_GROUPS = [[y * 4 + z for y in range(4)] for z in range(4)]
Z_GROUPS = [[y * 4 + z for z in range(4)] for y in range(4)]

CA, CM, R = 192, 128, 64
ROWS, HALF_A, HALF_M = CA + CM, CA // 2, CM // 2
HALF = HALF_A + HALF_M
Y_A, Y_M = HALF_A // 4, HALF_M // 4
TOK_STEPS = 4


def exchange(x, axis, groups):
    return lax.all_to_all(x, axis, 0, 0, axis_index_groups=groups, tiled=True)


def copies(x, count):
    return jnp.broadcast_to(x[None], (count,) + x.shape)


def shape(*dims, dtype=F32):
    return pltpu.VMEM(dims, dtype)


def far(*arrays):
    return [pltpu.with_memory_space_constraint(a, pltpu.HBM) for a in arrays]


def near(*arrays):
    return [pltpu.with_memory_space_constraint(a, pltpu.VMEM) for a in arrays]


LIMIT = pltpu.CompilerParams(vmem_limit_bytes=12 * 2**20)
VMEM = pl.BlockSpec(memory_space=pltpu.VMEM)


def pieces(x):
    a = x.astype(BF16)
    r = x - a.astype(F32)
    b = r.astype(BF16)
    c = (r - b.astype(F32)).astype(BF16)
    return jnp.concatenate([a, b, c], axis=0)


def exact_dot(x, basis, contract):
    n = x.shape[0]
    out = lax.dot_general(pieces(x), basis, (((1,), (contract,)), ((), ())), preferred_element_type=F32)
    return (out[2 * n :] + out[n : 2 * n]) + out[:n]


def grad_kernel(scale, a_in, m_in, a_h, m_h, a_b, m_b, a_eig, m_eig, q, send, keep, wide, acc, halves):
    step = pl.program_id(0)
    part_a = lax.dot_general(a_h[...], a_in[...], (((1,), (0,)), ((), ())), preferred_element_type=F32)
    part_m = lax.dot_general(m_h[...], m_in[...], (((0,), (0,)), ((), ())), preferred_element_type=F32)

    @pl.when(step == 0)
    def _():
        acc[:CA] = part_a
        acc[CA:] = part_m
        feats, cols = a_b.shape
        t = 0
        for basis in (a_b, m_b):
            for r in range(0, feats, 16):
                block = basis[r : r + 16].astype(F32)
                for i in range(2):
                    for c in range(cols // 128):
                        wide[t] = block[i * 8 : i * 8 + 8, c * 128 : c * 128 + 128]
                        t += 1
        for eig in (a_eig, m_eig):
            for c in range(cols // 128):
                wide[t] = jnp.broadcast_to(eig[:, c * 128 : c * 128 + 128], (8, 128))
                t += 1

    @pl.when(step > 0)
    def _():
        acc[:CA] += part_a
        acc[CA:] += part_m

    @pl.when(step == pl.num_programs(0) - 1)
    def _():
        cts = acc.shape[1] // 128
        for p in range(ROWS // R):
            g = acc[p * R : (p + 1) * R] * scale
            g = lax.dot_general(q[p], g, (((0,), (0,)), ((), ())), precision=HI, preferred_element_type=F32)
            for i in range(R // 8):
                row = p * R + i * 8
                if row < CA:
                    half, local = divmod(row, HALF_A)
                else:
                    half, local = divmod(row - CA, HALF_M)
                    local += HALF_A
                for c in range(cts):
                    halves[half, local // 8 * cts + c] = g[i * 8 : i * 8 + 8, c * 128 : c * 128 + 128]
        core = lax.axis_index("dp") % 2
        send[...] = halves[1 - core]
        keep[...] = halves[core]


def core_add_kernel(keep, both, out):
    core = lax.axis_index("dp") % 2
    out[...] = keep[...] + both[1 - core]


def rows_of(tiles, rows, first=0):
    cts = tiles.shape[0] // (HALF // 8)
    return jnp.concatenate(
        [
            jnp.concatenate([tiles[(first + r) * cts + c] for c in range(cts)], axis=1)
            for r in range(rows // 8)
        ]
    )


def spread_kernel(got, out):
    total = (got[0] + got[1]) + (got[2] + got[3])
    for k in range(out.shape[0]):
        out[k] = total


def rotate_kernel(pre, own, other, out, basis):
    feats, cols = basis.shape[0] // 2, basis.shape[1] // 2
    cts = cols // 128
    for side, source in enumerate((own, other)):
        for r in range(0, 2 * feats, 16):
            t = r // 8 * cts
            for c in range(cts):
                pair = jnp.concatenate([source[t + c], source[t + cts + c]])
                basis[r : r + 16, (side * cts + c) * 128 : (side * cts + c + 1) * 128] = pair.astype(BF16)
    rot_a = exact_dot(rows_of(pre, HALF_A), basis[:feats], 0)
    rot_m = exact_dot(rows_of(pre, HALF_M, HALF_A // 8), basis[feats:], 0)
    cts = 2 * cts
    for y in range(4):
        for rot, count, first, base in ((rot_a, Y_A // 8, y * Y_A, 0), (rot_m, Y_M // 8, y * Y_M, Y_A // 8)):
            for i in range(count):
                row = first + i * 8
                for c in range(cts):
                    out[y, (base + i) * cts + c] = rot[row : row + 8, c * 128 : c * 128 + 128]


def scale_kernel(got, own, other, eig, out):
    core = lax.axis_index("dp") % 2
    y = lax.axis_index("factor") // 4
    cts = got.shape[1] // ((Y_A + Y_M) // 8)
    eigs = own.shape[0] - cts
    lane = lax.broadcasted_iota(jnp.int32, (8, R), 1)
    sub = lax.broadcasted_iota(jnp.int32, (8, R), 0)
    quad = jnp.zeros((8, 128), F32)
    for rt in range((Y_A + Y_M) // 8):
        if rt < Y_A // 8:
            row, tail = core * HALF_A + y * Y_A + rt * 8, 0
        else:
            row, tail = CA + core * HALF_M + y * Y_M + (rt - Y_A // 8) * 8, cts // 2
        values = jnp.broadcast_to(eig[pl.ds(row // R, 1), :], (8, R))
        col = jnp.sum(jnp.where(lane == sub + row % R, values, 0.0), axis=1, keepdims=True)
        for c in range(cts):
            t = rt * cts + c
            rot = (got[0, t] + got[1, t]) + (got[2, t] + got[3, t])
            source = own if c < cts // 2 else other
            scaled = rot / (col * source[eigs + tail + c % (cts // 2)] + damping)
            quad += scaled * rot
            for k in range(4):
                out[k, t] = scaled
    for k in range(4):
        out[k, out.shape[1] - 1] = quad


def back_kernel(got, basis, out):
    feats = basis.shape[0] // 2
    cts = basis.shape[1] // 128

    def gather(count, base):
        return jnp.concatenate(
            [
                jnp.concatenate([got[y, (base + i) * cts + c] for c in range(cts)], axis=1)
                for y in range(4)
                for i in range(count)
            ]
        )

    back_a = exact_dot(gather(Y_A // 8, 0), basis[:feats], 1)
    back_m = exact_dot(gather(Y_M // 8, Y_A // 8), basis[feats:], 1)
    fts = feats // 128
    per = HALF // 8 * fts // 16
    for back, count, base in ((back_a, HALF_A // 8, 0), (back_m, HALF_M // 8, HALF_A // 8)):
        for i in range(count):
            for c in range(fts):
                t = (base + i) * fts + c
                out[t // per, t % per] = back[i * 8 : i * 8 + 8, c * 128 : c * 128 + 128]
    last = got.shape[1] - 1
    quad = (got[0, last] + got[1, last]) + (got[2, last] + got[3, last])
    for k in range(16):
        out[k, per] = quad


def final_kernel(both, q, attn, mlp):
    per = both.shape[2] - 1
    fts = attn.shape[1] // 128
    quad = jnp.sum(both[0, 0, per] + both[1, 0, per], keepdims=True)
    clip = jnp.minimum(1.0, jnp.sqrt(kl_limit / quad))
    for p in range(ROWS // R):
        rows = []
        for i in range(R // 8):
            row = p * R + i * 8
            if row < CA:
                half, local = divmod(row, HALF_A)
            else:
                half, local = divmod(row - CA, HALF_M)
                local += HALF_A
            ts = [local // 8 * fts + c for c in range(fts)]
            rows.append(jnp.concatenate([both[half, t // per, t % per] for t in ts], axis=1))
        b = jnp.concatenate(rows)
        b = clip * lax.dot_general(q[p], b, (((1,), (0,)), ((), ())), precision=HI, preferred_element_type=F32)
        if p * R < CA:
            attn[p * R : (p + 1) * R] = b
        else:
            mlp[p * R - CA : (p + 1) * R - CA] = b


def body(
    attn_in,
    mlp_in,
    attn_hgrad,
    mlp_hgrad,
    attn_basis,
    mlp_basis,
    attn_eig,
    mlp_eig,
    rank_basis,
    rank_eig,
):
    tokens, feats = attn_in.shape
    cols = attn_basis.shape[1]
    scale = 1.0 / (tokens * lax.axis_size("dp"))
    half_tiles = HALF // 8 * feats // 128
    y_tiles = HALF // 32 * 2 * cols // 128
    chunk = tokens // TOK_STEPS

    def whole(*dims):
        return pl.BlockSpec(dims, lambda i: (0,) * len(dims))

    basis_tiles = 2 * (feats + 8) // 8 * cols // 128
    send, keep, wide = pl.pallas_call(
        functools.partial(grad_kernel, scale),
        grid=(TOK_STEPS,),
        in_specs=[
            pl.BlockSpec((chunk, feats), lambda i: (i, 0)),
            pl.BlockSpec((chunk, feats), lambda i: (i, 0)),
            pl.BlockSpec((CA, chunk), lambda i: (0, i)),
            pl.BlockSpec((chunk, CM), lambda i: (i, 0)),
            whole(feats, cols),
            whole(feats, cols),
            whole(1, cols),
            whole(1, cols),
            whole(5, R, R),
        ],
        out_specs=[whole(half_tiles, 8, 128), whole(half_tiles, 8, 128), whole(basis_tiles, 8, 128)],
        out_shape=[shape(half_tiles, 8, 128), shape(half_tiles, 8, 128), shape(basis_tiles, 8, 128)],
        scratch_shapes=[pltpu.VMEM((ROWS, feats), F32), pltpu.VMEM((2, half_tiles, 8, 128), F32)],
        compiler_params=LIMIT,
        name="grad",
    )(
        *far(
            attn_in,
            mlp_in,
            attn_hgrad.T,
            mlp_hgrad,
            attn_basis,
            mlp_basis,
            attn_eig.reshape(1, -1),
            mlp_eig.reshape(1, -1),
            rank_basis,
        )
    )
    other = lax.ppermute(wide, "dp", [(i, i ^ 1) for i in range(lax.axis_size("dp"))])
    both = lax.all_gather(send, "dp", axis_index_groups=CORE_PAIRS)
    part = pl.pallas_call(
        core_add_kernel,
        in_specs=[VMEM] * 2,
        out_specs=VMEM,
        out_shape=shape(half_tiles, 8, 128),
        compiler_params=LIMIT,
        name="core_add",
    )(*near(keep, both))
    shard, other = lax.optimization_barrier((exchange(part.reshape(16, -1, 8, 128), "dp", CHIPS), other))
    shard = jnp.sum(shard, axis=0)
    pre = exchange(copies(shard, 16), "dp", CHIPS).reshape(-1, 8, 128)

    block, basis = pl.pallas_call(
        rotate_kernel,
        in_specs=[VMEM] * 3,
        out_specs=[VMEM] * 2,
        out_shape=[shape(4, y_tiles, 8, 128), shape(2 * feats, 2 * cols, dtype=BF16)],
        compiler_params=LIMIT,
        name="rotate",
    )(*near(pre, wide, other))
    block = pl.pallas_call(
        spread_kernel,
        in_specs=[VMEM],
        out_specs=VMEM,
        out_shape=shape(4, y_tiles, 8, 128),
        compiler_params=LIMIT,
        name="spread",
    )(*near(exchange(block, "factor", Y_GROUPS)))
    block = exchange(block, "factor", Z_GROUPS)
    scaled = pl.pallas_call(
        scale_kernel,
        in_specs=[VMEM] * 4,
        out_specs=VMEM,
        out_shape=shape(4, y_tiles + 1, 8, 128),
        compiler_params=LIMIT,
        name="scale",
    )(*near(block, wide, other, rank_eig))
    scaled = exchange(scaled, "factor", Y_GROUPS)
    back = pl.pallas_call(
        back_kernel,
        in_specs=[VMEM] * 2,
        out_specs=VMEM,
        out_shape=shape(16, half_tiles // 16 + 1, 8, 128),
        compiler_params=LIMIT, name="back",
    )(*near(scaled, basis))
    summed = jnp.sum(exchange(back, "dp", CHIPS), axis=0)
    back = exchange(copies(summed, 16), "dp", CHIPS)
    both = lax.all_gather(back, "dp", axis_index_groups=CORE_PAIRS)
    return tuple(
        pl.pallas_call(
            final_kernel,
            in_specs=[VMEM] * 2,
            out_specs=[VMEM] * 2,
            out_shape=[jax.ShapeDtypeStruct((CA, feats), F32), jax.ShapeDtypeStruct((CM, feats), F32)],
            compiler_params=LIMIT, name="final",
        )(*near(both, rank_basis))
    )


def solution(mesh):
    in_specs = (
        P("dp", "factor"),
        P("dp", "factor"),
        P("dp", None),
        P("dp", None),
        P("factor", "dp"),
        P("factor", "dp"),
        P("dp"),
        P("dp"),
        P(),
        P(),
    )
    out_specs = (P(None, "factor"), P(None, "factor"))


    return jax.shard_map(body, mesh=mesh, in_specs=in_specs, out_specs=out_specs, check_vma=False)
```

time: 855 us -> 132 us (0.15)
  waiting for transfers between devices: 768 us -> 9.39 us
  blocking collectives: 46.3 us -> 108 us
  between operations: 15.9 us -> 0.72 us
  matrix products: 12.5 us -> 0 us
    psum x3 -> x0, waiting for transfers between devices: 768 us -> none  [the longest x1 289 us: one_group(): back = lax.psum(back_part, 'dp')]
    all_to_all x0 -> x6, blocking collectives: none -> 89.2 us  [exchange(): return lax.all_to_all(x, axis, 0, 0, axis_index_groups=groups, tiled=True)]
    psum x1 -> x0, blocking collectives: 46.3 us -> none  [body(): quad = lax.psum(local_quad, 'factor')]
    all_gather x0 -> x2, blocking collectives: none -> 18.6 us  [the longest x1 9.86 us: body(): both = lax.all_gather(back, 'dp', axis_index_groups=CORE_PAIRS)]
    dot_general x10 -> x0, matrix products: 12.5 us -> none  [the longest x2 3.56 us: one_group(): lax.dot_general(hgrad, inputs, (((0,), (0,)), ((), ())), preferred_elemen...]
  transfers between devices with their start and end apart: 3 -> 2, of which waited for: 3 -> 2; matrix products, arithmetic and copies ran while one was open for 0% -> 0% of each run, Pallas kernels for 0% -> 0%
where the time goes in v4:
time: 132 us
  blocking collectives  108 us (82%)
  waiting for transfers between devices  9.39 us (7%)
  Pallas kernels  7.65 us (6%)
  starting transfers between devices  5.83 us (4%)
    all_to_all x6, blocking collectives, exchange(): return lax.all_to_all(x, axis, 0, 0, axis_index_groups=groups, tiled=True)  89.2 us
    all_gather x1, blocking collectives, body(): both = lax.all_gather(back, 'dp', axis_index_groups=CORE_PAIRS)  9.86 us
    all_gather x1, blocking collectives, body(): both = lax.all_gather(send, 'dp', axis_index_groups=CORE_PAIRS)  8.74 us
    all_to_all x1, waiting for transfers between devices, exchange(): return lax.all_to_all(x, axis, 0, 0, axis_index_groups=groups, tiled=True)  7.1 us
    pallas_call x1, Pallas kernels, body(): pl.pallas_call(functools.partial(grad_kernel, scale), grid=(TOK_STEPS,),...  4.4 us
    all_to_all x1, starting transfers between devices, exchange(): return lax.all_to_all(x, axis, 0, 0, axis_index_groups=groups, tiled=True)  3.54 us
  transfers between devices with their start and end apart: 2, of which 2 were waited for; matrix products, arithmetic and copies ran while one was open for 0% of the time, Pallas kernels for 0%

profile of v4, /device:TPU:1, one launch (start us, length us, event | category | flops | bytes accessed | tf_op | source)
XLA Modules:
  0.0 131.5 jit_solution(2985320903593530808)
XLA Ops:
  0.6 4.4 %grad.1 = (f32[80,8,128]{2,1,0:T(8,128)S(1)}, f32[80,8,128]{2,1,0:T(8,128)S(1)}, f32[260,8,128]{2,1,0:T(8,128)S(1)}) custom-call(bf16[1024,512]{1,0:T(8,128)(2,1)} %a_in.1, bf16[1024,512]{1,0:T(8,128)(2,1)} %m_in.1, bf16[192,1024]{1,0:T(8,128)(2,1)} %bitcast.10, bf16[1024,128]{1,0:T(8,128)(2,1)} %m_h.1, bf16[512,256]{1,0:T(8,128)(2,1)} %a_b.1, ...), custom_call_target="tpu_custom_call" | custom-call | tf_op jit(solution)/shard_map/grad/pallas_call | solution.py:257
  5.0 8.7 %all-gather = f32[160,8,128]{2,1,0:T(8,128)S(1)} all-gather(f32[80,8,128]{2,1,0:T(8,128)S(1)} %get-tuple-element.10), channel_id=2, replica_groups={{0,16},{32,48},{64,80},{96,112},{128,144},{160,176},{192,208},{224,240}..., dimensions={0}, use_global_device_ids=true | all-gather | bytes 983040 | tf_op jit(solution)/shard_map/all_gather | solution.py:290
  13.8 0.8 core_add.1
  14.5 3.5 %all-to-all-start = ((f32[16,5,8,128]{3,2,1,0:T(8,128)}), f32[16,5,8,128]{3,2,1,0:T(8,128)S(1)}, u32[]{:S(2)}, u32[]{:S(2)}) async-start(f32[16,5,8,128]{3,2,1,0:T(8,128)} %bitcast.4), calls=%async_computation | async-start | bytes 655360 | tf_op jit(solution)/shard_map/all_to_all | solution.py:29
  18.1 2.3 %collective-permute-start = (f32[260,8,128]{2,1,0:T(8,128)S(1)}, f32[260,8,128]{2,1,0:T(8,128)S(1)}, u32[]{:S(2)}, u32[]{:S(2)}) collective-permute-start(f32[260,8,128]{2,1,0:T(8,128)S(1)} %get-tuple-element.11.own), channel_id=1, source_target_pairs={{0,16},{16,0},{32,48},{48,32},{64,80},{80,64},{96,112},{112,96},{1... | collective-permute-start | bytes 3194888 | tf_op jit(solution)/shard_map/ppermute | solution.py:289
  20.4 2.3 %collective-permute-done.other = f32[260,8,128]{2,1,0:T(8,128)S(1)} collective-permute-done((f32[260,8,128]{2,1,0:T(8,128)S(1)}, f32[260,8,128]{2,1,0:T(8,128)S(1)}, u32[]{:S(2)}, u32[]{:S(2)}) %collective-permute-start) | collective-permute-done | bytes 1064992 | tf_op jit(solution)/shard_map/ppermute | solution.py:289
  22.7 7.1 %all-to-all-done = f32[16,5,8,128]{3,2,1,0:T(8,128)S(1)} async-done(((f32[16,5,8,128]{3,2,1,0:T(8,128)}), f32[16,5,8,128]{3,2,1,0:T(8,128)S(1)}, u32[]{:S(2)}, u32[]{:S(2)}) %all-to-all-start) | async-done | bytes 327712 | tf_op jit(solution)/shard_map/all_to_all | solution.py:29
  29.8 14.9 %all_to_all.35 = f32[16,5,8,128]{3,2,1,0:T(8,128)S(1)} all-to-all(f32[16,5,8,128]{3,2,1,0:T(8,128)S(1)} %broadcast_in_dim.4), channel_id=1, replica_groups={{0,32,64,96,128,160,192,224,256,288,320,352,384,416,448,480},{16,48,80,..., dimensions={0} | all-to-all | bytes 655360 | tf_op jit(solution)/shard_map/all_to_all | solution.py:29
  44.7 0.5 rotate.1
  45.2 0.0 copy-start.1
  45.2 8.9 %all_to_all.36.got = f32[4,20,8,128]{3,2,1,0:T(8,128)S(1)} all-to-all(f32[4,20,8,128]{3,2,1,0:T(8,128)S(1)} %get-tuple-element.14), channel_id=1, replica_groups={{0,4,8,12},{1,5,9,13},{2,6,10,14},{3,7,11,15},{16,20,24,28},{17,21,25,2..., dimensions={0} | all-to-all | bytes 655360 | tf_op jit(solution)/shard_map/all_to_all | solution.py:29
  54.1 29.9 %all_to_all.37.got = f32[4,20,8,128]{3,2,1,0:T(8,128)S(1)} all-to-all(f32[4,20,8,128]{3,2,1,0:T(8,128)S(1)} %spread.1), channel_id=1, replica_groups={{0,1,2,3},{4,5,6,7},{8,9,10,11},{12,13,14,15},{16,17,18,19},{20,21,22,2..., dimensions={0} | all-to-all | bytes 655360 | tf_op jit(solution)/shard_map/all_to_all | solution.py:29
  84.1 0.0 copy-done.1
  84.1 0.1 scale.1
  84.2 8.3 %all_to_all.38.got = f32[4,21,8,128]{3,2,1,0:T(8,128)S(1)} all-to-all(f32[4,21,8,128]{3,2,1,0:T(8,128)S(1)} %scale.1), channel_id=1, replica_groups={{0,4,8,12},{1,5,9,13},{2,6,10,14},{3,7,11,15},{16,20,24,28},{17,21,25,2..., dimensions={0} | all-to-all | bytes 688128 | tf_op jit(solution)/shard_map/all_to_all | solution.py:29
  92.5 0.5 back.1
  93.0 14.7 %all_to_all.39 = f32[16,6,8,128]{3,2,1,0:T(8,128)S(1)} all-to-all(f32[16,6,8,128]{3,2,1,0:T(8,128)S(1)} %back.1), channel_id=1, replica_groups={{0,32,64,96,128,160,192,224,256,288,320,352,384,416,448,480},{16,48,80,..., dimensions={0} | all-to-all | bytes 786432 | tf_op jit(solution)/shard_map/all_to_all | solution.py:29
  107.8 0.0 copy-start
  107.8 12.5 %all_to_all.40 = f32[16,6,8,128]{3,2,1,0:T(8,128)S(1)} all-to-all(f32[16,6,8,128]{3,2,1,0:T(8,128)S(1)} %broadcast_in_dim.5), channel_id=1, replica_groups={{0,32,64,96,128,160,192,224,256,288,320,352,384,416,448,480},{16,48,80,..., dimensions={0} | all-to-all | bytes 786432 | tf_op jit(solution)/shard_map/all_to_all | solution.py:29
  120.3 9.9 %all-gather.1 = f32[32,6,8,128]{3,2,1,0:T(8,128)S(1)} all-gather(f32[16,6,8,128]{3,2,1,0:T(8,128)S(1)} %all_to_all.40), channel_id=3, replica_groups={{0,16},{32,48},{64,80},{96,112},{128,144},{160,176},{192,208},{224,240}..., dimensions={0}, use_global_device_ids=true | all-gather | bytes 1179648 | tf_op jit(solution)/shard_map/all_gather | solution.py:338
  130.1 0.0 copy-done
  130.1 1.4 %final.1 = (f32[192,512]{1,0:T(8,128)}, f32[128,512]{1,0:T(8,128)}) custom-call(f32[2,16,6,8,128]{4,3,2,1,0:T(8,128)S(1)} %bitcast.7, f32[5,64,64]{2,1,0:T(8,128)S(1)} %copy-done), custom_call_target="tpu_custom_call" | custom-call | tf_op jit(solution)/shard_map/final/pallas_call | solution.py:340
  (5 shorter events, 0.1 us)
Async XLA Ops:
  14.5 15.2 %all-to-all-start = ((f32[16,5,8,128]{3,2,1,0:T(8,128)}), f32[16,5,8,128]{3,2,1,0:T(8,128)S(1)}, u32[]{:S(2)}, u32[]{:S(2)}) async-start(f32[16,5,8,128]{3,2,1,0:T(8,128)} %bitcast.4), calls=%async_computation | async-start | bytes 655360 | tf_op jit(solution)/shard_map/all_to_all | solution.py:29
  18.1 4.6 %collective-permute-start = (f32[260,8,128]{2,1,0:T(8,128)S(1)}, f32[260,8,128]{2,1,0:T(8,128)S(1)}, u32[]{:S(2)}, u32[]{:S(2)}) collective-permute-start(f32[260,8,128]{2,1,0:T(8,128)S(1)} %get-tuple-element.11.own), channel_id=1, source_target_pairs={{0,16},{16,0},{32,48},{48,32},{64,80},{80,64},{96,112},{112,96},{1... | collective-permute-start | bytes 3194888 | tf_op jit(solution)/shard_map/ppermute | solution.py:289
  45.2 38.9 %copy-start.1 = (f32[5,64]{1,0:T(8,128)S(1)}, f32[5,64]{1,0:T(8,128)}, u32[]{:S(2)}) copy-start(f32[5,64]{1,0:T(8,128)} %eig.1) | copy-start | bytes 3844
  107.8 22.4 %copy-start = (f32[5,64,64]{2,1,0:T(8,128)S(1)}, f32[5,64,64]{2,1,0:T(8,128)}, u32[]{:S(2)}) copy-start(f32[5,64,64]{2,1,0:T(8,128)} %q.3) | copy-start | bytes 245764

commit v5 on v4

--- a/solution.py
+++ b/solution.py
@@ -16,13 +16,14 @@
 CORE_PAIRS = [[x * 8 + z * 2 + c for c in range(2)] for x in range(4) for z in range(4)]
 CHIPS = [[x * 8 + z * 2 + c for x in range(4) for z in range(4)] for c in range(2)]
 Y_GROUPS = [[y * 4 + z for y in range(4)] for z in range(4)]
-Z_GROUPS = [[y * 4 + z for z in range(4)] for y in range(4)]
+Z_PAIRS = [(y * 4 + z, y * 4 + (z ^ 1)) for y in range(4) for z in range(4)]
+Z_CROSS = [(y * 4 + z, y * 4 + 3 - z) for y in range(4) for z in range(4)]
 
 CA, CM, R = 192, 128, 64
 ROWS, HALF_A, HALF_M = CA + CM, CA // 2, CM // 2
 HALF = HALF_A + HALF_M
 Y_A, Y_M = HALF_A // 4, HALF_M // 4
-TOK_STEPS = 4
+TOK_STEPS = 1
 
 
 def exchange(x, axis, groups):
@@ -126,10 +127,12 @@
     )
 
 
-def spread_kernel(got, out):
-    total = (got[0] + got[1]) + (got[2] + got[3])
-    for k in range(out.shape[0]):
-        out[k] = total
+def sum_kernel(got, out):
+    out[...] = (got[0] + got[1]) + (got[2] + got[3])
+
+
+def add_kernel(one, two, out):
+    out[...] = one[...] + two[...]
 
 
 def rotate_kernel(pre, own, other, out, basis):
@@ -152,10 +155,10 @@
                     out[y, (base + i) * cts + c] = rot[row : row + 8, c * 128 : c * 128 + 128]
 
 
-def scale_kernel(got, own, other, eig, out):
+def scale_kernel(one, two, own, other, eig, out):
     core = lax.axis_index("dp") % 2
     y = lax.axis_index("factor") // 4
-    cts = got.shape[1] // ((Y_A + Y_M) // 8)
+    cts = one.shape[0] // ((Y_A + Y_M) // 8)
     eigs = own.shape[0] - cts
     lane = lax.broadcasted_iota(jnp.int32, (8, R), 1)
     sub = lax.broadcasted_iota(jnp.int32, (8, R), 0)
@@ -169,7 +172,7 @@
         col = jnp.sum(jnp.where(lane == sub + row % R, values, 0.0), axis=1, keepdims=True)
         for c in range(cts):
             t = rt * cts + c
-            rot = (got[0, t] + got[1, t]) + (got[2, t] + got[3, t])
+            rot = one[t] + two[t]
             source = own if c < cts // 2 else other
             scaled = rot / (col * source[eigs + tail + c % (cts // 2)] + damping)
             quad += scaled * rot
@@ -309,22 +312,30 @@
         name="rotate",
     )(*near(pre, wide, other))
     block = pl.pallas_call(
-        spread_kernel,
+        sum_kernel,
         in_specs=[VMEM],
         out_specs=VMEM,
-        out_shape=shape(4, y_tiles, 8, 128),
-        compiler_params=LIMIT,
-        name="spread",
+        out_shape=shape(y_tiles, 8, 128),
+        compiler_params=LIMIT,
+        name="y_sum",
     )(*near(exchange(block, "factor", Y_GROUPS)))
-    block = exchange(block, "factor", Z_GROUPS)
+    block = pl.pallas_call(
+        add_kernel,
+        in_specs=[VMEM] * 2,
+        out_specs=VMEM,
+        out_shape=shape(y_tiles, 8, 128),
+        compiler_params=LIMIT,
+        name="z_add",
+    )(*near(block, lax.ppermute(block, "factor", Z_PAIRS)))
+    across = lax.ppermute(block, "factor", Z_CROSS)
     scaled = pl.pallas_call(
         scale_kernel,
-        in_specs=[VMEM] * 4,
+        in_specs=[VMEM] * 5,
         out_specs=VMEM,
         out_shape=shape(4, y_tiles + 1, 8, 128),
         compiler_params=LIMIT,
         name="scale",
-    )(*near(block, wide, other, rank_eig))
+    )(*near(block, across, wide, other, rank_eig))
     scaled = exchange(scaled, "factor", Y_GROUPS)
     back = pl.pallas_call(
         back_kernel,

time: 132 us -> 127 us (0.962)
  blocking collectives: 108 us -> 82 us
  starting transfers between devices: 5.83 us -> 21.6 us
  waiting for transfers between devices: 9.39 us -> 15.2 us
  Pallas kernels: 7.65 us -> 6.33 us
    all_to_all x6 -> x5, blocking collectives: 89.2 us -> 59.8 us  [exchange(): return lax.all_to_all(x, axis, 0, 0, axis_index_groups=groups, tiled=True)]
    ppermute x0 -> x2, starting transfers between devices: none -> 15.8 us  [the longest x1 8.82 us: body(): lax.ppermute(block, 'factor', Z_PAIRS)]
    ppermute x0 -> x2, waiting for transfers between devices: none -> 5.76 us  [the longest x1 3.14 us: body(): lax.ppermute(block, 'factor', Z_PAIRS)]
    all_gather x1, blocking collectives: 9.86 us -> 13.5 us  [body(): both = lax.all_gather(back, 'dp', axis_index_groups=CORE_PAIRS)]
  transfers between devices with their start and end apart: 2 -> 4, of which waited for: 2 -> 4; matrix products, arithmetic and copies ran while one was open for 0% -> 0% of each run, Pallas kernels for 0% -> 0%
where the time goes in v5:
time: 127 us; the launch traced here: 126 us
  blocking collectives  82 us (65%)
  starting transfers between devices  21.6 us (17%)
  waiting for transfers between devices  15.2 us (12%)
  Pallas kernels  6.33 us (5%)
    all_to_all x5, blocking collectives, exchange(): return lax.all_to_all(x, axis, 0, 0, axis_index_groups=groups, tiled=True)  59.8 us
    all_gather x1, blocking collectives, body(): both = lax.all_gather(back, 'dp', axis_index_groups=CORE_PAIRS)  13.5 us
    ppermute x1, starting transfers between devices, body(): lax.ppermute(block, 'factor', Z_PAIRS)  8.82 us
    all_gather x1, blocking collectives, body(): both = lax.all_gather(send, 'dp', axis_index_groups=CORE_PAIRS)  8.74 us
    all_to_all x1, waiting for transfers between devices, exchange(): return lax.all_to_all(x, axis, 0, 0, axis_index_groups=groups, tiled=True)  7.1 us
    ppermute x1, starting transfers between devices, body(): across = lax.ppermute(block, 'factor', Z_CROSS)  6.99 us
    all_to_all x1, starting transfers between devices, exchange(): return lax.all_to_all(x, axis, 0, 0, axis_index_groups=groups, tiled=True)  3.54 us
    ppermute x1, waiting for transfers between devices, body(): lax.ppermute(block, 'factor', Z_PAIRS)  3.14 us
  transfers between devices with their start and end apart: 4, of which 4 were waited for; matrix products, arithmetic and copies ran while one was open for 0% of the time, Pallas kernels for 0%

profile of v5, /device:TPU:1, one launch (start us, length us, event | category | flops | bytes accessed | tf_op | source)
XLA Modules:
  0.0 126.0 jit_solution(13804668937511940074)
XLA Ops:
  0.6 3.1 %grad.1 = (f32[80,8,128]{2,1,0:T(8,128)S(1)}, f32[80,8,128]{2,1,0:T(8,128)S(1)}, f32[260,8,128]{2,1,0:T(8,128)S(1)}) custom-call(bf16[1024,512]{1,0:T(8,128)(2,1)} %a_in.1, bf16[1024,512]{1,0:T(8,128)(2,1)} %m_in.1, bf16[192,1024]{1,0:T(8,128)(2,1)} %bitcast.10, bf16[1024,128]{1,0:T(8,128)(2,1)} %m_h.1, bf16[512,256]{1,0:T(8,128)(2,1)} %a_b.1, ...), custom_call_target="tpu_custom_call" | custom-call | tf_op jit(solution)/shard_map/grad/pallas_call | solution.py:260
  3.7 8.7 %all-gather = f32[160,8,128]{2,1,0:T(8,128)S(1)} all-gather(f32[80,8,128]{2,1,0:T(8,128)S(1)} %get-tuple-element.10), channel_id=2, replica_groups={{0,16},{32,48},{64,80},{96,112},{128,144},{160,176},{192,208},{224,240}..., dimensions={0}, use_global_device_ids=true | all-gather | bytes 983040 | tf_op jit(solution)/shard_map/all_gather | solution.py:293
  12.5 0.8 core_add.1
  13.2 3.5 %all-to-all-start = ((f32[16,5,8,128]{3,2,1,0:T(8,128)}), f32[16,5,8,128]{3,2,1,0:T(8,128)S(1)}, u32[]{:S(2)}, u32[]{:S(2)}) async-start(f32[16,5,8,128]{3,2,1,0:T(8,128)} %bitcast.4), calls=%async_computation | async-start | bytes 655360 | tf_op jit(solution)/shard_map/all_to_all | solution.py:30
  16.8 2.3 %collective-permute-start = (f32[260,8,128]{2,1,0:T(8,128)S(1)}, f32[260,8,128]{2,1,0:T(8,128)S(1)}, u32[]{:S(2)}, u32[]{:S(2)}) collective-permute-start(f32[260,8,128]{2,1,0:T(8,128)S(1)} %get-tuple-element.11.own), channel_id=1, source_target_pairs={{0,16},{16,0},{32,48},{48,32},{64,80},{80,64},{96,112},{112,96},{1... | collective-permute-start | bytes 3194888 | tf_op jit(solution)/shard_map/ppermute | solution.py:292
  19.1 2.3 %collective-permute-done.other = f32[260,8,128]{2,1,0:T(8,128)S(1)} collective-permute-done((f32[260,8,128]{2,1,0:T(8,128)S(1)}, f32[260,8,128]{2,1,0:T(8,128)S(1)}, u32[]{:S(2)}, u32[]{:S(2)}) %collective-permute-start) | collective-permute-done | bytes 1064992 | tf_op jit(solution)/shard_map/ppermute | solution.py:292
  21.4 7.1 %all-to-all-done = f32[16,5,8,128]{3,2,1,0:T(8,128)S(1)} async-done(((f32[16,5,8,128]{3,2,1,0:T(8,128)}), f32[16,5,8,128]{3,2,1,0:T(8,128)S(1)}, u32[]{:S(2)}, u32[]{:S(2)}) %all-to-all-start) | async-done | bytes 327712 | tf_op jit(solution)/shard_map/all_to_all | solution.py:30
  28.5 14.9 %all_to_all.30 = f32[16,5,8,128]{3,2,1,0:T(8,128)S(1)} all-to-all(f32[16,5,8,128]{3,2,1,0:T(8,128)S(1)} %broadcast_in_dim.4), channel_id=1, replica_groups={{0,32,64,96,128,160,192,224,256,288,320,352,384,416,448,480},{16,48,80,..., dimensions={0} | all-to-all | bytes 655360 | tf_op jit(solution)/shard_map/all_to_all | solution.py:30
  43.4 0.5 rotate.1
  43.9 0.0 copy-start.1
  43.9 8.9 %all_to_all.31.got = f32[4,20,8,128]{3,2,1,0:T(8,128)S(1)} all-to-all(f32[4,20,8,128]{3,2,1,0:T(8,128)S(1)} %get-tuple-element.14), channel_id=1, replica_groups={{0,4,8,12},{1,5,9,13},{2,6,10,14},{3,7,11,15},{16,20,24,28},{17,21,25,2..., dimensions={0} | all-to-all | bytes 655360 | tf_op jit(solution)/shard_map/all_to_all | solution.py:30
  52.8 8.8 %collective-permute-start.1 = (f32[20,8,128]{2,1,0:T(8,128)S(1)}, f32[20,8,128]{2,1,0:T(8,128)S(1)}, u32[]{:S(2)}, u32[]{:S(2)}) collective-permute-start(f32[20,8,128]{2,1,0:T(8,128)S(1)} %y_sum.1.one), channel_id=1, source_target_pairs={{0,1},{1,0},{2,3},{3,2},{4,5},{5,4},{6,7},{7,6},{8,9},{9,8},{10,11... | collective-permute-start | bytes 245768 | tf_op jit(solution)/shard_map/ppermute | solution.py:329
  61.6 3.1 %collective-permute-done.1.two = f32[20,8,128]{2,1,0:T(8,128)S(1)} collective-permute-done((f32[20,8,128]{2,1,0:T(8,128)S(1)}, f32[20,8,128]{2,1,0:T(8,128)S(1)}, u32[]{:S(2)}, u32[]{:S(2)}) %collective-permute-start.1) | collective-permute-done | bytes 81952 | tf_op jit(solution)/shard_map/ppermute | solution.py:329
  64.8 7.0 %collective-permute-start.2 = (f32[20,8,128]{2,1,0:T(8,128)S(1)}, f32[20,8,128]{2,1,0:T(8,128)S(1)}, u32[]{:S(2)}, u32[]{:S(2)}) collective-permute-start(f32[20,8,128]{2,1,0:T(8,128)S(1)} %z_add.1.one), channel_id=1, source_target_pairs={{0,3},{1,2},{2,1},{3,0},{4,7},{5,6},{6,5},{7,4},{8,11},{9,10},{10,... | collective-permute-start | bytes 245768 | tf_op jit(solution)/shard_map/ppermute | solution.py:330
  71.8 2.6 %collective-permute-done.2.two = f32[20,8,128]{2,1,0:T(8,128)S(1)} collective-permute-done((f32[20,8,128]{2,1,0:T(8,128)S(1)}, f32[20,8,128]{2,1,0:T(8,128)S(1)}, u32[]{:S(2)}, u32[]{:S(2)}) %collective-permute-start.2) | collective-permute-done | bytes 81952 | tf_op jit(solution)/shard_map/ppermute | solution.py:330
  74.4 0.1 scale.1
  74.5 10.6 %all_to_all.32.got = f32[4,21,8,128]{3,2,1,0:T(8,128)S(1)} all-to-all(f32[4,21,8,128]{3,2,1,0:T(8,128)S(1)} %scale.1), channel_id=1, replica_groups={{0,4,8,12},{1,5,9,13},{2,6,10,14},{3,7,11,15},{16,20,24,28},{17,21,25,2..., dimensions={0} | all-to-all | bytes 688128 | tf_op jit(solution)/shard_map/all_to_all | solution.py:30
  85.2 0.5 back.1
  85.6 12.8 %all_to_all.33 = f32[16,6,8,128]{3,2,1,0:T(8,128)S(1)} all-to-all(f32[16,6,8,128]{3,2,1,0:T(8,128)S(1)} %back.1), channel_id=1, replica_groups={{0,32,64,96,128,160,192,224,256,288,320,352,384,416,448,480},{16,48,80,..., dimensions={0} | all-to-all | bytes 786432 | tf_op jit(solution)/shard_map/all_to_all | solution.py:30
  98.5 0.0 copy-start
  98.5 12.6 %all_to_all.34 = f32[16,6,8,128]{3,2,1,0:T(8,128)S(1)} all-to-all(f32[16,6,8,128]{3,2,1,0:T(8,128)S(1)} %broadcast_in_dim.5), channel_id=1, replica_groups={{0,32,64,96,128,160,192,224,256,288,320,352,384,416,448,480},{16,48,80,..., dimensions={0} | all-to-all | bytes 786432 | tf_op jit(solution)/shard_map/all_to_all | solution.py:30
  111.1 13.5 %all-gather.1 = f32[32,6,8,128]{3,2,1,0:T(8,128)S(1)} all-gather(f32[16,6,8,128]{3,2,1,0:T(8,128)S(1)} %all_to_all.34), channel_id=3, replica_groups={{0,16},{32,48},{64,80},{96,112},{128,144},{160,176},{192,208},{224,240}..., dimensions={0}, use_global_device_ids=true | all-gather | bytes 1179648 | tf_op jit(solution)/shard_map/all_gather | solution.py:349
  124.6 0.0 copy-done
  124.6 1.4 %final.1 = (f32[192,512]{1,0:T(8,128)}, f32[128,512]{1,0:T(8,128)}) custom-call(f32[2,16,6,8,128]{4,3,2,1,0:T(8,128)S(1)} %bitcast.7, f32[5,64,64]{2,1,0:T(8,128)S(1)} %copy-done), custom_call_target="tpu_custom_call" | custom-call | tf_op jit(solution)/shard_map/final/pallas_call | solution.py:351
  (7 shorter events, 0.1 us)
Async XLA Ops:
  13.2 15.2 %all-to-all-start = ((f32[16,5,8,128]{3,2,1,0:T(8,128)}), f32[16,5,8,128]{3,2,1,0:T(8,128)S(1)}, u32[]{:S(2)}, u32[]{:S(2)}) async-start(f32[16,5,8,128]{3,2,1,0:T(8,128)} %bitcast.4), calls=%async_computation | async-start | bytes 655360 | tf_op jit(solution)/shard_map/all_to_all | solution.py:30
  16.8 4.6 %collective-permute-start = (f32[260,8,128]{2,1,0:T(8,128)S(1)}, f32[260,8,128]{2,1,0:T(8,128)S(1)}, u32[]{:S(2)}, u32[]{:S(2)}) collective-permute-start(f32[260,8,128]{2,1,0:T(8,128)S(1)} %get-tuple-element.11.own), channel_id=1, source_target_pairs={{0,16},{16,0},{32,48},{48,32},{64,80},{80,64},{96,112},{112,96},{1... | collective-permute-start | bytes 3194888 | tf_op jit(solution)/shard_map/ppermute | solution.py:292
  43.9 30.5 %copy-start.1 = (f32[5,64]{1,0:T(8,128)S(1)}, f32[5,64]{1,0:T(8,128)}, u32[]{:S(2)}) copy-start(f32[5,64]{1,0:T(8,128)} %eig.1) | copy-start | bytes 3844
  52.8 12.0 %collective-permute-start.1 = (f32[20,8,128]{2,1,0:T(8,128)S(1)}, f32[20,8,128]{2,1,0:T(8,128)S(1)}, u32[]{:S(2)}, u32[]{:S(2)}) collective-permute-start(f32[20,8,128]{2,1,0:T(8,128)S(1)} %y_sum.1.one), channel_id=1, source_target_pairs={{0,1},{1,0},{2,3},{3,2},{4,5},{5,4},{6,7},{7,6},{8,9},{9,8},{10,11... | collective-permute-start | bytes 245768 | tf_op jit(solution)/shard_map/ppermute | solution.py:329
  64.8 9.6 %collective-permute-start.2 = (f32[20,8,128]{2,1,0:T(8,128)S(1)}, f32[20,8,128]{2,1,0:T(8,128)S(1)}, u32[]{:S(2)}, u32[]{:S(2)}) collective-permute-start(f32[20,8,128]{2,1,0:T(8,128)S(1)} %z_add.1.one), channel_id=1, source_target_pairs={{0,3},{1,2},{2,1},{3,0},{4,7},{5,6},{6,5},{7,4},{8,11},{9,10},{10,... | collective-permute-start | bytes 245768 | tf_op jit(solution)/shard_map/ppermute | solution.py:330
  98.5 26.2 %copy-start = (f32[5,64,64]{2,1,0:T(8,128)S(1)}, f32[5,64,64]{2,1,0:T(8,128)}, u32[]{:S(2)}) copy-start(f32[5,64,64]{2,1,0:T(8,128)} %q.3) | copy-start | bytes 245764

commit v6 on v5

--- a/solution.py
+++ b/solution.py
@@ -23,7 +23,6 @@
 ROWS, HALF_A, HALF_M = CA + CM, CA // 2, CM // 2
 HALF = HALF_A + HALF_M
 Y_A, Y_M = HALF_A // 4, HALF_M // 4
-TOK_STEPS = 1
 
 
 def exchange(x, axis, groups):
@@ -48,6 +47,7 @@
 
 LIMIT = pltpu.CompilerParams(vmem_limit_bytes=12 * 2**20)
 VMEM = pl.BlockSpec(memory_space=pltpu.VMEM)
+HBM = pl.BlockSpec(memory_space=pltpu.HBM)
 
 
 def pieces(x):
@@ -64,52 +64,53 @@
     return (out[2 * n :] + out[n : 2 * n]) + out[:n]
 
 
-def grad_kernel(scale, a_in, m_in, a_h, m_h, a_b, m_b, a_eig, m_eig, q, send, keep, wide, acc, halves):
-    step = pl.program_id(0)
-    part_a = lax.dot_general(a_h[...], a_in[...], (((1,), (0,)), ((), ())), preferred_element_type=F32)
-    part_m = lax.dot_general(m_h[...], m_in[...], (((0,), (0,)), ((), ())), preferred_element_type=F32)
-
-    @pl.when(step == 0)
-    def _():
-        acc[:CA] = part_a
-        acc[CA:] = part_m
-        feats, cols = a_b.shape
-        t = 0
-        for basis in (a_b, m_b):
-            for r in range(0, feats, 16):
-                block = basis[r : r + 16].astype(F32)
-                for i in range(2):
-                    for c in range(cols // 128):
-                        wide[t] = block[i * 8 : i * 8 + 8, c * 128 : c * 128 + 128]
-                        t += 1
-        for eig in (a_eig, m_eig):
-            for c in range(cols // 128):
-                wide[t] = jnp.broadcast_to(eig[:, c * 128 : c * 128 + 128], (8, 128))
-                t += 1
-
-    @pl.when(step > 0)
-    def _():
-        acc[:CA] += part_a
-        acc[CA:] += part_m
-
-    @pl.when(step == pl.num_programs(0) - 1)
-    def _():
-        cts = acc.shape[1] // 128
-        for p in range(ROWS // R):
-            g = acc[p * R : (p + 1) * R] * scale
-            g = lax.dot_general(q[p], g, (((0,), (0,)), ((), ())), precision=HI, preferred_element_type=F32)
+def grad_kernel(scale, *refs):
+    sources, (send, keep, wide), landed = refs[:9], refs[9:12], refs[12:21]
+    halves, arrived = refs[21:]
+    loads = [pltpu.make_async_copy(s, d, arrived.at[i]) for i, (s, d) in enumerate(zip(sources, landed))]
+    for load in loads:
+        load.start()
+    a_b, m_b, a_eig, m_eig, q, a_h, a_in, m_h, m_in = landed
+    feats, cols = a_b.shape
+    t = 0
+    for i, basis in enumerate((a_b, m_b)):
+        loads[i].wait()
+        for r in range(0, feats, 16):
+            block = basis[r : r + 16].astype(F32)
+            for k in range(2):
+                for c in range(cols // 128):
+                    wide[t] = block[k * 8 : k * 8 + 8, c * 128 : c * 128 + 128]
+                    t += 1
+    for i, eig in enumerate((a_eig, m_eig)):
+        loads[2 + i].wait()
+        for c in range(cols // 128):
+            wide[t] = jnp.broadcast_to(eig[:, c * 128 : c * 128 + 128], (8, 128))
+            t += 1
+    loads[4].wait()
+
+    def share(part, first, rows, base):
+        for p in range(2 * rows // R):
+            g = part[p * R : (p + 1) * R] * scale
+            g = lax.dot_general(
+                q[first + p], g, (((0,), (0,)), ((), ())), precision=HI, preferred_element_type=F32
+            )
             for i in range(R // 8):
-                row = p * R + i * 8
-                if row < CA:
-                    half, local = divmod(row, HALF_A)
-                else:
-                    half, local = divmod(row - CA, HALF_M)
-                    local += HALF_A
-                for c in range(cts):
-                    halves[half, local // 8 * cts + c] = g[i * 8 : i * 8 + 8, c * 128 : c * 128 + 128]
-        core = lax.axis_index("dp") % 2
-        send[...] = halves[1 - core]
-        keep[...] = halves[core]
+                half, local = divmod(p * R + i * 8, rows)
+                for c in range(feats // 128):
+                    at = (base + local) // 8 * (feats // 128) + c
+                    halves[half, at] = g[i * 8 : i * 8 + 8, c * 128 : c * 128 + 128]
+
+    loads[5].wait()
+    loads[6].wait()
+    part = lax.dot_general(a_h[...], a_in[...], (((1,), (0,)), ((), ())), preferred_element_type=F32)
+    share(part, 0, HALF_A, 0)
+    loads[7].wait()
+    loads[8].wait()
+    part = lax.dot_general(m_h[...], m_in[...], (((0,), (0,)), ((), ())), preferred_element_type=F32)
+    share(part, CA // R, HALF_M, HALF_A)
+    core = lax.axis_index("dp") % 2
+    send[...] = halves[1 - core]
+    keep[...] = halves[core]
 
 
 def core_add_kernel(keep, both, out):
@@ -210,11 +211,12 @@
         out[k, per] = quad
 
 
-def final_kernel(both, q, attn, mlp):
+def final_kernel(both, q, attn, mlp, result, stored):
     per = both.shape[2] - 1
     fts = attn.shape[1] // 128
     quad = jnp.sum(both[0, 0, per] + both[1, 0, per], keepdims=True)
     clip = jnp.minimum(1.0, jnp.sqrt(kl_limit / quad))
+    stores = []
     for p in range(ROWS // R):
         rows = []
         for i in range(R // 8):
@@ -228,10 +230,12 @@
             rows.append(jnp.concatenate([both[half, t // per, t % per] for t in ts], axis=1))
         b = jnp.concatenate(rows)
         b = clip * lax.dot_general(q[p], b, (((1,), (0,)), ((), ())), precision=HI, preferred_element_type=F32)
-        if p * R < CA:
-            attn[p * R : (p + 1) * R] = b
-        else:
-            mlp[p * R - CA : (p + 1) * R - CA] = b
+        result[p] = b
+        target = attn.at[p * R : (p + 1) * R] if p * R < CA else mlp.at[p * R - CA : (p + 1) * R - CA]
+        stores.append(pltpu.make_async_copy(result.at[p], target, stored.at[p]))
+        stores[-1].start()
+    for store in stores:
+        store.wait()
 
 
 def body(
@@ -251,44 +255,28 @@
     scale = 1.0 / (tokens * lax.axis_size("dp"))
     half_tiles = HALF // 8 * feats // 128
     y_tiles = HALF // 32 * 2 * cols // 128
-    chunk = tokens // TOK_STEPS
-
-    def whole(*dims):
-        return pl.BlockSpec(dims, lambda i: (0,) * len(dims))
-
     basis_tiles = 2 * (feats + 8) // 8 * cols // 128
+    sources = (
+        attn_basis,
+        mlp_basis,
+        attn_eig.reshape(1, -1),
+        mlp_eig.reshape(1, -1),
+        rank_basis,
+        attn_hgrad.T,
+        attn_in,
+        mlp_hgrad,
+        mlp_in,
+    )
     send, keep, wide = pl.pallas_call(
         functools.partial(grad_kernel, scale),
-        grid=(TOK_STEPS,),
-        in_specs=[
-            pl.BlockSpec((chunk, feats), lambda i: (i, 0)),
-            pl.BlockSpec((chunk, feats), lambda i: (i, 0)),
-            pl.BlockSpec((CA, chunk), lambda i: (0, i)),
-            pl.BlockSpec((chunk, CM), lambda i: (i, 0)),
-            whole(feats, cols),
-            whole(feats, cols),
-            whole(1, cols),
-            whole(1, cols),
-            whole(5, R, R),
-        ],
-        out_specs=[whole(half_tiles, 8, 128), whole(half_tiles, 8, 128), whole(basis_tiles, 8, 128)],
+        in_specs=[HBM] * len(sources),
+        out_specs=[VMEM] * 3,
         out_shape=[shape(half_tiles, 8, 128), shape(half_tiles, 8, 128), shape(basis_tiles, 8, 128)],
-        scratch_shapes=[pltpu.VMEM((ROWS, feats), F32), pltpu.VMEM((2, half_tiles, 8, 128), F32)],
+        scratch_shapes=[pltpu.VMEM(s.shape, s.dtype) for s in sources]
+        + [pltpu.VMEM((2, half_tiles, 8, 128), F32), pltpu.SemaphoreType.DMA((len(sources),))],
         compiler_params=LIMIT,
         name="grad",
-    )(
-        *far(
-            attn_in,
-            mlp_in,
-            attn_hgrad.T,
-            mlp_hgrad,
-            attn_basis,
-            mlp_basis,
-            attn_eig.reshape(1, -1),
-            mlp_eig.reshape(1, -1),
-            rank_basis,
-        )
-    )
+    )(*far(*sources))
     other = lax.ppermute(wide, "dp", [(i, i ^ 1) for i in range(lax.axis_size("dp"))])
     both = lax.all_gather(send, "dp", axis_index_groups=CORE_PAIRS)
     part = pl.pallas_call(
@@ -299,8 +287,8 @@
         compiler_params=LIMIT,
         name="core_add",
     )(*near(keep, both))
-    shard, other = lax.optimization_barrier((exchange(part.reshape(16, -1, 8, 128), "dp", CHIPS), other))
-    shard = jnp.sum(shard, axis=0)
+    part, other = lax.optimization_barrier((part, other))
+    shard = jnp.sum(exchange(part.reshape(16, -1, 8, 128), "dp", CHIPS), axis=0)
     pre = exchange(copies(shard, 16), "dp", CHIPS).reshape(-1, 8, 128)
 
     block, basis = pl.pallas_call(
@@ -351,9 +339,11 @@
         pl.pallas_call(
             final_kernel,
             in_specs=[VMEM] * 2,
-            out_specs=[VMEM] * 2,
+            out_specs=[HBM] * 2,
+            scratch_shapes=[pltpu.VMEM((ROWS // R, R, feats), F32), pltpu.SemaphoreType.DMA((ROWS // R,))],
+            compiler_params=LIMIT,
             out_shape=[jax.ShapeDtypeStruct((CA, feats), F32), jax.ShapeDtypeStruct((CM, feats), F32)],
-            compiler_params=LIMIT, name="final",
+            name="final",
         )(*near(both, rank_basis))
     )
 

time: 127 us -> 128 us (level)
  waiting for transfers between devices: 15.2 us -> 5.76 us
  blocking collectives: 82 us -> 91.1 us
  starting transfers between devices: 21.6 us -> 24.5 us
    all_to_all x5 -> x6, blocking collectives: 59.8 us -> 74.8 us  [exchange(): return lax.all_to_all(x, axis, 0, 0, axis_index_groups=groups, tiled=True)]
    all_to_all x1 -> x0, waiting for transfers between devices: 7.1 us -> none  [exchange(): return lax.all_to_all(x, axis, 0, 0, axis_index_groups=groups, tiled=True)]
    ppermute x1, starting transfers between devices: 2.28 us -> 8.75 us  [body(): lax.ppermute(wide, 'dp', [(i, i ^ 1) for i in range(lax.axis_size('dp'))])]
    all_gather x1, blocking collectives: 8.74 us -> 2.76 us  [body(): both = lax.all_gather(send, 'dp', axis_index_groups=CORE_PAIRS)]
    all_to_all x1 -> x0, starting transfers between devices: 3.54 us -> none  [exchange(): return lax.all_to_all(x, axis, 0, 0, axis_index_groups=groups, tiled=True)]
    ppermute x1, waiting for transfers between devices: 2.29 us -> 0.01 us  [body(): lax.ppermute(wide, 'dp', [(i, i ^ 1) for i in range(lax.axis_size('dp'))])]
  transfers between devices with their start and end apart: 4 -> 3, of which waited for: 4 -> 2; matrix products, arithmetic and copies ran while one was open for 0% -> 0% of each run, Pallas kernels for 0% -> 0%
where the time goes in v6:
time: 128 us
  blocking collectives  91.1 us (71%)
  starting transfers between devices  24.5 us (19%)
  waiting for transfers between devices  5.76 us (4%)
  Pallas kernels  5.7 us (4%)
    all_to_all x6, blocking collectives, exchange(): return lax.all_to_all(x, axis, 0, 0, axis_index_groups=groups, tiled=True)  74.8 us
    all_gather x1, blocking collectives, body(): both = lax.all_gather(back, 'dp', axis_index_groups=CORE_PAIRS)  13.5 us
    ppermute x1, starting transfers between devices, body(): lax.ppermute(block, 'factor', Z_PAIRS)  8.81 us
    ppermute x1, starting transfers between devices, body(): lax.ppermute(wide, 'dp', [(i, i ^ 1) for i in range(lax.axis_size('dp'))])  8.75 us
    ppermute x1, starting transfers between devices, body(): across = lax.ppermute(block, 'factor', Z_CROSS)  6.98 us
    pallas_call x1, Pallas kernels, body(): pl.pallas_call(functools.partial(grad_kernel, scale), in_specs=[HBM] * le...  3.2 us
    ppermute x1, waiting for transfers between devices, body(): lax.ppermute(block, 'factor', Z_PAIRS)  3.14 us
    all_gather x1, blocking collectives, body(): both = lax.all_gather(send, 'dp', axis_index_groups=CORE_PAIRS)  2.76 us
  transfers between devices with their start and end apart: 3, of which 2 were waited for; matrix products, arithmetic and copies ran while one was open for 0% of the time, Pallas kernels for 0%

profile of v6, /device:TPU:1, one launch (start us, length us, event | category | flops | bytes accessed | tf_op | source)
XLA Modules:
  0.0 128.0 jit_solution(7938263373674960129)
XLA Ops:
  0.6 3.2 %grad.1 = (f32[80,8,128]{2,1,0:T(8,128)S(1)}, f32[80,8,128]{2,1,0:T(8,128)S(1)}, f32[260,8,128]{2,1,0:T(8,128)S(1)}) custom-call(bf16[512,256]{1,0:T(8,128)(2,1)} %refs_0_.1, bf16[512,256]{1,0:T(8,128)(2,1)} %refs_1_.1, f32[1,256]{1,0:T(1,128)} %bitcast.12, f32[1,256]{1,0:T(1,128)} %bitcast.13, f32[5,64,64]{2,1,0:T(8,128)} %q.1, bf16[192,1024]{1,0:T(8,128)(2,1)} %bitcast.11, ...), custom_call_target="tpu_custom_call" | custom-call | tf_op jit(solution)/shard_map/grad/pallas_call | solution.py:270
  3.8 8.7 %collective-permute-start = (f32[260,8,128]{2,1,0:T(8,128)S(1)}, f32[260,8,128]{2,1,0:T(8,128)S(1)}, u32[]{:S(2)}, u32[]{:S(2)}) collective-permute-start(f32[260,8,128]{2,1,0:T(8,128)S(1)} %get-tuple-element.11.own), channel_id=1, source_target_pairs={{0,16},{16,0},{32,48},{48,32},{64,80},{80,64},{96,112},{112,96},{1... | collective-permute-start | bytes 3194888 | tf_op jit(solution)/shard_map/ppermute | solution.py:280
  12.6 2.8 %all-gather = f32[160,8,128]{2,1,0:T(8,128)S(1)} all-gather(f32[80,8,128]{2,1,0:T(8,128)S(1)} %get-tuple-element.10), channel_id=2, replica_groups={{0,16},{32,48},{64,80},{96,112},{128,144},{160,176},{192,208},{224,240}..., dimensions={0}, use_global_device_ids=true | all-gather | bytes 983040 | tf_op jit(solution)/shard_map/all_gather | solution.py:281
  15.4 0.0 collective-permute-done.other
  15.4 14.0 %all_to_all.30 = f32[16,5,8,128]{3,2,1,0:T(8,128)S(1)} all-to-all(f32[16,5,8,128]{3,2,1,0:T(8,128)S(1)} %bitcast.9), channel_id=1, replica_groups={{0,32,64,96,128,160,192,224,256,288,320,352,384,416,448,480},{16,48,80,..., dimensions={0} | all-to-all | bytes 655360 | tf_op jit(solution)/shard_map/all_to_all | solution.py:29
  29.4 15.0 %all_to_all.31 = f32[16,5,8,128]{3,2,1,0:T(8,128)S(1)} all-to-all(f32[16,5,8,128]{3,2,1,0:T(8,128)S(1)} %broadcast_in_dim.4), channel_id=1, replica_groups={{0,32,64,96,128,160,192,224,256,288,320,352,384,416,448,480},{16,48,80,..., dimensions={0} | all-to-all | bytes 655360 | tf_op jit(solution)/shard_map/all_to_all | solution.py:29
  44.4 0.5 rotate.1
  44.9 0.0 copy-start.1
  44.9 9.9 %all_to_all.32.got = f32[4,20,8,128]{3,2,1,0:T(8,128)S(1)} all-to-all(f32[4,20,8,128]{3,2,1,0:T(8,128)S(1)} %get-tuple-element.14), channel_id=1, replica_groups={{0,4,8,12},{1,5,9,13},{2,6,10,14},{3,7,11,15},{16,20,24,28},{17,21,25,2..., dimensions={0} | all-to-all | bytes 655360 | tf_op jit(solution)/shard_map/all_to_all | solution.py:29
  54.8 8.8 %collective-permute-start.1 = (f32[20,8,128]{2,1,0:T(8,128)S(1)}, f32[20,8,128]{2,1,0:T(8,128)S(1)}, u32[]{:S(2)}, u32[]{:S(2)}) collective-permute-start(f32[20,8,128]{2,1,0:T(8,128)S(1)} %y_sum.1.one), channel_id=1, source_target_pairs={{0,1},{1,0},{2,3},{3,2},{4,5},{5,4},{6,7},{7,6},{8,9},{9,8},{10,11... | collective-permute-start | bytes 245768 | tf_op jit(solution)/shard_map/ppermute | solution.py:317
  63.6 3.1 %collective-permute-done.1.two = f32[20,8,128]{2,1,0:T(8,128)S(1)} collective-permute-done((f32[20,8,128]{2,1,0:T(8,128)S(1)}, f32[20,8,128]{2,1,0:T(8,128)S(1)}, u32[]{:S(2)}, u32[]{:S(2)}) %collective-permute-start.1) | collective-permute-done | bytes 81952 | tf_op jit(solution)/shard_map/ppermute | solution.py:317
  66.8 7.0 %collective-permute-start.2 = (f32[20,8,128]{2,1,0:T(8,128)S(1)}, f32[20,8,128]{2,1,0:T(8,128)S(1)}, u32[]{:S(2)}, u32[]{:S(2)}) collective-permute-start(f32[20,8,128]{2,1,0:T(8,128)S(1)} %z_add.1.one), channel_id=1, source_target_pairs={{0,3},{1,2},{2,1},{3,0},{4,7},{5,6},{6,5},{7,4},{8,11},{9,10},{10,... | collective-permute-start | bytes 245768 | tf_op jit(solution)/shard_map/ppermute | solution.py:318
  73.7 2.6 %collective-permute-done.2.two = f32[20,8,128]{2,1,0:T(8,128)S(1)} collective-permute-done((f32[20,8,128]{2,1,0:T(8,128)S(1)}, f32[20,8,128]{2,1,0:T(8,128)S(1)}, u32[]{:S(2)}, u32[]{:S(2)}) %collective-permute-start.2) | collective-permute-done | bytes 81952 | tf_op jit(solution)/shard_map/ppermute | solution.py:318
  76.4 0.0 copy-done.1
  76.4 0.1 scale.1
  76.5 10.6 %all_to_all.33.got = f32[4,21,8,128]{3,2,1,0:T(8,128)S(1)} all-to-all(f32[4,21,8,128]{3,2,1,0:T(8,128)S(1)} %scale.1), channel_id=1, replica_groups={{0,4,8,12},{1,5,9,13},{2,6,10,14},{3,7,11,15},{16,20,24,28},{17,21,25,2..., dimensions={0} | all-to-all | bytes 688128 | tf_op jit(solution)/shard_map/all_to_all | solution.py:29
  87.1 0.5 back.1
  87.6 12.8 %all_to_all.34 = f32[16,6,8,128]{3,2,1,0:T(8,128)S(1)} all-to-all(f32[16,6,8,128]{3,2,1,0:T(8,128)S(1)} %back.1), channel_id=1, replica_groups={{0,32,64,96,128,160,192,224,256,288,320,352,384,416,448,480},{16,48,80,..., dimensions={0} | all-to-all | bytes 786432 | tf_op jit(solution)/shard_map/all_to_all | solution.py:29
  100.4 0.0 copy-start
  100.4 12.6 %all_to_all.35 = f32[16,6,8,128]{3,2,1,0:T(8,128)S(1)} all-to-all(f32[16,6,8,128]{3,2,1,0:T(8,128)S(1)} %broadcast_in_dim.5), channel_id=1, replica_groups={{0,32,64,96,128,160,192,224,256,288,320,352,384,416,448,480},{16,48,80,..., dimensions={0} | all-to-all | bytes 786432 | tf_op jit(solution)/shard_map/all_to_all | solution.py:29
  113.1 13.5 %all-gather.1 = f32[32,6,8,128]{3,2,1,0:T(8,128)S(1)} all-gather(f32[16,6,8,128]{3,2,1,0:T(8,128)S(1)} %all_to_all.35), channel_id=3, replica_groups={{0,16},{32,48},{64,80},{96,112},{128,144},{160,176},{192,208},{224,240}..., dimensions={0}, use_global_device_ids=true | all-gather | bytes 1179648 | tf_op jit(solution)/shard_map/all_gather | solution.py:337
  126.6 0.0 copy-done
  126.6 1.4 %final.1 = (f32[192,512]{1,0:T(8,128)}, f32[128,512]{1,0:T(8,128)}) custom-call(f32[2,16,6,8,128]{4,3,2,1,0:T(8,128)S(1)} %bitcast.7, f32[5,64,64]{2,1,0:T(8,128)S(1)} %copy-done), custom_call_target="tpu_custom_call" | custom-call | tf_op jit(solution)/shard_map/final/pallas_call | solution.py:339
  (7 shorter events, 0.2 us)
Async XLA Ops:
  3.8 11.6 %collective-permute-start = (f32[260,8,128]{2,1,0:T(8,128)S(1)}, f32[260,8,128]{2,1,0:T(8,128)S(1)}, u32[]{:S(2)}, u32[]{:S(2)}) collective-permute-start(f32[260,8,128]{2,1,0:T(8,128)S(1)} %get-tuple-element.11.own), channel_id=1, source_target_pairs={{0,16},{16,0},{32,48},{48,32},{64,80},{80,64},{96,112},{112,96},{1... | collective-permute-start | bytes 3194888 | tf_op jit(solution)/shard_map/ppermute | solution.py:280
  44.9 31.5 %copy-start.1 = (f32[5,64]{1,0:T(8,128)S(1)}, f32[5,64]{1,0:T(8,128)}, u32[]{:S(2)}) copy-start(f32[5,64]{1,0:T(8,128)} %eig.1) | copy-start | bytes 3844
  54.8 12.0 %collective-permute-start.1 = (f32[20,8,128]{2,1,0:T(8,128)S(1)}, f32[20,8,128]{2,1,0:T(8,128)S(1)}, u32[]{:S(2)}, u32[]{:S(2)}) collective-permute-start(f32[20,8,128]{2,1,0:T(8,128)S(1)} %y_sum.1.one), channel_id=1, source_target_pairs={{0,1},{1,0},{2,3},{3,2},{4,5},{5,4},{6,7},{7,6},{8,9},{9,8},{10,11... | collective-permute-start | bytes 245768 | tf_op jit(solution)/shard_map/ppermute | solution.py:317
  66.8 9.6 %collective-permute-start.2 = (f32[20,8,128]{2,1,0:T(8,128)S(1)}, f32[20,8,128]{2,1,0:T(8,128)S(1)}, u32[]{:S(2)}, u32[]{:S(2)}) collective-permute-start(f32[20,8,128]{2,1,0:T(8,128)S(1)} %z_add.1.one), channel_id=1, source_target_pairs={{0,3},{1,2},{2,1},{3,0},{4,7},{5,6},{6,5},{7,4},{8,11},{9,10},{10,... | collective-permute-start | bytes 245768 | tf_op jit(solution)/shard_map/ppermute | solution.py:318
  100.4 26.2 %copy-start = (f32[5,64,64]{2,1,0:T(8,128)S(1)}, f32[5,64,64]{2,1,0:T(8,128)}, u32[]{:S(2)}) copy-start(f32[5,64,64]{2,1,0:T(8,128)} %q.1) | copy-start | bytes 245764

commit v7 on v6

--- a/solution.py
+++ b/solution.py
@@ -7,10 +7,8 @@
 from jax.experimental.pallas import tpu as pltpu
 from jax.sharding import PartitionSpec as P
 
-
 damping = 0.001
 kl_limit = 8000.0
-HI = lax.Precision.HIGHEST
 F32, BF16 = jnp.float32, jnp.bfloat16
 
 CORE_PAIRS = [[x * 8 + z * 2 + c for c in range(2)] for x in range(4) for z in range(4)]
@@ -54,14 +52,22 @@
     a = x.astype(BF16)
     r = x - a.astype(F32)
     b = r.astype(BF16)
-    c = (r - b.astype(F32)).astype(BF16)
-    return jnp.concatenate([a, b, c], axis=0)
+    return a, b, (r - b.astype(F32)).astype(BF16)
 
 
 def exact_dot(x, basis, contract):
     n = x.shape[0]
-    out = lax.dot_general(pieces(x), basis, (((1,), (contract,)), ((), ())), preferred_element_type=F32)
+    stacked = jnp.concatenate(pieces(x), axis=0)
+    out = lax.dot_general(stacked, basis, (((1,), (contract,)), ((), ())), preferred_element_type=F32)
     return (out[2 * n :] + out[n : 2 * n]) + out[:n]
+
+
+def rank_dot(blocks, x):
+    qa, qb, qc = pieces(blocks)
+    a, b, c = pieces(x)
+    left = jnp.concatenate([qc, qa, qb, qb, qa, qa], axis=1)
+    right = jnp.concatenate([a, c, b, a, b, a], axis=0)
+    return lax.dot_general(left, right, (((1,), (0,)), ((), ())), preferred_element_type=F32)
 
 
 def grad_kernel(scale, *refs):
@@ -90,10 +96,7 @@
 
     def share(part, first, rows, base):
         for p in range(2 * rows // R):
-            g = part[p * R : (p + 1) * R] * scale
-            g = lax.dot_general(
-                q[first + p], g, (((0,), (0,)), ((), ())), precision=HI, preferred_element_type=F32
-            )
+            g = rank_dot(q[first + p].T, part[p * R : (p + 1) * R] * scale)
             for i in range(R // 8):
                 half, local = divmod(p * R + i * 8, rows)
                 for c in range(feats // 128):
@@ -229,7 +232,7 @@
             ts = [local // 8 * fts + c for c in range(fts)]
             rows.append(jnp.concatenate([both[half, t // per, t % per] for t in ts], axis=1))
         b = jnp.concatenate(rows)
-        b = clip * lax.dot_general(q[p], b, (((1,), (0,)), ((), ())), precision=HI, preferred_element_type=F32)
+        b = clip * rank_dot(q[p], b)
         result[p] = b
         target = attn.at[p * R : (p + 1) * R] if p * R < CA else mlp.at[p * R - CA : (p + 1) * R - CA]
         stores.append(pltpu.make_async_copy(result.at[p], target, stored.at[p]))
@@ -287,8 +290,8 @@
         compiler_params=LIMIT,
         name="core_add",
     )(*near(keep, both))
-    part, other = lax.optimization_barrier((part, other))
-    shard = jnp.sum(exchange(part.reshape(16, -1, 8, 128), "dp", CHIPS), axis=0)
+    shard, other = lax.optimization_barrier((exchange(part.reshape(16, -1, 8, 128), "dp", CHIPS), other))
+    shard = jnp.sum(shard, axis=0)
     pre = exchange(copies(shard, 16), "dp", CHIPS).reshape(-1, 8, 128)
 
     block, basis = pl.pallas_call(
@@ -363,5 +366,4 @@
     )
     out_specs = (P(None, "factor"), P(None, "factor"))
 
-
     return jax.shard_map(body, mesh=mesh, in_specs=in_specs, out_specs=out_specs, check_vma=False)

time: 128 us -> 126 us (0.984)
  waiting for transfers between devices: 5.76 us -> 15.2 us
  blocking collectives: 91.1 us -> 82.1 us
  starting transfers between devices: 24.5 us -> 21.6 us
    all_to_all x6 -> x5, blocking collectives: 74.8 us -> 59.8 us  [exchange(): return lax.all_to_all(x, axis, 0, 0, axis_index_groups=groups, tiled=True)]
    all_to_all x0 -> x1, waiting for transfers between devices: none -> 7.1 us  [exchange(): return lax.all_to_all(x, axis, 0, 0, axis_index_groups=groups, tiled=True)]
    ppermute x1, starting transfers between devices: 8.75 us -> 2.28 us  [body(): lax.ppermute(wide, 'dp', [(i, i ^ 1) for i in range(lax.axis_size('dp'))])]
    all_gather x1, blocking collectives: 2.76 us -> 8.74 us  [body(): both = lax.all_gather(send, 'dp', axis_index_groups=CORE_PAIRS)]
    all_to_all x0 -> x1, starting transfers between devices: none -> 3.54 us  [exchange(): return lax.all_to_all(x, axis, 0, 0, axis_index_groups=groups, tiled=True)]
    ppermute x1, waiting for transfers between devices: 0.01 us -> 2.29 us  [body(): lax.ppermute(wide, 'dp', [(i, i ^ 1) for i in range(lax.axis_size('dp'))])]
  transfers between devices with their start and end apart: 3 -> 4, of which waited for: 2 -> 4; matrix products, arithmetic and copies ran while one was open for 0% -> 0% of each run, Pallas kernels for 0% -> 0%
where the time goes in v7:
time: 126 us
  blocking collectives  82.1 us (65%)
  starting transfers between devices  21.6 us (17%)
  waiting for transfers between devices  15.2 us (12%)
  Pallas kernels  6.05 us (5%)
    all_to_all x5, blocking collectives, exchange(): return lax.all_to_all(x, axis, 0, 0, axis_index_groups=groups, tiled=True)  59.8 us
    all_gather x1, blocking collectives, body(): both = lax.all_gather(back, 'dp', axis_index_groups=CORE_PAIRS)  13.5 us
    ppermute x1, starting transfers between devices, body(): lax.ppermute(block, 'factor', Z_PAIRS)  8.81 us
    all_gather x1, blocking collectives, body(): both = lax.all_gather(send, 'dp', axis_index_groups=CORE_PAIRS)  8.74 us
    all_to_all x1, waiting for transfers between devices, exchange(): return lax.all_to_all(x, axis, 0, 0, axis_index_groups=groups, tiled=True)  7.1 us
    ppermute x1, starting transfers between devices, body(): across = lax.ppermute(block, 'factor', Z_CROSS)  6.99 us
    all_to_all x1, starting transfers between devices, exchange(): return lax.all_to_all(x, axis, 0, 0, axis_index_groups=groups, tiled=True)  3.54 us
    ppermute x1, waiting for transfers between devices, body(): lax.ppermute(block, 'factor', Z_PAIRS)  3.14 us
  transfers between devices with their start and end apart: 4, of which 4 were waited for; matrix products, arithmetic and copies ran while one was open for 0% of the time, Pallas kernels for 0%

profile of v7, /device:TPU:1, one launch (start us, length us, event | category | flops | bytes accessed | tf_op | source)
XLA Modules:
  0.0 125.7 jit_solution(1400626282767238533)
XLA Ops:
  0.6 3.0 %grad.1 = (f32[80,8,128]{2,1,0:T(8,128)S(1)}, f32[80,8,128]{2,1,0:T(8,128)S(1)}, f32[260,8,128]{2,1,0:T(8,128)S(1)}) custom-call(bf16[512,256]{1,0:T(8,128)(2,1)} %refs_0_.1, bf16[512,256]{1,0:T(8,128)(2,1)} %refs_1_.1, f32[1,256]{1,0:T(1,128)} %bitcast.11, f32[1,256]{1,0:T(1,128)} %bitcast.12, f32[5,64,64]{2,1,0:T(8,128)} %q.1, bf16[192,1024]{1,0:T(8,128)(2,1)} %bitcast.10, ...), custom_call_target="tpu_custom_call" | custom-call | tf_op jit(solution)/shard_map/grad/pallas_call | solution.py:273
  3.6 8.7 %all-gather = f32[160,8,128]{2,1,0:T(8,128)S(1)} all-gather(f32[80,8,128]{2,1,0:T(8,128)S(1)} %get-tuple-element.10), channel_id=2, replica_groups={{0,16},{32,48},{64,80},{96,112},{128,144},{160,176},{192,208},{224,240}..., dimensions={0}, use_global_device_ids=true | all-gather | bytes 983040 | tf_op jit(solution)/shard_map/all_gather | solution.py:284
  12.4 0.8 core_add.1
  13.1 3.5 %all-to-all-start = ((f32[16,5,8,128]{3,2,1,0:T(8,128)}), f32[16,5,8,128]{3,2,1,0:T(8,128)S(1)}, u32[]{:S(2)}, u32[]{:S(2)}) async-start(f32[16,5,8,128]{3,2,1,0:T(8,128)} %bitcast.4), calls=%async_computation | async-start | bytes 655360 | tf_op jit(solution)/shard_map/all_to_all | solution.py:27
  16.7 2.3 %collective-permute-start = (f32[260,8,128]{2,1,0:T(8,128)S(1)}, f32[260,8,128]{2,1,0:T(8,128)S(1)}, u32[]{:S(2)}, u32[]{:S(2)}) collective-permute-start(f32[260,8,128]{2,1,0:T(8,128)S(1)} %get-tuple-element.11.own), channel_id=1, source_target_pairs={{0,16},{16,0},{32,48},{48,32},{64,80},{80,64},{96,112},{112,96},{1... | collective-permute-start | bytes 3194888 | tf_op jit(solution)/shard_map/ppermute | solution.py:283
  19.0 2.3 %collective-permute-done.other = f32[260,8,128]{2,1,0:T(8,128)S(1)} collective-permute-done((f32[260,8,128]{2,1,0:T(8,128)S(1)}, f32[260,8,128]{2,1,0:T(8,128)S(1)}, u32[]{:S(2)}, u32[]{:S(2)}) %collective-permute-start) | collective-permute-done | bytes 1064992 | tf_op jit(solution)/shard_map/ppermute | solution.py:283
  21.3 7.1 %all-to-all-done = f32[16,5,8,128]{3,2,1,0:T(8,128)S(1)} async-done(((f32[16,5,8,128]{3,2,1,0:T(8,128)}), f32[16,5,8,128]{3,2,1,0:T(8,128)S(1)}, u32[]{:S(2)}, u32[]{:S(2)}) %all-to-all-start) | async-done | bytes 327712 | tf_op jit(solution)/shard_map/all_to_all | solution.py:27
  28.4 14.9 %all_to_all.30 = f32[16,5,8,128]{3,2,1,0:T(8,128)S(1)} all-to-all(f32[16,5,8,128]{3,2,1,0:T(8,128)S(1)} %broadcast_in_dim.4), channel_id=1, replica_groups={{0,32,64,96,128,160,192,224,256,288,320,352,384,416,448,480},{16,48,80,..., dimensions={0} | all-to-all | bytes 655360 | tf_op jit(solution)/shard_map/all_to_all | solution.py:27
  43.3 0.5 rotate.1
  43.8 0.0 copy-start.1
  43.8 8.9 %all_to_all.31.got = f32[4,20,8,128]{3,2,1,0:T(8,128)S(1)} all-to-all(f32[4,20,8,128]{3,2,1,0:T(8,128)S(1)} %get-tuple-element.14), channel_id=1, replica_groups={{0,4,8,12},{1,5,9,13},{2,6,10,14},{3,7,11,15},{16,20,24,28},{17,21,25,2..., dimensions={0} | all-to-all | bytes 655360 | tf_op jit(solution)/shard_map/all_to_all | solution.py:27
  52.7 8.8 %collective-permute-start.1 = (f32[20,8,128]{2,1,0:T(8,128)S(1)}, f32[20,8,128]{2,1,0:T(8,128)S(1)}, u32[]{:S(2)}, u32[]{:S(2)}) collective-permute-start(f32[20,8,128]{2,1,0:T(8,128)S(1)} %y_sum.1.one), channel_id=1, source_target_pairs={{0,1},{1,0},{2,3},{3,2},{4,5},{5,4},{6,7},{7,6},{8,9},{9,8},{10,11... | collective-permute-start | bytes 245768 | tf_op jit(solution)/shard_map/ppermute | solution.py:320
  61.5 3.1 %collective-permute-done.1.two = f32[20,8,128]{2,1,0:T(8,128)S(1)} collective-permute-done((f32[20,8,128]{2,1,0:T(8,128)S(1)}, f32[20,8,128]{2,1,0:T(8,128)S(1)}, u32[]{:S(2)}, u32[]{:S(2)}) %collective-permute-start.1) | collective-permute-done | bytes 81952 | tf_op jit(solution)/shard_map/ppermute | solution.py:320
  64.7 7.0 %collective-permute-start.2 = (f32[20,8,128]{2,1,0:T(8,128)S(1)}, f32[20,8,128]{2,1,0:T(8,128)S(1)}, u32[]{:S(2)}, u32[]{:S(2)}) collective-permute-start(f32[20,8,128]{2,1,0:T(8,128)S(1)} %z_add.1.one), channel_id=1, source_target_pairs={{0,3},{1,2},{2,1},{3,0},{4,7},{5,6},{6,5},{7,4},{8,11},{9,10},{10,... | collective-permute-start | bytes 245768 | tf_op jit(solution)/shard_map/ppermute | solution.py:321
  71.7 2.6 %collective-permute-done.2.two = f32[20,8,128]{2,1,0:T(8,128)S(1)} collective-permute-done((f32[20,8,128]{2,1,0:T(8,128)S(1)}, f32[20,8,128]{2,1,0:T(8,128)S(1)}, u32[]{:S(2)}, u32[]{:S(2)}) %collective-permute-start.2) | collective-permute-done | bytes 81952 | tf_op jit(solution)/shard_map/ppermute | solution.py:321
  74.3 0.0 copy-done.1
  74.3 0.1 scale.1
  74.4 10.6 %all_to_all.32.got = f32[4,21,8,128]{3,2,1,0:T(8,128)S(1)} all-to-all(f32[4,21,8,128]{3,2,1,0:T(8,128)S(1)} %scale.1), channel_id=1, replica_groups={{0,4,8,12},{1,5,9,13},{2,6,10,14},{3,7,11,15},{16,20,24,28},{17,21,25,2..., dimensions={0} | all-to-all | bytes 688128 | tf_op jit(solution)/shard_map/all_to_all | solution.py:27
  85.0 0.5 back.1
  85.5 12.8 %all_to_all.33 = f32[16,6,8,128]{3,2,1,0:T(8,128)S(1)} all-to-all(f32[16,6,8,128]{3,2,1,0:T(8,128)S(1)} %back.1), channel_id=1, replica_groups={{0,32,64,96,128,160,192,224,256,288,320,352,384,416,448,480},{16,48,80,..., dimensions={0} | all-to-all | bytes 786432 | tf_op jit(solution)/shard_map/all_to_all | solution.py:27
  98.4 0.0 copy-start
  98.4 12.6 %all_to_all.34 = f32[16,6,8,128]{3,2,1,0:T(8,128)S(1)} all-to-all(f32[16,6,8,128]{3,2,1,0:T(8,128)S(1)} %broadcast_in_dim.5), channel_id=1, replica_groups={{0,32,64,96,128,160,192,224,256,288,320,352,384,416,448,480},{16,48,80,..., dimensions={0} | all-to-all | bytes 786432 | tf_op jit(solution)/shard_map/all_to_all | solution.py:27
  111.0 13.5 %all-gather.1 = f32[32,6,8,128]{3,2,1,0:T(8,128)S(1)} all-gather(f32[16,6,8,128]{3,2,1,0:T(8,128)S(1)} %all_to_all.34), channel_id=3, replica_groups={{0,16},{32,48},{64,80},{96,112},{128,144},{160,176},{192,208},{224,240}..., dimensions={0}, use_global_device_ids=true | all-gather | bytes 1179648 | tf_op jit(solution)/shard_map/all_gather | solution.py:340
  124.5 1.2 final.1
  (7 shorter events, 0.1 us)
Async XLA Ops:
  13.1 15.2 %all-to-all-start = ((f32[16,5,8,128]{3,2,1,0:T(8,128)}), f32[16,5,8,128]{3,2,1,0:T(8,128)S(1)}, u32[]{:S(2)}, u32[]{:S(2)}) async-start(f32[16,5,8,128]{3,2,1,0:T(8,128)} %bitcast.4), calls=%async_computation | async-start | bytes 655360 | tf_op jit(solution)/shard_map/all_to_all | solution.py:27
  16.7 4.6 %collective-permute-start = (f32[260,8,128]{2,1,0:T(8,128)S(1)}, f32[260,8,128]{2,1,0:T(8,128)S(1)}, u32[]{:S(2)}, u32[]{:S(2)}) collective-permute-start(f32[260,8,128]{2,1,0:T(8,128)S(1)} %get-tuple-element.11.own), channel_id=1, source_target_pairs={{0,16},{16,0},{32,48},{48,32},{64,80},{80,64},{96,112},{112,96},{1... | collective-permute-start | bytes 3194888 | tf_op jit(solution)/shard_map/ppermute | solution.py:283
  43.8 30.5 %copy-start.1 = (f32[5,64]{1,0:T(8,128)S(1)}, f32[5,64]{1,0:T(8,128)}, u32[]{:S(2)}) copy-start(f32[5,64]{1,0:T(8,128)} %eig.1) | copy-start | bytes 3844
  52.7 12.0 %collective-permute-start.1 = (f32[20,8,128]{2,1,0:T(8,128)S(1)}, f32[20,8,128]{2,1,0:T(8,128)S(1)}, u32[]{:S(2)}, u32[]{:S(2)}) collective-permute-start(f32[20,8,128]{2,1,0:T(8,128)S(1)} %y_sum.1.one), channel_id=1, source_target_pairs={{0,1},{1,0},{2,3},{3,2},{4,5},{5,4},{6,7},{7,6},{8,9},{9,8},{10,11... | collective-permute-start | bytes 245768 | tf_op jit(solution)/shard_map/ppermute | solution.py:320
  64.7 9.6 %collective-permute-start.2 = (f32[20,8,128]{2,1,0:T(8,128)S(1)}, f32[20,8,128]{2,1,0:T(8,128)S(1)}, u32[]{:S(2)}, u32[]{:S(2)}) collective-permute-start(f32[20,8,128]{2,1,0:T(8,128)S(1)} %z_add.1.one), channel_id=1, source_target_pairs={{0,3},{1,2},{2,1},{3,0},{4,7},{5,6},{6,5},{7,4},{8,11},{9,10},{10,... | collective-permute-start | bytes 245768 | tf_op jit(solution)/shard_map/ppermute | solution.py:321
  98.4 26.2 %copy-start = (f32[5,64,64]{2,1,0:T(8,128)S(1)}, f32[5,64,64]{2,1,0:T(8,128)}, u32[]{:S(2)}) copy-start(f32[5,64,64]{2,1,0:T(8,128)} %q.1) | copy-start | bytes 245764

commit v8 on v7

--- a/solution.py
+++ b/solution.py
@@ -70,29 +70,42 @@
     return lax.dot_general(left, right, (((1,), (0,)), ((), ())), preferred_element_type=F32)
 
 
-def grad_kernel(scale, *refs):
-    sources, (send, keep, wide), landed = refs[:9], refs[9:12], refs[12:21]
-    halves, arrived = refs[21:]
-    loads = [pltpu.make_async_copy(s, d, arrived.at[i]) for i, (s, d) in enumerate(zip(sources, landed))]
-    for load in loads:
-        load.start()
-    a_b, m_b, a_eig, m_eig, q, a_h, a_in, m_h, m_in = landed
+def widen_kernel(a_b, m_b, a_eig, m_eig, wide):
+    t = 0
     feats, cols = a_b.shape
-    t = 0
-    for i, basis in enumerate((a_b, m_b)):
-        loads[i].wait()
+    for basis in (a_b, m_b):
         for r in range(0, feats, 16):
             block = basis[r : r + 16].astype(F32)
             for k in range(2):
                 for c in range(cols // 128):
                     wide[t] = block[k * 8 : k * 8 + 8, c * 128 : c * 128 + 128]
                     t += 1
-    for i, eig in enumerate((a_eig, m_eig)):
-        loads[2 + i].wait()
+    for eig in (a_eig, m_eig):
         for c in range(cols // 128):
             wide[t] = jnp.broadcast_to(eig[:, c * 128 : c * 128 + 128], (8, 128))
             t += 1
-    loads[4].wait()
+
+
+def join_kernel(own, other, basis):
+    rows, cols = basis.shape
+    cts = cols // 256
+    for side, source in enumerate((own, other)):
+        for r in range(0, rows, 16):
+            t = r // 8 * cts
+            for c in range(cts):
+                pair = jnp.concatenate([source[t + c], source[t + cts + c]])
+                basis[r : r + 16, (side * cts + c) * 128 : (side * cts + c + 1) * 128] = pair.astype(BF16)
+
+
+def grad_kernel(scale, *refs):
+    sources, (send, keep), landed = refs[:5], refs[5:7], refs[7:12]
+    halves, arrived = refs[12:]
+    loads = [pltpu.make_async_copy(s, d, arrived.at[i]) for i, (s, d) in enumerate(zip(sources, landed))]
+    for load in loads:
+        load.start()
+    q, a_h, a_in, m_h, m_in = landed
+    feats = a_in.shape[1]
+    loads[0].wait()
 
     def share(part, first, rows, base):
         for p in range(2 * rows // R):
@@ -103,12 +116,12 @@
                     at = (base + local) // 8 * (feats // 128) + c
                     halves[half, at] = g[i * 8 : i * 8 + 8, c * 128 : c * 128 + 128]
 
-    loads[5].wait()
-    loads[6].wait()
+    loads[1].wait()
+    loads[2].wait()
     part = lax.dot_general(a_h[...], a_in[...], (((1,), (0,)), ((), ())), preferred_element_type=F32)
     share(part, 0, HALF_A, 0)
-    loads[7].wait()
-    loads[8].wait()
+    loads[3].wait()
+    loads[4].wait()
     part = lax.dot_general(m_h[...], m_in[...], (((0,), (0,)), ((), ())), preferred_element_type=F32)
     share(part, CA // R, HALF_M, HALF_A)
     core = lax.axis_index("dp") % 2
@@ -139,18 +152,10 @@
     out[...] = one[...] + two[...]
 
 
-def rotate_kernel(pre, own, other, out, basis):
-    feats, cols = basis.shape[0] // 2, basis.shape[1] // 2
-    cts = cols // 128
-    for side, source in enumerate((own, other)):
-        for r in range(0, 2 * feats, 16):
-            t = r // 8 * cts
-            for c in range(cts):
-                pair = jnp.concatenate([source[t + c], source[t + cts + c]])
-                basis[r : r + 16, (side * cts + c) * 128 : (side * cts + c + 1) * 128] = pair.astype(BF16)
+def rotate_kernel(pre, basis, out):
+    feats, cts = basis.shape[0] // 2, basis.shape[1] // 128
     rot_a = exact_dot(rows_of(pre, HALF_A), basis[:feats], 0)
     rot_m = exact_dot(rows_of(pre, HALF_M, HALF_A // 8), basis[feats:], 0)
-    cts = 2 * cts
     for y in range(4):
         for rot, count, first, base in ((rot_a, Y_A // 8, y * Y_A, 0), (rot_m, Y_M // 8, y * Y_M, Y_A // 8)):
             for i in range(count):
@@ -259,28 +264,17 @@
     half_tiles = HALF // 8 * feats // 128
     y_tiles = HALF // 32 * 2 * cols // 128
     basis_tiles = 2 * (feats + 8) // 8 * cols // 128
-    sources = (
-        attn_basis,
-        mlp_basis,
-        attn_eig.reshape(1, -1),
-        mlp_eig.reshape(1, -1),
-        rank_basis,
-        attn_hgrad.T,
-        attn_in,
-        mlp_hgrad,
-        mlp_in,
-    )
-    send, keep, wide = pl.pallas_call(
+    sources = (rank_basis, attn_hgrad.T, attn_in, mlp_hgrad, mlp_in)
+    send, keep = pl.pallas_call(
         functools.partial(grad_kernel, scale),
         in_specs=[HBM] * len(sources),
-        out_specs=[VMEM] * 3,
-        out_shape=[shape(half_tiles, 8, 128), shape(half_tiles, 8, 128), shape(basis_tiles, 8, 128)],
+        out_specs=[VMEM] * 2,
+        out_shape=[shape(half_tiles, 8, 128)] * 2,
         scratch_shapes=[pltpu.VMEM(s.shape, s.dtype) for s in sources]
         + [pltpu.VMEM((2, half_tiles, 8, 128), F32), pltpu.SemaphoreType.DMA((len(sources),))],
         compiler_params=LIMIT,
         name="grad",
     )(*far(*sources))
-    other = lax.ppermute(wide, "dp", [(i, i ^ 1) for i in range(lax.axis_size("dp"))])
     both = lax.all_gather(send, "dp", axis_index_groups=CORE_PAIRS)
     part = pl.pallas_call(
         core_add_kernel,
@@ -290,18 +284,37 @@
         compiler_params=LIMIT,
         name="core_add",
     )(*near(keep, both))
-    shard, other = lax.optimization_barrier((exchange(part.reshape(16, -1, 8, 128), "dp", CHIPS), other))
+
+    part, attn_basis, mlp_basis = lax.optimization_barrier((part, attn_basis, mlp_basis))
+    wide = pl.pallas_call(
+        widen_kernel,
+        in_specs=[VMEM] * 4,
+        out_specs=VMEM,
+        out_shape=shape(basis_tiles, 8, 128),
+        compiler_params=LIMIT,
+        name="widen",
+    )(*near(attn_basis, mlp_basis, attn_eig.reshape(1, -1), mlp_eig.reshape(1, -1)))
+    other = lax.ppermute(wide, "dp", [(i, i ^ 1) for i in range(lax.axis_size("dp"))])
+    basis = pl.pallas_call(
+        join_kernel,
+        in_specs=[VMEM] * 2,
+        out_specs=VMEM,
+        out_shape=shape(2 * feats, 2 * cols, dtype=BF16),
+        compiler_params=LIMIT,
+        name="join",
+    )(*near(wide, other))
+    shard, basis = lax.optimization_barrier((exchange(part.reshape(16, -1, 8, 128), "dp", CHIPS), basis))
     shard = jnp.sum(shard, axis=0)
     pre = exchange(copies(shard, 16), "dp", CHIPS).reshape(-1, 8, 128)
 
-    block, basis = pl.pallas_call(
+    block = pl.pallas_call(
         rotate_kernel,
-        in_specs=[VMEM] * 3,
-        out_specs=[VMEM] * 2,
-        out_shape=[shape(4, y_tiles, 8, 128), shape(2 * feats, 2 * cols, dtype=BF16)],
+        in_specs=[VMEM] * 2,
+        out_specs=VMEM,
+        out_shape=shape(4, y_tiles, 8, 128),
         compiler_params=LIMIT,
         name="rotate",
-    )(*near(pre, wide, other))
+    )(*near(pre, basis))
     block = pl.pallas_call(
         sum_kernel,
         in_specs=[VMEM],

time: 126 us -> 126 us (level)
  no operation moved by 1% of the time
where the time goes in v8:
time: 126 us
  blocking collectives  82.3 us (65%)
  starting transfers between devices  21.6 us (17%)
  waiting for transfers between devices  14.6 us (12%)
  Pallas kernels  6.04 us (5%)
    all_to_all x5, blocking collectives, exchange(): return lax.all_to_all(x, axis, 0, 0, axis_index_groups=groups, tiled=True)  60 us
    all_gather x1, blocking collectives, body(): both = lax.all_gather(back, 'dp', axis_index_groups=CORE_PAIRS)  13.5 us
    ppermute x1, starting transfers between devices, body(): lax.ppermute(block, 'factor', Z_PAIRS)  8.82 us
    all_gather x1, blocking collectives, body(): both = lax.all_gather(send, 'dp', axis_index_groups=CORE_PAIRS)  8.74 us
    ppermute x1, starting transfers between devices, body(): across = lax.ppermute(block, 'factor', Z_CROSS)  7 us
    all_to_all x1, waiting for transfers between devices, exchange(): return lax.all_to_all(x, axis, 0, 0, axis_index_groups=groups, tiled=True)  6.61 us
    all_to_all x1, starting transfers between devices, exchange(): return lax.all_to_all(x, axis, 0, 0, axis_index_groups=groups, tiled=True)  3.54 us
    ppermute x1, waiting for transfers between devices, body(): lax.ppermute(block, 'factor', Z_PAIRS)  3.13 us
  transfers between devices with their start and end apart: 4, of which 4 were waited for; matrix products, arithmetic and copies ran while one was open for 0% of the time, Pallas kernels for 0%

profile of v8, /device:TPU:1, one launch (start us, length us, event | category | flops | bytes accessed | tf_op | source)
XLA Modules:
  0.0 125.5 jit_solution(13132116441220872279)
XLA Ops:
  0.6 2.8 %grad.1 = (f32[80,8,128]{2,1,0:T(8,128)S(1)}, f32[80,8,128]{2,1,0:T(8,128)S(1)}) custom-call(f32[5,64,64]{2,1,0:T(8,128)} %q.1, bf16[192,1024]{1,0:T(8,128)(2,1)} %bitcast.12, bf16[1024,512]{1,0:T(8,128)(2,1)} %refs_2_.1, bf16[1024,128]{1,0:T(8,128)(2,1)} %refs_3_.1, bf16[1024,512]{1,0:T(8,128)(2,1)} %refs_4_.1), custom_call_target="tpu_custom_call" | custom-call | tf_op jit(solution)/shard_map/grad/pallas_call | solution.py:268
  3.4 8.7 %all-gather = f32[160,8,128]{2,1,0:T(8,128)S(1)} all-gather(f32[80,8,128]{2,1,0:T(8,128)S(1)} %get-tuple-element.10), channel_id=2, replica_groups={{0,16},{32,48},{64,80},{96,112},{128,144},{160,176},{192,208},{224,240}..., dimensions={0}, use_global_device_ids=true | all-gather | bytes 983040 | tf_op jit(solution)/shard_map/all_gather | solution.py:278
  12.2 0.8 core_add.1
  13.0 3.5 %all-to-all-start = ((f32[16,5,8,128]{3,2,1,0:T(8,128)}), f32[16,5,8,128]{3,2,1,0:T(8,128)S(1)}, u32[]{:S(2)}, u32[]{:S(2)}) async-start(f32[16,5,8,128]{3,2,1,0:T(8,128)} %bitcast.2), calls=%async_computation | async-start | bytes 655360 | tf_op jit(solution)/shard_map/all_to_all | solution.py:27
  16.6 0.1 widen.1.own
  16.6 2.3 %collective-permute-start = (f32[260,8,128]{2,1,0:T(8,128)S(1)}, f32[260,8,128]{2,1,0:T(8,128)S(1)}, u32[]{:S(2)}, u32[]{:S(2)}) collective-permute-start(f32[260,8,128]{2,1,0:T(8,128)S(1)} %widen.1.own), channel_id=1, source_target_pairs={{0,16},{16,0},{32,48},{48,32},{64,80},{80,64},{96,112},{112,96},{1... | collective-permute-start | bytes 3194888 | tf_op jit(solution)/shard_map/ppermute | solution.py:297
  18.9 2.3 %collective-permute-done.other = f32[260,8,128]{2,1,0:T(8,128)S(1)} collective-permute-done((f32[260,8,128]{2,1,0:T(8,128)S(1)}, f32[260,8,128]{2,1,0:T(8,128)S(1)}, u32[]{:S(2)}, u32[]{:S(2)}) %collective-permute-start) | collective-permute-done | bytes 1064992 | tf_op jit(solution)/shard_map/ppermute | solution.py:297
  21.2 0.1 join.1.basis
  21.4 6.6 %all-to-all-done = f32[16,5,8,128]{3,2,1,0:T(8,128)S(1)} async-done(((f32[16,5,8,128]{3,2,1,0:T(8,128)}), f32[16,5,8,128]{3,2,1,0:T(8,128)S(1)}, u32[]{:S(2)}, u32[]{:S(2)}) %all-to-all-start) | async-done | bytes 327712 | tf_op jit(solution)/shard_map/all_to_all | solution.py:27
  28.0 15.1 %all_to_all.30 = f32[16,5,8,128]{3,2,1,0:T(8,128)S(1)} all-to-all(f32[16,5,8,128]{3,2,1,0:T(8,128)S(1)} %broadcast_in_dim.4), channel_id=1, replica_groups={{0,32,64,96,128,160,192,224,256,288,320,352,384,416,448,480},{16,48,80,..., dimensions={0} | all-to-all | bytes 655360 | tf_op jit(solution)/shard_map/all_to_all | solution.py:27
  43.1 0.4 rotate.1
  43.6 8.9 %all_to_all.31.got = f32[4,20,8,128]{3,2,1,0:T(8,128)S(1)} all-to-all(f32[4,20,8,128]{3,2,1,0:T(8,128)S(1)} %rotate.1), channel_id=1, replica_groups={{0,4,8,12},{1,5,9,13},{2,6,10,14},{3,7,11,15},{16,20,24,28},{17,21,25,2..., dimensions={0} | all-to-all | bytes 655360 | tf_op jit(solution)/shard_map/all_to_all | solution.py:27
  52.5 8.8 %collective-permute-start.1 = (f32[20,8,128]{2,1,0:T(8,128)S(1)}, f32[20,8,128]{2,1,0:T(8,128)S(1)}, u32[]{:S(2)}, u32[]{:S(2)}) collective-permute-start(f32[20,8,128]{2,1,0:T(8,128)S(1)} %y_sum.1.one), channel_id=1, source_target_pairs={{0,1},{1,0},{2,3},{3,2},{4,5},{5,4},{6,7},{7,6},{8,9},{9,8},{10,11... | collective-permute-start | bytes 245768 | tf_op jit(solution)/shard_map/ppermute | solution.py:333
  61.3 3.1 %collective-permute-done.1.two = f32[20,8,128]{2,1,0:T(8,128)S(1)} collective-permute-done((f32[20,8,128]{2,1,0:T(8,128)S(1)}, f32[20,8,128]{2,1,0:T(8,128)S(1)}, u32[]{:S(2)}, u32[]{:S(2)}) %collective-permute-start.1) | collective-permute-done | bytes 81952 | tf_op jit(solution)/shard_map/ppermute | solution.py:333
  64.5 7.0 %collective-permute-start.2 = (f32[20,8,128]{2,1,0:T(8,128)S(1)}, f32[20,8,128]{2,1,0:T(8,128)S(1)}, u32[]{:S(2)}, u32[]{:S(2)}) collective-permute-start(f32[20,8,128]{2,1,0:T(8,128)S(1)} %z_add.1.one), channel_id=1, source_target_pairs={{0,3},{1,2},{2,1},{3,0},{4,7},{5,6},{6,5},{7,4},{8,11},{9,10},{10,... | collective-permute-start | bytes 245768 | tf_op jit(solution)/shard_map/ppermute | solution.py:334
  71.5 2.6 %collective-permute-done.2.two = f32[20,8,128]{2,1,0:T(8,128)S(1)} collective-permute-done((f32[20,8,128]{2,1,0:T(8,128)S(1)}, f32[20,8,128]{2,1,0:T(8,128)S(1)}, u32[]{:S(2)}, u32[]{:S(2)}) %collective-permute-start.2) | collective-permute-done | bytes 81952 | tf_op jit(solution)/shard_map/ppermute | solution.py:334
  74.1 0.1 scale.1
  74.2 10.6 %all_to_all.32.got = f32[4,21,8,128]{3,2,1,0:T(8,128)S(1)} all-to-all(f32[4,21,8,128]{3,2,1,0:T(8,128)S(1)} %scale.1), channel_id=1, replica_groups={{0,4,8,12},{1,5,9,13},{2,6,10,14},{3,7,11,15},{16,20,24,28},{17,21,25,2..., dimensions={0} | all-to-all | bytes 688128 | tf_op jit(solution)/shard_map/all_to_all | solution.py:27
  84.8 0.5 back.1
  85.3 12.8 %all_to_all.33 = f32[16,6,8,128]{3,2,1,0:T(8,128)S(1)} all-to-all(f32[16,6,8,128]{3,2,1,0:T(8,128)S(1)} %back.1), channel_id=1, replica_groups={{0,32,64,96,128,160,192,224,256,288,320,352,384,416,448,480},{16,48,80,..., dimensions={0} | all-to-all | bytes 786432 | tf_op jit(solution)/shard_map/all_to_all | solution.py:27
  98.1 0.0 copy-start
  98.1 12.6 %all_to_all.34 = f32[16,6,8,128]{3,2,1,0:T(8,128)S(1)} all-to-all(f32[16,6,8,128]{3,2,1,0:T(8,128)S(1)} %broadcast_in_dim.5), channel_id=1, replica_groups={{0,32,64,96,128,160,192,224,256,288,320,352,384,416,448,480},{16,48,80,..., dimensions={0} | all-to-all | bytes 786432 | tf_op jit(solution)/shard_map/all_to_all | solution.py:27
  110.8 13.5 %all-gather.1 = f32[32,6,8,128]{3,2,1,0:T(8,128)S(1)} all-gather(f32[16,6,8,128]{3,2,1,0:T(8,128)S(1)} %all_to_all.34), channel_id=3, replica_groups={{0,16},{32,48},{64,80},{96,112},{128,144},{160,176},{192,208},{224,240}..., dimensions={0}, use_global_device_ids=true | all-gather | bytes 1179648 | tf_op jit(solution)/shard_map/all_gather | solution.py:353
  124.3 1.2 final.1
  (17 shorter events, 0.2 us)
Async XLA Ops:
  12.2 4.3 %copy-start.1 = (bf16[512,256]{1,0:T(8,128)(2,1)S(1)}, bf16[512,256]{1,0:T(8,128)(2,1)}, u32[]{:S(2)}) copy-start(bf16[512,256]{1,0:T(8,128)(2,1)} %a_b) | copy-start | bytes 786436
  12.2 4.3 %copy-start.2 = (bf16[512,256]{1,0:T(8,128)(2,1)S(1)}, bf16[512,256]{1,0:T(8,128)(2,1)}, u32[]{:S(2)}) copy-start(bf16[512,256]{1,0:T(8,128)(2,1)} %m_b) | copy-start | bytes 786436
  12.2 4.3 %copy-start.4 = (f32[256]{0:T(256)S(1)}, f32[256]{0:T(256)}, u32[]{:S(2)}) copy-start(f32[256]{0:T(256)} %param.16) | copy-start | bytes 3076
  12.2 4.4 %copy-start.5 = (f32[256]{0:T(256)S(1)}, f32[256]{0:T(256)}, u32[]{:S(2)}) copy-start(f32[256]{0:T(256)} %param.17) | copy-start | bytes 3076
  13.0 15.0 %all-to-all-start = ((f32[16,5,8,128]{3,2,1,0:T(8,128)}), f32[16,5,8,128]{3,2,1,0:T(8,128)S(1)}, u32[]{:S(2)}, u32[]{:S(2)}) async-start(f32[16,5,8,128]{3,2,1,0:T(8,128)} %bitcast.2), calls=%async_computation | async-start | bytes 655360 | tf_op jit(solution)/shard_map/all_to_all | solution.py:27
  16.6 4.6 %collective-permute-start = (f32[260,8,128]{2,1,0:T(8,128)S(1)}, f32[260,8,128]{2,1,0:T(8,128)S(1)}, u32[]{:S(2)}, u32[]{:S(2)}) collective-permute-start(f32[260,8,128]{2,1,0:T(8,128)S(1)} %widen.1.own), channel_id=1, source_target_pairs={{0,16},{16,0},{32,48},{48,32},{64,80},{80,64},{96,112},{112,96},{1... | collective-permute-start | bytes 3194888 | tf_op jit(solution)/shard_map/ppermute | solution.py:297
  43.6 30.5 %copy-start.3 = (f32[5,64]{1,0:T(8,128)S(1)}, f32[5,64]{1,0:T(8,128)}, u32[]{:S(2)}) copy-start(f32[5,64]{1,0:T(8,128)} %eig.1) | copy-start | bytes 3844
  52.5 12.0 %collective-permute-start.1 = (f32[20,8,128]{2,1,0:T(8,128)S(1)}, f32[20,8,128]{2,1,0:T(8,128)S(1)}, u32[]{:S(2)}, u32[]{:S(2)}) collective-permute-start(f32[20,8,128]{2,1,0:T(8,128)S(1)} %y_sum.1.one), channel_id=1, source_target_pairs={{0,1},{1,0},{2,3},{3,2},{4,5},{5,4},{6,7},{7,6},{8,9},{9,8},{10,11... | collective-permute-start | bytes 245768 | tf_op jit(solution)/shard_map/ppermute | solution.py:333
  64.5 9.6 %collective-permute-start.2 = (f32[20,8,128]{2,1,0:T(8,128)S(1)}, f32[20,8,128]{2,1,0:T(8,128)S(1)}, u32[]{:S(2)}, u32[]{:S(2)}) collective-permute-start(f32[20,8,128]{2,1,0:T(8,128)S(1)} %z_add.1.one), channel_id=1, source_target_pairs={{0,3},{1,2},{2,1},{3,0},{4,7},{5,6},{6,5},{7,4},{8,11},{9,10},{10,... | collective-permute-start | bytes 245768 | tf_op jit(solution)/shard_map/ppermute | solution.py:334
  98.1 26.2 %copy-start = (f32[5,64,64]{2,1,0:T(8,128)S(1)}, f32[5,64,64]{2,1,0:T(8,128)}, u32[]{:S(2)}) copy-start(f32[5,64,64]{2,1,0:T(8,128)} %q.1) | copy-start | bytes 245764

commit v9 on v8

--- a/solution.py
+++ b/solution.py
@@ -63,10 +63,10 @@
 
 
 def rank_dot(blocks, x):
-    qa, qb, qc = pieces(blocks)
-    a, b, c = pieces(x)
-    left = jnp.concatenate([qc, qa, qb, qb, qa, qa], axis=1)
-    right = jnp.concatenate([a, c, b, a, b, a], axis=0)
+    qa, qb, _ = pieces(blocks)
+    a, b, _ = pieces(x)
+    left = jnp.concatenate([qb, qa, qb, qa], axis=1)
+    right = jnp.concatenate([b, b, a, a], axis=0)
     return lax.dot_general(left, right, (((1,), (0,)), ((), ())), preferred_element_type=F32)
 
 
@@ -191,7 +191,7 @@
         out[k, out.shape[1] - 1] = quad
 
 
-def back_kernel(got, basis, out):
+def back_kernel(got, basis, out, quad):
     feats = basis.shape[0] // 2
     cts = basis.shape[1] // 128
 
@@ -214,15 +214,25 @@
                 t = (base + i) * fts + c
                 out[t // per, t % per] = back[i * 8 : i * 8 + 8, c * 128 : c * 128 + 128]
     last = got.shape[1] - 1
-    quad = (got[0, last] + got[1, last]) + (got[2, last] + got[3, last])
-    for k in range(16):
-        out[k, per] = quad
+    quad[...] = (got[0, last] + got[1, last]) + (got[2, last] + got[3, last])
+
+
+def share_kernel(got, quad, out):
+    total = got[0]
+    for k in range(1, got.shape[0]):
+        total = total + got[k]
+    for k in range(out.shape[0]):
+        out[k, : got.shape[1]] = total
+        out[k, got.shape[1]] = quad[...]
 
 
 def final_kernel(both, q, attn, mlp, result, stored):
     per = both.shape[2] - 1
     fts = attn.shape[1] // 128
-    quad = jnp.sum(both[0, 0, per] + both[1, 0, per], keepdims=True)
+    quad = both[0, 0, per] + both[1, 0, per]
+    for k in range(1, both.shape[1]):
+        quad = quad + (both[0, k, per] + both[1, k, per])
+    quad = jnp.sum(quad, keepdims=True)
     clip = jnp.minimum(1.0, jnp.sqrt(kl_limit / quad))
     stores = []
     for p in range(ROWS // R):
@@ -341,15 +351,23 @@
         name="scale",
     )(*near(block, across, wide, other, rank_eig))
     scaled = exchange(scaled, "factor", Y_GROUPS)
+    back, quad = pl.pallas_call(
+        back_kernel,
+        in_specs=[VMEM] * 2,
+        out_specs=[VMEM] * 2,
+        out_shape=[shape(16, half_tiles // 16, 8, 128), shape(8, 128)],
+        compiler_params=LIMIT,
+        name="back",
+    )(*near(scaled, basis))
     back = pl.pallas_call(
-        back_kernel,
+        share_kernel,
         in_specs=[VMEM] * 2,
         out_specs=VMEM,
         out_shape=shape(16, half_tiles // 16 + 1, 8, 128),
-        compiler_params=LIMIT, name="back",
-    )(*near(scaled, basis))
-    summed = jnp.sum(exchange(back, "dp", CHIPS), axis=0)
-    back = exchange(copies(summed, 16), "dp", CHIPS)
+        compiler_params=LIMIT,
+        name="share",
+    )(*near(exchange(back, "dp", CHIPS), quad))
+    back = exchange(back, "dp", CHIPS)
     both = lax.all_gather(back, "dp", axis_index_groups=CORE_PAIRS)
     return tuple(
         pl.pallas_call(

time: 126 us -> 125 us (level)
  no operation moved by 1% of the time
where the time goes in v9:
time: 125 us
  blocking collectives  81.6 us (65%)
  starting transfers between devices  21.6 us (17%)
  waiting for transfers between devices  14.6 us (12%)
  Pallas kernels  5.83 us (5%)
    all_to_all x5, blocking collectives, exchange(): return lax.all_to_all(x, axis, 0, 0, axis_index_groups=groups, tiled=True)  59.4 us
    all_gather x1, blocking collectives, body(): both = lax.all_gather(back, 'dp', axis_index_groups=CORE_PAIRS)  13.5 us
    ppermute x1, starting transfers between devices, body(): lax.ppermute(block, 'factor', Z_PAIRS)  8.81 us
    all_gather x1, blocking collectives, body(): both = lax.all_gather(send, 'dp', axis_index_groups=CORE_PAIRS)  8.75 us
    ppermute x1, starting transfers between devices, body(): across = lax.ppermute(block, 'factor', Z_CROSS)  6.99 us
    all_to_all x1, waiting for transfers between devices, exchange(): return lax.all_to_all(x, axis, 0, 0, axis_index_groups=groups, tiled=True)  6.61 us
    all_to_all x1, starting transfers between devices, exchange(): return lax.all_to_all(x, axis, 0, 0, axis_index_groups=groups, tiled=True)  3.54 us
    ppermute x1, waiting for transfers between devices, body(): lax.ppermute(block, 'factor', Z_PAIRS)  3.13 us
  transfers between devices with their start and end apart: 4, of which 4 were waited for; matrix products, arithmetic and copies ran while one was open for 0% of the time, Pallas kernels for 0%

profile of v9, /device:TPU:1, one launch (start us, length us, event | category | flops | bytes accessed | tf_op | source)
XLA Modules:
  0.0 124.6 jit_solution(2296385561381751419)
XLA Ops:
  0.6 2.7 %grad.1 = (f32[80,8,128]{2,1,0:T(8,128)S(1)}, f32[80,8,128]{2,1,0:T(8,128)S(1)}) custom-call(f32[5,64,64]{2,1,0:T(8,128)} %q.1, bf16[192,1024]{1,0:T(8,128)(2,1)} %bitcast.12, bf16[1024,512]{1,0:T(8,128)(2,1)} %refs_2_.1, bf16[1024,128]{1,0:T(8,128)(2,1)} %refs_3_.1, bf16[1024,512]{1,0:T(8,128)(2,1)} %refs_4_.1), custom_call_target="tpu_custom_call" | custom-call | tf_op jit(solution)/shard_map/grad/pallas_call | solution.py:278
  3.3 8.7 %all-gather = f32[160,8,128]{2,1,0:T(8,128)S(1)} all-gather(f32[80,8,128]{2,1,0:T(8,128)S(1)} %get-tuple-element.12), channel_id=2, replica_groups={{0,16},{32,48},{64,80},{96,112},{128,144},{160,176},{192,208},{224,240}..., dimensions={0}, use_global_device_ids=true | all-gather | bytes 983040 | tf_op jit(solution)/shard_map/all_gather | solution.py:288
  12.1 0.8 core_add.1
  12.8 3.5 %all-to-all-start = ((f32[16,5,8,128]{3,2,1,0:T(8,128)}), f32[16,5,8,128]{3,2,1,0:T(8,128)S(1)}, u32[]{:S(2)}, u32[]{:S(2)}) async-start(f32[16,5,8,128]{3,2,1,0:T(8,128)} %bitcast.2), calls=%async_computation | async-start | bytes 655360 | tf_op jit(solution)/shard_map/all_to_all | solution.py:27
  16.4 0.1 widen.1.own
  16.5 2.3 %collective-permute-start = (f32[260,8,128]{2,1,0:T(8,128)S(1)}, f32[260,8,128]{2,1,0:T(8,128)S(1)}, u32[]{:S(2)}, u32[]{:S(2)}) collective-permute-start(f32[260,8,128]{2,1,0:T(8,128)S(1)} %widen.1.own), channel_id=1, source_target_pairs={{0,16},{16,0},{32,48},{48,32},{64,80},{80,64},{96,112},{112,96},{1... | collective-permute-start | bytes 3194888 | tf_op jit(solution)/shard_map/ppermute | solution.py:307
  18.8 2.3 %collective-permute-done.other = f32[260,8,128]{2,1,0:T(8,128)S(1)} collective-permute-done((f32[260,8,128]{2,1,0:T(8,128)S(1)}, f32[260,8,128]{2,1,0:T(8,128)S(1)}, u32[]{:S(2)}, u32[]{:S(2)}) %collective-permute-start) | collective-permute-done | bytes 1064992 | tf_op jit(solution)/shard_map/ppermute | solution.py:307
  21.1 0.1 join.1.basis
  21.2 6.6 %all-to-all-done = f32[16,5,8,128]{3,2,1,0:T(8,128)S(1)} async-done(((f32[16,5,8,128]{3,2,1,0:T(8,128)}), f32[16,5,8,128]{3,2,1,0:T(8,128)S(1)}, u32[]{:S(2)}, u32[]{:S(2)}) %all-to-all-start) | async-done | bytes 327712 | tf_op jit(solution)/shard_map/all_to_all | solution.py:27
  27.9 15.1 %all_to_all.30 = f32[16,5,8,128]{3,2,1,0:T(8,128)S(1)} all-to-all(f32[16,5,8,128]{3,2,1,0:T(8,128)S(1)} %broadcast_in_dim.2), channel_id=1, replica_groups={{0,32,64,96,128,160,192,224,256,288,320,352,384,416,448,480},{16,48,80,..., dimensions={0} | all-to-all | bytes 655360 | tf_op jit(solution)/shard_map/all_to_all | solution.py:27
  43.0 0.4 rotate.1
  43.4 8.9 %all_to_all.31.got = f32[4,20,8,128]{3,2,1,0:T(8,128)S(1)} all-to-all(f32[4,20,8,128]{3,2,1,0:T(8,128)S(1)} %rotate.1), channel_id=1, replica_groups={{0,4,8,12},{1,5,9,13},{2,6,10,14},{3,7,11,15},{16,20,24,28},{17,21,25,2..., dimensions={0} | all-to-all | bytes 655360 | tf_op jit(solution)/shard_map/all_to_all | solution.py:27
  52.3 8.8 %collective-permute-start.1 = (f32[20,8,128]{2,1,0:T(8,128)S(1)}, f32[20,8,128]{2,1,0:T(8,128)S(1)}, u32[]{:S(2)}, u32[]{:S(2)}) collective-permute-start(f32[20,8,128]{2,1,0:T(8,128)S(1)} %y_sum.1.one), channel_id=1, source_target_pairs={{0,1},{1,0},{2,3},{3,2},{4,5},{5,4},{6,7},{7,6},{8,9},{9,8},{10,11... | collective-permute-start | bytes 245768 | tf_op jit(solution)/shard_map/ppermute | solution.py:343
  61.2 3.1 %collective-permute-done.1.two = f32[20,8,128]{2,1,0:T(8,128)S(1)} collective-permute-done((f32[20,8,128]{2,1,0:T(8,128)S(1)}, f32[20,8,128]{2,1,0:T(8,128)S(1)}, u32[]{:S(2)}, u32[]{:S(2)}) %collective-permute-start.1) | collective-permute-done | bytes 81952 | tf_op jit(solution)/shard_map/ppermute | solution.py:343
  64.3 7.0 %collective-permute-start.2 = (f32[20,8,128]{2,1,0:T(8,128)S(1)}, f32[20,8,128]{2,1,0:T(8,128)S(1)}, u32[]{:S(2)}, u32[]{:S(2)}) collective-permute-start(f32[20,8,128]{2,1,0:T(8,128)S(1)} %z_add.1.one), channel_id=1, source_target_pairs={{0,3},{1,2},{2,1},{3,0},{4,7},{5,6},{6,5},{7,4},{8,11},{9,10},{10,... | collective-permute-start | bytes 245768 | tf_op jit(solution)/shard_map/ppermute | solution.py:344
  71.3 2.6 %collective-permute-done.2.two = f32[20,8,128]{2,1,0:T(8,128)S(1)} collective-permute-done((f32[20,8,128]{2,1,0:T(8,128)S(1)}, f32[20,8,128]{2,1,0:T(8,128)S(1)}, u32[]{:S(2)}, u32[]{:S(2)}) %collective-permute-start.2) | collective-permute-done | bytes 81952 | tf_op jit(solution)/shard_map/ppermute | solution.py:344
  73.9 0.1 scale.1
  74.1 10.6 %all_to_all.32.got = f32[4,21,8,128]{3,2,1,0:T(8,128)S(1)} all-to-all(f32[4,21,8,128]{3,2,1,0:T(8,128)S(1)} %scale.1), channel_id=1, replica_groups={{0,4,8,12},{1,5,9,13},{2,6,10,14},{3,7,11,15},{16,20,24,28},{17,21,25,2..., dimensions={0} | all-to-all | bytes 688128 | tf_op jit(solution)/shard_map/all_to_all | solution.py:27
  84.7 0.5 back.1
  85.2 11.8 %all_to_all.33.got = f32[16,5,8,128]{3,2,1,0:T(8,128)S(1)} all-to-all(f32[16,5,8,128]{3,2,1,0:T(8,128)S(1)} %get-tuple-element.18), channel_id=1, replica_groups={{0,32,64,96,128,160,192,224,256,288,320,352,384,416,448,480},{16,48,80,..., dimensions={0} | all-to-all | bytes 655360 | tf_op jit(solution)/shard_map/all_to_all | solution.py:27
  97.0 0.0 copy-start
  97.0 12.9 %all_to_all.34 = f32[16,6,8,128]{3,2,1,0:T(8,128)S(1)} all-to-all(f32[16,6,8,128]{3,2,1,0:T(8,128)S(1)} %share.1), channel_id=1, replica_groups={{0,32,64,96,128,160,192,224,256,288,320,352,384,416,448,480},{16,48,80,..., dimensions={0} | all-to-all | bytes 786432 | tf_op jit(solution)/shard_map/all_to_all | solution.py:27
  109.9 13.5 %all-gather.1 = f32[32,6,8,128]{3,2,1,0:T(8,128)S(1)} all-gather(f32[16,6,8,128]{3,2,1,0:T(8,128)S(1)} %all_to_all.34), channel_id=3, replica_groups={{0,16},{32,48},{64,80},{96,112},{128,144},{160,176},{192,208},{224,240}..., dimensions={0}, use_global_device_ids=true | all-gather | bytes 1179648 | tf_op jit(solution)/shard_map/all_gather | solution.py:371
  123.4 1.1 final.1
  (16 shorter events, 0.1 us)
Async XLA Ops:
  12.0 4.3 %copy-start.1 = (bf16[512,256]{1,0:T(8,128)(2,1)S(1)}, bf16[512,256]{1,0:T(8,128)(2,1)}, u32[]{:S(2)}) copy-start(bf16[512,256]{1,0:T(8,128)(2,1)} %a_b) | copy-start | bytes 786436
  12.0 4.3 %copy-start.2 = (bf16[512,256]{1,0:T(8,128)(2,1)S(1)}, bf16[512,256]{1,0:T(8,128)(2,1)}, u32[]{:S(2)}) copy-start(bf16[512,256]{1,0:T(8,128)(2,1)} %m_b) | copy-start | bytes 786436
  12.0 4.3 %copy-start.4 = (f32[256]{0:T(256)S(1)}, f32[256]{0:T(256)}, u32[]{:S(2)}) copy-start(f32[256]{0:T(256)} %param.16) | copy-start | bytes 3076
  12.1 4.4 %copy-start.5 = (f32[256]{0:T(256)S(1)}, f32[256]{0:T(256)}, u32[]{:S(2)}) copy-start(f32[256]{0:T(256)} %param.17) | copy-start | bytes 3076
  12.8 15.0 %all-to-all-start = ((f32[16,5,8,128]{3,2,1,0:T(8,128)}), f32[16,5,8,128]{3,2,1,0:T(8,128)S(1)}, u32[]{:S(2)}, u32[]{:S(2)}) async-start(f32[16,5,8,128]{3,2,1,0:T(8,128)} %bitcast.2), calls=%async_computation | async-start | bytes 655360 | tf_op jit(solution)/shard_map/all_to_all | solution.py:27
  16.5 4.6 %collective-permute-start = (f32[260,8,128]{2,1,0:T(8,128)S(1)}, f32[260,8,128]{2,1,0:T(8,128)S(1)}, u32[]{:S(2)}, u32[]{:S(2)}) collective-permute-start(f32[260,8,128]{2,1,0:T(8,128)S(1)} %widen.1.own), channel_id=1, source_target_pairs={{0,16},{16,0},{32,48},{48,32},{64,80},{80,64},{96,112},{112,96},{1... | collective-permute-start | bytes 3194888 | tf_op jit(solution)/shard_map/ppermute | solution.py:307
  43.4 30.5 %copy-start.3 = (f32[5,64]{1,0:T(8,128)S(1)}, f32[5,64]{1,0:T(8,128)}, u32[]{:S(2)}) copy-start(f32[5,64]{1,0:T(8,128)} %eig.1) | copy-start | bytes 3844
  52.3 12.0 %collective-permute-start.1 = (f32[20,8,128]{2,1,0:T(8,128)S(1)}, f32[20,8,128]{2,1,0:T(8,128)S(1)}, u32[]{:S(2)}, u32[]{:S(2)}) collective-permute-start(f32[20,8,128]{2,1,0:T(8,128)S(1)} %y_sum.1.one), channel_id=1, source_target_pairs={{0,1},{1,0},{2,3},{3,2},{4,5},{5,4},{6,7},{7,6},{8,9},{9,8},{10,11... | collective-permute-start | bytes 245768 | tf_op jit(solution)/shard_map/ppermute | solution.py:343
  64.3 9.6 %collective-permute-start.2 = (f32[20,8,128]{2,1,0:T(8,128)S(1)}, f32[20,8,128]{2,1,0:T(8,128)S(1)}, u32[]{:S(2)}, u32[]{:S(2)}) collective-permute-start(f32[20,8,128]{2,1,0:T(8,128)S(1)} %z_add.1.one), channel_id=1, source_target_pairs={{0,3},{1,2},{2,1},{3,0},{4,7},{5,6},{6,5},{7,4},{8,11},{9,10},{10,... | collective-permute-start | bytes 245768 | tf_op jit(solution)/shard_map/ppermute | solution.py:344
  97.0 26.4 %copy-start = (f32[5,64,64]{2,1,0:T(8,128)S(1)}, f32[5,64,64]{2,1,0:T(8,128)}, u32[]{:S(2)}) copy-start(f32[5,64,64]{2,1,0:T(8,128)} %q.1) | copy-start | bytes 245764

commit v10 on v9

--- a/solution.py
+++ b/solution.py
@@ -12,7 +12,7 @@
 F32, BF16 = jnp.float32, jnp.bfloat16
 
 CORE_PAIRS = [[x * 8 + z * 2 + c for c in range(2)] for x in range(4) for z in range(4)]
-CHIPS = [[x * 8 + z * 2 + c for x in range(4) for z in range(4)] for c in range(2)]
+CHIPS = [[x * 8 + (z if x % 2 == 0 else 3 - z) * 2 + c for x in range(4) for z in range(4)] for c in range(2)]
 Y_GROUPS = [[y * 4 + z for y in range(4)] for z in range(4)]
 Z_PAIRS = [(y * 4 + z, y * 4 + (z ^ 1)) for y in range(4) for z in range(4)]
 Z_CROSS = [(y * 4 + z, y * 4 + 3 - z) for y in range(4) for z in range(4)]

time: 125 us -> 122 us (0.976)
  waiting for transfers between devices: 14.6 us -> 12.2 us
  blocking collectives: 81.6 us -> 79.5 us
  starting transfers between devices: 21.6 us -> 22.9 us
    all_gather x1, blocking collectives: 13.5 us -> 7.56 us  [body(): both = lax.all_gather(back, 'dp', axis_index_groups=CORE_PAIRS)]
    all_to_all x5, blocking collectives: 59.4 us -> 63.2 us  [exchange(): return lax.all_to_all(x, axis, 0, 0, axis_index_groups=groups, tiled=True)]
    all_to_all x1, waiting for transfers between devices: 6.61 us -> 4.05 us  [exchange(): return lax.all_to_all(x, axis, 0, 0, axis_index_groups=groups, tiled=True)]
    ppermute x1, waiting for transfers between devices: 2.62 us -> 4.09 us  [body(): across = lax.ppermute(block, 'factor', Z_CROSS)]
    ppermute x1, waiting for transfers between devices: 3.13 us -> 1.82 us  [body(): lax.ppermute(block, 'factor', Z_PAIRS)]
    ppermute x1, starting transfers between devices: 6.99 us -> 8.26 us  [body(): across = lax.ppermute(block, 'factor', Z_CROSS)]
where the time goes in v10:
time: 122 us; the launch traced here: 121 us
  blocking collectives  79.5 us (65%)
  starting transfers between devices  22.9 us (19%)
  waiting for transfers between devices  12.2 us (10%)
  Pallas kernels  5.83 us (5%)
    all_to_all x5, blocking collectives, exchange(): return lax.all_to_all(x, axis, 0, 0, axis_index_groups=groups, tiled=True)  63.2 us
    ppermute x1, starting transfers between devices, body(): lax.ppermute(block, 'factor', Z_PAIRS)  8.81 us
    all_gather x1, blocking collectives, body(): both = lax.all_gather(send, 'dp', axis_index_groups=CORE_PAIRS)  8.75 us
    ppermute x1, starting transfers between devices, body(): across = lax.ppermute(block, 'factor', Z_CROSS)  8.26 us
    all_gather x1, blocking collectives, body(): both = lax.all_gather(back, 'dp', axis_index_groups=CORE_PAIRS)  7.56 us
    ppermute x1, waiting for transfers between devices, body(): across = lax.ppermute(block, 'factor', Z_CROSS)  4.09 us
    all_to_all x1, waiting for transfers between devices, exchange(): return lax.all_to_all(x, axis, 0, 0, axis_index_groups=groups, tiled=True)  4.05 us
    all_to_all x1, starting transfers between devices, exchange(): return lax.all_to_all(x, axis, 0, 0, axis_index_groups=groups, tiled=True)  3.54 us
  transfers between devices with their start and end apart: 4, of which 4 were waited for; matrix products, arithmetic and copies ran while one was open for 0% of the time, Pallas kernels for 0%

profile of v10, /device:TPU:1, one launch (start us, length us, event | category | flops | bytes accessed | tf_op | source)
XLA Modules:
  0.0 121.4 jit_solution(11301784079657260324)
XLA Ops:
  0.6 2.7 %grad.1 = (f32[80,8,128]{2,1,0:T(8,128)S(1)}, f32[80,8,128]{2,1,0:T(8,128)S(1)}) custom-call(f32[5,64,64]{2,1,0:T(8,128)} %q.1, bf16[192,1024]{1,0:T(8,128)(2,1)} %bitcast.12, bf16[1024,512]{1,0:T(8,128)(2,1)} %refs_2_.1, bf16[1024,128]{1,0:T(8,128)(2,1)} %refs_3_.1, bf16[1024,512]{1,0:T(8,128)(2,1)} %refs_4_.1), custom_call_target="tpu_custom_call" | custom-call | tf_op jit(solution)/shard_map/grad/pallas_call | solution.py:278
  3.3 8.7 %all-gather = f32[160,8,128]{2,1,0:T(8,128)S(1)} all-gather(f32[80,8,128]{2,1,0:T(8,128)S(1)} %get-tuple-element.12), channel_id=2, replica_groups={{0,16},{32,48},{64,80},{96,112},{128,144},{160,176},{192,208},{224,240}..., dimensions={0}, use_global_device_ids=true | all-gather | bytes 983040 | tf_op jit(solution)/shard_map/all_gather | solution.py:288
  12.1 0.8 core_add.1
  12.8 3.5 %all-to-all-start = ((f32[16,5,8,128]{3,2,1,0:T(8,128)}), f32[16,5,8,128]{3,2,1,0:T(8,128)S(1)}, u32[]{:S(2)}, u32[]{:S(2)}) async-start(f32[16,5,8,128]{3,2,1,0:T(8,128)} %bitcast.2), calls=%async_computation | async-start | bytes 655360 | tf_op jit(solution)/shard_map/all_to_all | solution.py:27
  16.4 0.1 widen.1.own
  16.5 2.3 %collective-permute-start = (f32[260,8,128]{2,1,0:T(8,128)S(1)}, f32[260,8,128]{2,1,0:T(8,128)S(1)}, u32[]{:S(2)}, u32[]{:S(2)}) collective-permute-start(f32[260,8,128]{2,1,0:T(8,128)S(1)} %widen.1.own), channel_id=1, source_target_pairs={{0,16},{16,0},{32,48},{48,32},{64,80},{80,64},{96,112},{112,96},{1... | collective-permute-start | bytes 3194888 | tf_op jit(solution)/shard_map/ppermute | solution.py:307
  18.8 2.3 %collective-permute-done.other = f32[260,8,128]{2,1,0:T(8,128)S(1)} collective-permute-done((f32[260,8,128]{2,1,0:T(8,128)S(1)}, f32[260,8,128]{2,1,0:T(8,128)S(1)}, u32[]{:S(2)}, u32[]{:S(2)}) %collective-permute-start) | collective-permute-done | bytes 1064992 | tf_op jit(solution)/shard_map/ppermute | solution.py:307
  21.1 0.1 join.1.basis
  21.2 4.1 %all-to-all-done = f32[16,5,8,128]{3,2,1,0:T(8,128)S(1)} async-done(((f32[16,5,8,128]{3,2,1,0:T(8,128)}), f32[16,5,8,128]{3,2,1,0:T(8,128)S(1)}, u32[]{:S(2)}, u32[]{:S(2)}) %all-to-all-start) | async-done | bytes 327712 | tf_op jit(solution)/shard_map/all_to_all | solution.py:27
  25.3 14.7 %all_to_all.30 = f32[16,5,8,128]{3,2,1,0:T(8,128)S(1)} all-to-all(f32[16,5,8,128]{3,2,1,0:T(8,128)S(1)} %broadcast_in_dim.2), channel_id=1, replica_groups={{0,32,64,96,224,192,160,128,256,288,320,352,480,448,416,384},{16,48,80,..., dimensions={0} | all-to-all | bytes 655360 | tf_op jit(solution)/shard_map/all_to_all | solution.py:27
  40.0 0.4 rotate.1
  40.4 0.0 copy-start.3
  40.4 9.2 %all_to_all.31.got = f32[4,20,8,128]{3,2,1,0:T(8,128)S(1)} all-to-all(f32[4,20,8,128]{3,2,1,0:T(8,128)S(1)} %rotate.1), channel_id=1, replica_groups={{0,4,8,12},{1,5,9,13},{2,6,10,14},{3,7,11,15},{16,20,24,28},{17,21,25,2..., dimensions={0} | all-to-all | bytes 655360 | tf_op jit(solution)/shard_map/all_to_all | solution.py:27
  49.6 8.8 %collective-permute-start.1 = (f32[20,8,128]{2,1,0:T(8,128)S(1)}, f32[20,8,128]{2,1,0:T(8,128)S(1)}, u32[]{:S(2)}, u32[]{:S(2)}) collective-permute-start(f32[20,8,128]{2,1,0:T(8,128)S(1)} %y_sum.1.one), channel_id=1, source_target_pairs={{0,1},{1,0},{2,3},{3,2},{4,5},{5,4},{6,7},{7,6},{8,9},{9,8},{10,11... | collective-permute-start | bytes 245768 | tf_op jit(solution)/shard_map/ppermute | solution.py:343
  58.5 1.8 %collective-permute-done.1.two = f32[20,8,128]{2,1,0:T(8,128)S(1)} collective-permute-done((f32[20,8,128]{2,1,0:T(8,128)S(1)}, f32[20,8,128]{2,1,0:T(8,128)S(1)}, u32[]{:S(2)}, u32[]{:S(2)}) %collective-permute-start.1) | collective-permute-done | bytes 81952 | tf_op jit(solution)/shard_map/ppermute | solution.py:343
  60.3 8.3 %collective-permute-start.2 = (f32[20,8,128]{2,1,0:T(8,128)S(1)}, f32[20,8,128]{2,1,0:T(8,128)S(1)}, u32[]{:S(2)}, u32[]{:S(2)}) collective-permute-start(f32[20,8,128]{2,1,0:T(8,128)S(1)} %z_add.1.one), channel_id=1, source_target_pairs={{0,3},{1,2},{2,1},{3,0},{4,7},{5,6},{6,5},{7,4},{8,11},{9,10},{10,... | collective-permute-start | bytes 245768 | tf_op jit(solution)/shard_map/ppermute | solution.py:344
  68.6 4.1 %collective-permute-done.2.two = f32[20,8,128]{2,1,0:T(8,128)S(1)} collective-permute-done((f32[20,8,128]{2,1,0:T(8,128)S(1)}, f32[20,8,128]{2,1,0:T(8,128)S(1)}, u32[]{:S(2)}, u32[]{:S(2)}) %collective-permute-start.2) | collective-permute-done | bytes 81952 | tf_op jit(solution)/shard_map/ppermute | solution.py:344
  72.7 0.1 scale.1
  72.8 8.3 %all_to_all.32.got = f32[4,21,8,128]{3,2,1,0:T(8,128)S(1)} all-to-all(f32[4,21,8,128]{3,2,1,0:T(8,128)S(1)} %scale.1), channel_id=1, replica_groups={{0,4,8,12},{1,5,9,13},{2,6,10,14},{3,7,11,15},{16,20,24,28},{17,21,25,2..., dimensions={0} | all-to-all | bytes 688128 | tf_op jit(solution)/shard_map/all_to_all | solution.py:27
  81.1 0.5 back.1
  81.6 18.3 %all_to_all.33.got = f32[16,5,8,128]{3,2,1,0:T(8,128)S(1)} all-to-all(f32[16,5,8,128]{3,2,1,0:T(8,128)S(1)} %get-tuple-element.18), channel_id=1, replica_groups={{0,32,64,96,224,192,160,128,256,288,320,352,480,448,416,384},{16,48,80,..., dimensions={0} | all-to-all | bytes 655360 | tf_op jit(solution)/shard_map/all_to_all | solution.py:27
  100.0 12.7 %all_to_all.34 = f32[16,6,8,128]{3,2,1,0:T(8,128)S(1)} all-to-all(f32[16,6,8,128]{3,2,1,0:T(8,128)S(1)} %share.1), channel_id=1, replica_groups={{0,32,64,96,224,192,160,128,256,288,320,352,480,448,416,384},{16,48,80,..., dimensions={0} | all-to-all | bytes 786432 | tf_op jit(solution)/shard_map/all_to_all | solution.py:27
  112.7 7.6 %all-gather.1 = f32[32,6,8,128]{3,2,1,0:T(8,128)S(1)} all-gather(f32[16,6,8,128]{3,2,1,0:T(8,128)S(1)} %all_to_all.34), channel_id=3, replica_groups={{0,16},{32,48},{64,80},{96,112},{128,144},{160,176},{192,208},{224,240}..., dimensions={0}, use_global_device_ids=true | all-gather | bytes 1179648 | tf_op jit(solution)/shard_map/all_gather | solution.py:371
  120.2 1.1 final.1
  (16 shorter events, 0.1 us)
Async XLA Ops:
  12.0 4.3 %copy-start.1 = (bf16[512,256]{1,0:T(8,128)(2,1)S(1)}, bf16[512,256]{1,0:T(8,128)(2,1)}, u32[]{:S(2)}) copy-start(bf16[512,256]{1,0:T(8,128)(2,1)} %a_b) | copy-start | bytes 786436
  12.0 4.3 %copy-start.2 = (bf16[512,256]{1,0:T(8,128)(2,1)S(1)}, bf16[512,256]{1,0:T(8,128)(2,1)}, u32[]{:S(2)}) copy-start(bf16[512,256]{1,0:T(8,128)(2,1)} %m_b) | copy-start | bytes 786436
  12.0 4.3 %copy-start.4 = (f32[256]{0:T(256)S(1)}, f32[256]{0:T(256)}, u32[]{:S(2)}) copy-start(f32[256]{0:T(256)} %param.16) | copy-start | bytes 3076
  12.1 4.4 %copy-start.5 = (f32[256]{0:T(256)S(1)}, f32[256]{0:T(256)}, u32[]{:S(2)}) copy-start(f32[256]{0:T(256)} %param.17) | copy-start | bytes 3076
  12.8 12.4 %all-to-all-start = ((f32[16,5,8,128]{3,2,1,0:T(8,128)}), f32[16,5,8,128]{3,2,1,0:T(8,128)S(1)}, u32[]{:S(2)}, u32[]{:S(2)}) async-start(f32[16,5,8,128]{3,2,1,0:T(8,128)} %bitcast.2), calls=%async_computation | async-start | bytes 655360 | tf_op jit(solution)/shard_map/all_to_all | solution.py:27
  16.5 4.6 %collective-permute-start = (f32[260,8,128]{2,1,0:T(8,128)S(1)}, f32[260,8,128]{2,1,0:T(8,128)S(1)}, u32[]{:S(2)}, u32[]{:S(2)}) collective-permute-start(f32[260,8,128]{2,1,0:T(8,128)S(1)} %widen.1.own), channel_id=1, source_target_pairs={{0,16},{16,0},{32,48},{48,32},{64,80},{80,64},{96,112},{112,96},{1... | collective-permute-start | bytes 3194888 | tf_op jit(solution)/shard_map/ppermute | solution.py:307
  40.4 32.3 %copy-start.3 = (f32[5,64]{1,0:T(8,128)S(1)}, f32[5,64]{1,0:T(8,128)}, u32[]{:S(2)}) copy-start(f32[5,64]{1,0:T(8,128)} %eig.1) | copy-start | bytes 3844
  49.6 10.6 %collective-permute-start.1 = (f32[20,8,128]{2,1,0:T(8,128)S(1)}, f32[20,8,128]{2,1,0:T(8,128)S(1)}, u32[]{:S(2)}, u32[]{:S(2)}) collective-permute-start(f32[20,8,128]{2,1,0:T(8,128)S(1)} %y_sum.1.one), channel_id=1, source_target_pairs={{0,1},{1,0},{2,3},{3,2},{4,5},{5,4},{6,7},{7,6},{8,9},{9,8},{10,11... | collective-permute-start | bytes 245768 | tf_op jit(solution)/shard_map/ppermute | solution.py:343
  60.3 12.4 %collective-permute-start.2 = (f32[20,8,128]{2,1,0:T(8,128)S(1)}, f32[20,8,128]{2,1,0:T(8,128)S(1)}, u32[]{:S(2)}, u32[]{:S(2)}) collective-permute-start(f32[20,8,128]{2,1,0:T(8,128)S(1)} %z_add.1.one), channel_id=1, source_target_pairs={{0,3},{1,2},{2,1},{3,0},{4,7},{5,6},{6,5},{7,4},{8,11},{9,10},{10,... | collective-permute-start | bytes 245768 | tf_op jit(solution)/shard_map/ppermute | solution.py:344
  99.9 20.3 %copy-start = (f32[5,64,64]{2,1,0:T(8,128)S(1)}, f32[5,64,64]{2,1,0:T(8,128)}, u32[]{:S(2)}) copy-start(f32[5,64,64]{2,1,0:T(8,128)} %q.1) | copy-start | bytes 245764

commit v11 on v10

--- a/solution.py
+++ b/solution.py
@@ -50,21 +50,19 @@
 
 def pieces(x):
     a = x.astype(BF16)
-    r = x - a.astype(F32)
-    b = r.astype(BF16)
-    return a, b, (r - b.astype(F32)).astype(BF16)
+    return a, (x - a.astype(F32)).astype(BF16)
 
 
 def exact_dot(x, basis, contract):
     n = x.shape[0]
     stacked = jnp.concatenate(pieces(x), axis=0)
     out = lax.dot_general(stacked, basis, (((1,), (contract,)), ((), ())), preferred_element_type=F32)
-    return (out[2 * n :] + out[n : 2 * n]) + out[:n]
+    return out[n:] + out[:n]
 
 
 def rank_dot(blocks, x):
-    qa, qb, _ = pieces(blocks)
-    a, b, _ = pieces(x)
+    qa, qb = pieces(blocks)
+    a, b = pieces(x)
     left = jnp.concatenate([qb, qa, qb, qa], axis=1)
     right = jnp.concatenate([b, b, a, a], axis=0)
     return lax.dot_general(left, right, (((1,), (0,)), ((), ())), preferred_element_type=F32)
@@ -340,8 +338,8 @@
         out_shape=shape(y_tiles, 8, 128),
         compiler_params=LIMIT,
         name="z_add",
-    )(*near(block, lax.ppermute(block, "factor", Z_PAIRS)))
-    across = lax.ppermute(block, "factor", Z_CROSS)
+    )(*near(block, lax.ppermute(block, "factor", Z_CROSS)))
+    across = lax.ppermute(block, "factor", Z_PAIRS)
     scaled = pl.pallas_call(
         scale_kernel,
         in_specs=[VMEM] * 5,

time: 122 us -> 121 us (level)
  blocking collectives: 79.5 us -> 80.8 us
    all_gather x1, blocking collectives: 7.56 us -> 9.21 us  [body(): both = lax.all_gather(back, 'dp', axis_index_groups=CORE_PAIRS)]
where the time goes in v11:
time: 121 us; the launch traced here: 120 us
  blocking collectives  80.8 us (67%)
  starting transfers between devices  21.9 us (18%)
  waiting for transfers between devices  11.1 us (9%)
  Pallas kernels  5.74 us (5%)
    all_to_all x5, blocking collectives, exchange(): return lax.all_to_all(x, axis, 0, 0, axis_index_groups=groups, tiled=True)  62.9 us
    ppermute x1, starting transfers between devices, body(): lax.ppermute(block, 'factor', Z_CROSS)  9.75 us
    all_gather x1, blocking collectives, body(): both = lax.all_gather(back, 'dp', axis_index_groups=CORE_PAIRS)  9.21 us
    all_gather x1, blocking collectives, body(): both = lax.all_gather(send, 'dp', axis_index_groups=CORE_PAIRS)  8.75 us
    ppermute x1, starting transfers between devices, body(): across = lax.ppermute(block, 'factor', Z_PAIRS)  6.27 us
    all_to_all x1, waiting for transfers between devices, exchange(): return lax.all_to_all(x, axis, 0, 0, axis_index_groups=groups, tiled=True)  4.05 us
    all_to_all x1, starting transfers between devices, exchange(): return lax.all_to_all(x, axis, 0, 0, axis_index_groups=groups, tiled=True)  3.54 us
    ppermute x1, waiting for transfers between devices, body(): across = lax.ppermute(block, 'factor', Z_PAIRS)  2.91 us
  transfers between devices with their start and end apart: 4, of which 4 were waited for; matrix products, arithmetic and copies ran while one was open for 0% of the time, Pallas kernels for 0%

profile of v11, /device:TPU:1, one launch (start us, length us, event | category | flops | bytes accessed | tf_op | source)
XLA Modules:
  0.0 120.4 jit_solution(7540063517960922682)
XLA Ops:
  0.6 2.7 %grad.1 = (f32[80,8,128]{2,1,0:T(8,128)S(1)}, f32[80,8,128]{2,1,0:T(8,128)S(1)}) custom-call(f32[5,64,64]{2,1,0:T(8,128)} %q.1, bf16[192,1024]{1,0:T(8,128)(2,1)} %bitcast.12, bf16[1024,512]{1,0:T(8,128)(2,1)} %refs_2_.1, bf16[1024,128]{1,0:T(8,128)(2,1)} %refs_3_.1, bf16[1024,512]{1,0:T(8,128)(2,1)} %refs_4_.1), custom_call_target="tpu_custom_call" | custom-call | tf_op jit(solution)/shard_map/grad/pallas_call | solution.py:276
  3.3 8.7 %all-gather = f32[160,8,128]{2,1,0:T(8,128)S(1)} all-gather(f32[80,8,128]{2,1,0:T(8,128)S(1)} %get-tuple-element.12), channel_id=2, replica_groups={{0,16},{32,48},{64,80},{96,112},{128,144},{160,176},{192,208},{224,240}..., dimensions={0}, use_global_device_ids=true | all-gather | bytes 983040 | tf_op jit(solution)/shard_map/all_gather | solution.py:286
  12.1 0.8 core_add.1
  12.8 3.5 %all-to-all-start = ((f32[16,5,8,128]{3,2,1,0:T(8,128)}), f32[16,5,8,128]{3,2,1,0:T(8,128)S(1)}, u32[]{:S(2)}, u32[]{:S(2)}) async-start(f32[16,5,8,128]{3,2,1,0:T(8,128)} %bitcast.2), calls=%async_computation | async-start | bytes 655360 | tf_op jit(solution)/shard_map/all_to_all | solution.py:27
  16.4 0.1 widen.1.own
  16.5 2.3 %collective-permute-start = (f32[260,8,128]{2,1,0:T(8,128)S(1)}, f32[260,8,128]{2,1,0:T(8,128)S(1)}, u32[]{:S(2)}, u32[]{:S(2)}) collective-permute-start(f32[260,8,128]{2,1,0:T(8,128)S(1)} %widen.1.own), channel_id=1, source_target_pairs={{0,16},{16,0},{32,48},{48,32},{64,80},{80,64},{96,112},{112,96},{1... | collective-permute-start | bytes 3194888 | tf_op jit(solution)/shard_map/ppermute | solution.py:305
  18.8 2.3 %collective-permute-done.other = f32[260,8,128]{2,1,0:T(8,128)S(1)} collective-permute-done((f32[260,8,128]{2,1,0:T(8,128)S(1)}, f32[260,8,128]{2,1,0:T(8,128)S(1)}, u32[]{:S(2)}, u32[]{:S(2)}) %collective-permute-start) | collective-permute-done | bytes 1064992 | tf_op jit(solution)/shard_map/ppermute | solution.py:305
  21.1 0.1 join.1.basis
  21.2 4.1 %all-to-all-done = f32[16,5,8,128]{3,2,1,0:T(8,128)S(1)} async-done(((f32[16,5,8,128]{3,2,1,0:T(8,128)}), f32[16,5,8,128]{3,2,1,0:T(8,128)S(1)}, u32[]{:S(2)}, u32[]{:S(2)}) %all-to-all-start) | async-done | bytes 327712 | tf_op jit(solution)/shard_map/all_to_all | solution.py:27
  25.3 14.7 %all_to_all.30 = f32[16,5,8,128]{3,2,1,0:T(8,128)S(1)} all-to-all(f32[16,5,8,128]{3,2,1,0:T(8,128)S(1)} %broadcast_in_dim.2), channel_id=1, replica_groups={{0,32,64,96,224,192,160,128,256,288,320,352,480,448,416,384},{16,48,80,..., dimensions={0} | all-to-all | bytes 655360 | tf_op jit(solution)/shard_map/all_to_all | solution.py:27
  40.0 0.3 rotate.1
  40.3 0.0 copy-start.3
  40.3 9.2 %all_to_all.31.got = f32[4,20,8,128]{3,2,1,0:T(8,128)S(1)} all-to-all(f32[4,20,8,128]{3,2,1,0:T(8,128)S(1)} %rotate.1), channel_id=1, replica_groups={{0,4,8,12},{1,5,9,13},{2,6,10,14},{3,7,11,15},{16,20,24,28},{17,21,25,2..., dimensions={0} | all-to-all | bytes 655360 | tf_op jit(solution)/shard_map/all_to_all | solution.py:27
  49.6 9.7 %collective-permute-start.1 = (f32[20,8,128]{2,1,0:T(8,128)S(1)}, f32[20,8,128]{2,1,0:T(8,128)S(1)}, u32[]{:S(2)}, u32[]{:S(2)}) collective-permute-start(f32[20,8,128]{2,1,0:T(8,128)S(1)} %y_sum.1.one), channel_id=1, source_target_pairs={{0,3},{1,2},{2,1},{3,0},{4,7},{5,6},{6,5},{7,4},{8,11},{9,10},{10,... | collective-permute-start | bytes 245768 | tf_op jit(solution)/shard_map/ppermute | solution.py:341
  59.3 1.9 %collective-permute-done.1.two = f32[20,8,128]{2,1,0:T(8,128)S(1)} collective-permute-done((f32[20,8,128]{2,1,0:T(8,128)S(1)}, f32[20,8,128]{2,1,0:T(8,128)S(1)}, u32[]{:S(2)}, u32[]{:S(2)}) %collective-permute-start.1) | collective-permute-done | bytes 81952 | tf_op jit(solution)/shard_map/ppermute | solution.py:341
  61.2 6.3 %collective-permute-start.2 = (f32[20,8,128]{2,1,0:T(8,128)S(1)}, f32[20,8,128]{2,1,0:T(8,128)S(1)}, u32[]{:S(2)}, u32[]{:S(2)}) collective-permute-start(f32[20,8,128]{2,1,0:T(8,128)S(1)} %z_add.1.one), channel_id=1, source_target_pairs={{0,1},{1,0},{2,3},{3,2},{4,5},{5,4},{6,7},{7,6},{8,9},{9,8},{10,11... | collective-permute-start | bytes 245768 | tf_op jit(solution)/shard_map/ppermute | solution.py:342
  67.5 2.9 %collective-permute-done.2.two = f32[20,8,128]{2,1,0:T(8,128)S(1)} collective-permute-done((f32[20,8,128]{2,1,0:T(8,128)S(1)}, f32[20,8,128]{2,1,0:T(8,128)S(1)}, u32[]{:S(2)}, u32[]{:S(2)}) %collective-permute-start.2) | collective-permute-done | bytes 81952 | tf_op jit(solution)/shard_map/ppermute | solution.py:342
  70.4 0.1 scale.1
  70.5 8.6 %all_to_all.32.got = f32[4,21,8,128]{3,2,1,0:T(8,128)S(1)} all-to-all(f32[4,21,8,128]{3,2,1,0:T(8,128)S(1)} %scale.1), channel_id=1, replica_groups={{0,4,8,12},{1,5,9,13},{2,6,10,14},{3,7,11,15},{16,20,24,28},{17,21,25,2..., dimensions={0} | all-to-all | bytes 688128 | tf_op jit(solution)/shard_map/all_to_all | solution.py:27
  79.2 0.5 back.1
  79.7 17.8 %all_to_all.33.got = f32[16,5,8,128]{3,2,1,0:T(8,128)S(1)} all-to-all(f32[16,5,8,128]{3,2,1,0:T(8,128)S(1)} %get-tuple-element.18), channel_id=1, replica_groups={{0,32,64,96,224,192,160,128,256,288,320,352,480,448,416,384},{16,48,80,..., dimensions={0} | all-to-all | bytes 655360 | tf_op jit(solution)/shard_map/all_to_all | solution.py:27
  97.5 12.5 %all_to_all.34 = f32[16,6,8,128]{3,2,1,0:T(8,128)S(1)} all-to-all(f32[16,6,8,128]{3,2,1,0:T(8,128)S(1)} %share.1), channel_id=1, replica_groups={{0,32,64,96,224,192,160,128,256,288,320,352,480,448,416,384},{16,48,80,..., dimensions={0} | all-to-all | bytes 786432 | tf_op jit(solution)/shard_map/all_to_all | solution.py:27
  110.1 9.2 %all-gather.1 = f32[32,6,8,128]{3,2,1,0:T(8,128)S(1)} all-gather(f32[16,6,8,128]{3,2,1,0:T(8,128)S(1)} %all_to_all.34), channel_id=3, replica_groups={{0,16},{32,48},{64,80},{96,112},{128,144},{160,176},{192,208},{224,240}..., dimensions={0}, use_global_device_ids=true | all-gather | bytes 1179648 | tf_op jit(solution)/shard_map/all_gather | solution.py:369
  119.3 1.1 final.1
  (16 shorter events, 0.1 us)
Async XLA Ops:
  12.0 4.3 %copy-start.1 = (bf16[512,256]{1,0:T(8,128)(2,1)S(1)}, bf16[512,256]{1,0:T(8,128)(2,1)}, u32[]{:S(2)}) copy-start(bf16[512,256]{1,0:T(8,128)(2,1)} %a_b) | copy-start | bytes 786436
  12.0 4.3 %copy-start.2 = (bf16[512,256]{1,0:T(8,128)(2,1)S(1)}, bf16[512,256]{1,0:T(8,128)(2,1)}, u32[]{:S(2)}) copy-start(bf16[512,256]{1,0:T(8,128)(2,1)} %m_b) | copy-start | bytes 786436
  12.0 4.3 %copy-start.4 = (f32[256]{0:T(256)S(1)}, f32[256]{0:T(256)}, u32[]{:S(2)}) copy-start(f32[256]{0:T(256)} %param.16) | copy-start | bytes 3076
  12.1 4.4 %copy-start.5 = (f32[256]{0:T(256)S(1)}, f32[256]{0:T(256)}, u32[]{:S(2)}) copy-start(f32[256]{0:T(256)} %param.17) | copy-start | bytes 3076
  12.8 12.4 %all-to-all-start = ((f32[16,5,8,128]{3,2,1,0:T(8,128)}), f32[16,5,8,128]{3,2,1,0:T(8,128)S(1)}, u32[]{:S(2)}, u32[]{:S(2)}) async-start(f32[16,5,8,128]{3,2,1,0:T(8,128)} %bitcast.2), calls=%async_computation | async-start | bytes 655360 | tf_op jit(solution)/shard_map/all_to_all | solution.py:27
  16.5 4.6 %collective-permute-start = (f32[260,8,128]{2,1,0:T(8,128)S(1)}, f32[260,8,128]{2,1,0:T(8,128)S(1)}, u32[]{:S(2)}, u32[]{:S(2)}) collective-permute-start(f32[260,8,128]{2,1,0:T(8,128)S(1)} %widen.1.own), channel_id=1, source_target_pairs={{0,16},{16,0},{32,48},{48,32},{64,80},{80,64},{96,112},{112,96},{1... | collective-permute-start | bytes 3194888 | tf_op jit(solution)/shard_map/ppermute | solution.py:305
  40.3 30.1 %copy-start.3 = (f32[5,64]{1,0:T(8,128)S(1)}, f32[5,64]{1,0:T(8,128)}, u32[]{:S(2)}) copy-start(f32[5,64]{1,0:T(8,128)} %eig.1) | copy-start | bytes 3844
  49.6 11.6 %collective-permute-start.1 = (f32[20,8,128]{2,1,0:T(8,128)S(1)}, f32[20,8,128]{2,1,0:T(8,128)S(1)}, u32[]{:S(2)}, u32[]{:S(2)}) collective-permute-start(f32[20,8,128]{2,1,0:T(8,128)S(1)} %y_sum.1.one), channel_id=1, source_target_pairs={{0,3},{1,2},{2,1},{3,0},{4,7},{5,6},{6,5},{7,4},{8,11},{9,10},{10,... | collective-permute-start | bytes 245768 | tf_op jit(solution)/shard_map/ppermute | solution.py:341
  61.2 9.2 %collective-permute-start.2 = (f32[20,8,128]{2,1,0:T(8,128)S(1)}, f32[20,8,128]{2,1,0:T(8,128)S(1)}, u32[]{:S(2)}, u32[]{:S(2)}) collective-permute-start(f32[20,8,128]{2,1,0:T(8,128)S(1)} %z_add.1.one), channel_id=1, source_target_pairs={{0,1},{1,0},{2,3},{3,2},{4,5},{5,4},{6,7},{7,6},{8,9},{9,8},{10,11... | collective-permute-start | bytes 245768 | tf_op jit(solution)/shard_map/ppermute | solution.py:342
  97.5 21.8 %copy-start = (f32[5,64,64]{2,1,0:T(8,128)S(1)}, f32[5,64,64]{2,1,0:T(8,128)}, u32[]{:S(2)}) copy-start(f32[5,64,64]{2,1,0:T(8,128)} %q.1) | copy-start | bytes 245764
